TPU v7x, 32 devices: a whole 2x2x4 slice. The times are simulated.
32 devices in a mesh: slab: 2 (over y), frames: 4 (over z), medoids: 4 (over x, core).
Axes of the slice: x: 2, y: 2, z: 4, core: 2. Of those that a mesh axis runs over, the one named last changes fastest.
Arguments:
- frames: bfloat16 [16384, 512], P(('slab', 'frames')), parts along dimension 0, may hold values from -6 to 6
- medoids: bfloat16 [4, 8192, 512], P('medoids', 'frames'), may hold values from -6 to 6
- tile_ids: int32 [4, 128, 24], P('medoids', ('slab', 'frames')), parts along dimension 1, may hold values from 0 to 63, as said below
- tile_counts: int32 [4, 128], P('medoids', ('slab', 'frames')), parts along dimension 1, may hold values from 1 to 24, as said below
- plan: int32 [128], P('slab'), parts along dimension 0, may hold values from 0 to 63, as said below
Outputs:
- nearest: float32 [16384], P(('slab', 'frames')), parts along dimension 0
- second: float32 [16384], P(('slab', 'frames')), parts along dimension 0
There are 2 independent parts, one for each index of `slab`. A program takes and returns all parts, laid end to end along the dimension named above; an argument that names none is the same for every part. Nothing has to cross between parts.
Inputs may be any that keep to these rules, and one draw needn't show every extreme that they name: plan is a permutation. Of the frame tiles 16 i to 16 i + 15, at most 4 stand at positions 16 j to 16 j + 15 of plan's inverse for one j, and exactly 4 for some j, for every i. `tile_ids`: the 24 entries of one list are distinct; entries at l >= tile_counts[m, g] are ignored. `tile_counts`: the largest value is reached in every draw.
All inputs are finite; a program needn't handle non-finite values.
Results may differ from a plain program's by a relative error of at most 0.0003.
Values may be sent and summed in bfloat16 or wider, within the bound.
No kernel may reach another device: no remote copies, remote signals or barrier semaphores. Data moves between devices by JAX's collectives and lax.ppermute only.
A program may use at most 64 MiB of HBM per device.

v0:
```python
import functools

import jax
import jax.numpy as jnp
from jax import lax
from jax.experimental import pallas as pl
from jax.experimental.pallas import tpu as pltpu
from jax.sharding import PartitionSpec as P


TILE = 128


big_value = 1e30
per_block = 8
unroll = 4


def fold_two(left_one, left_two, right_one, right_two):
    first = jnp.minimum(left_one, right_one)
    second = jnp.minimum(jnp.maximum(left_one, right_one), jnp.minimum(left_two, right_two))
    return (first, second)


def tile_pass(frame_tile, ids, count, group_rows, group_norm):
    width = frame_tile.shape[1]
    rows_tile = frame_tile.shape[0]
    frame_norm = jnp.sum(jnp.square(frame_tile.astype(jnp.float32)), axis=1)

    def step(block, carry):
        start = (block * per_block).astype(jnp.int32)
        chosen = lax.dynamic_slice_in_dim(ids, start, per_block)
        live = start + jnp.arange(per_block, dtype=jnp.int32) < count
        rows = group_rows[chosen].reshape(per_block * rows_tile, width)
        norms = group_norm[chosen].reshape(per_block * rows_tile)
        inner = lax.dot_general(
            frame_tile, rows, (((1,), (1,)), ((), ())), preferred_element_type=jnp.float32
        )
        dist = (frame_norm[:, None] + norms[None, :] - 2.0 * inner) / width
        keep = jnp.repeat(live, rows_tile)
        dist = jnp.where(keep[None, :], dist, jnp.float32(big_value))
        lowest = -lax.top_k(-dist, 2)[0]
        return fold_two(carry[0], carry[1], lowest[:, 0], lowest[:, 1])

    start_pair = (
        jnp.full((rows_tile,), big_value, jnp.float32),
        jnp.full((rows_tile,), big_value, jnp.float32),
    )
    blocks = (count + per_block - 1) // per_block
    return lax.fori_loop(0, blocks, step, start_pair)


def all_tiles(tiles, ids, counts, group_rows, group_norm):
    number = tiles.shape[0]

    def one_tile(index, carry):
        found_one, found_two = tile_pass(
            tiles[index], ids[index], counts[index], group_rows, group_norm
        )
        return (carry[0].at[index].set(found_one), carry[1].at[index].set(found_two))

    empty = jnp.zeros((number, TILE), jnp.float32)
    return lax.fori_loop(0, number, one_tile, (empty, empty))


def across_groups(first, second):
    every_one, every_two = (
        lax.all_gather(first[None], "medoids", axis=0, tiled=True),
        lax.all_gather(second[None], "medoids", axis=0, tiled=True),
    )
    best_one, best_two = (every_one[0], every_two[0])
    for group in range(1, every_one.shape[0]):
        best_one, best_two = fold_two(best_one, best_two, every_one[group], every_two[group])
    return (best_one, best_two)


def gathered_medoids(frames, medoids, tile_ids, tile_counts, plan):
    width = frames.shape[1]
    blocks = frames.shape[0] // TILE
    members = lax.axis_size("frames")
    member = lax.axis_index("frames")
    capacity = (blocks + members - 1) // members
    group = lax.all_gather(medoids[0], "frames", axis=0, tiled=True)
    group_tiles = group.shape[0] // TILE
    group_rows = group.reshape(group_tiles, TILE, width)
    group_norm = jnp.sum(jnp.square(group.astype(jnp.float32)), axis=1).reshape(group_tiles, TILE)
    total = plan.shape[0]
    position = jnp.zeros((total,), jnp.int32).at[plan].set(jnp.arange(total, dtype=jnp.int32))
    target = (position // blocks).reshape(members, blocks)
    matching = target[:, :, None] == target[:, None, :]
    earlier = jnp.arange(blocks)[None, :] < jnp.arange(blocks)[:, None]
    slot_table = jnp.sum(jnp.logical_and(matching, earlier[None]), axis=2)
    my_target = lax.dynamic_index_in_dim(target, member, 0, keepdims=False)
    my_slot = lax.dynamic_index_in_dim(slot_table, member, 0, keepdims=False)
    arriving = lax.dynamic_slice_in_dim(plan, member * blocks, blocks)
    sender = arriving // blocks
    sender_slot = slot_table.reshape(-1)[arriving]
    tiles = frames.reshape(blocks, TILE, width)
    outgoing_tiles = (
        jnp.zeros((members, capacity, TILE, width), frames.dtype).at[my_target, my_slot].set(tiles)
    )
    outgoing_ids = (
        jnp.zeros((members, capacity, tile_ids.shape[2]), jnp.int32)
        .at[my_target, my_slot]
        .set(tile_ids[0])
    )
    outgoing_counts = (
        jnp.zeros((members, capacity), jnp.int32).at[my_target, my_slot].set(tile_counts[0])
    )
    incoming_tiles, incoming_ids, incoming_counts = (
        lax.all_to_all(outgoing_tiles, "frames", split_axis=0, concat_axis=0, tiled=True),
        lax.all_to_all(outgoing_ids, "frames", split_axis=0, concat_axis=0, tiled=True),
        lax.all_to_all(outgoing_counts, "frames", split_axis=0, concat_axis=0, tiled=True),
    )
    placed_tiles = incoming_tiles[sender, sender_slot]
    placed_ids = incoming_ids[sender, sender_slot]
    placed_counts = incoming_counts[sender, sender_slot]
    first, second = all_tiles(placed_tiles, placed_ids, placed_counts, group_rows, group_norm)
    first, second = across_groups(first, second)
    return (first.reshape(-1), second.reshape(-1))


def column_of(squares):
    total = squares[:, 0:TILE]
    for at_lane in range(TILE, squares.shape[1], TILE):
        total = total + squares[:, at_lane : at_lane + TILE]
    return jnp.sum(total.T, axis=0, keepdims=True)


def row_pair(one, two):
    one, two = one.T, two.T
    rows = one.shape[0]
    while rows > 8:
        half = rows // 2
        one, two = fold_two(one[:half], two[:half], one[half:], two[half:])
        rows = half
    for shift in (4, 2, 1):
        one, two = fold_two(one, two, pltpu.roll(one, shift, 0), pltpu.roll(two, shift, 0))
    return one[0:1], two[0:1]


def prepare_kernel(members, where_ref, ids_ref, counts_ref, group_ref, lists_ref, norms_ref):
    tiles_here = group_ref.shape[0] // TILE
    lanes = lists_ref.shape[1] // members
    member = where_ref[0]

    def split(tile, _):
        def take(at, numbers):
            entry = ids_ref[tile, at]
            owner = entry // tiles_here
            distance = jnp.bitwise_xor(owner, member)
            place = jnp.int32(0)
            for shard in range(members):
                place = jnp.where(distance == shard, numbers[shard], place)
            lists_ref[tile, distance * lanes + place] = entry - owner * tiles_here
            return tuple(
                numbers[shard] + (distance == shard).astype(jnp.int32) for shard in range(members)
            )

        numbers = lax.fori_loop(0, counts_ref[0, tile], take, (jnp.int32(0),) * members)
        for shard in range(members):
            lists_ref[tile, shard * lanes + lanes - 1] = numbers[shard]
        return 0

    lax.fori_loop(0, ids_ref.shape[0], split, 0)

    for tile in range(tiles_here):
        rows = group_ref[tile * TILE : (tile + 1) * TILE, :].astype(jnp.float32)
        norms_ref[tile : tile + 1, :] = 0.5 * column_of(rows * rows)


def search_tile(frame_tile, slots, zslot, tile, lists_ref, rows_ref, norms_ref, dummy, base):
    last_lane = lists_ref.shape[3] - 1
    tiles_here = base
    ends = []
    number = jnp.int32(0)
    for slot in slots:
        number = number + lists_ref[zslot, slot, tile, last_lane]
        ends.append(number)

    def block(at, carry):
        one, two = carry
        picked, picked_norm = [], []
        for step in range(unroll):
            place = at * unroll + step
            live = place < number
            slot = jnp.int32(slots[0])
            start = jnp.int32(0)
            for index in range(1, len(slots)):
                beyond = place >= ends[index - 1]
                slot = jnp.where(beyond, slots[index], slot)
                start = jnp.where(beyond, ends[index - 1], start)
            place = jnp.where(live, place - start, 0)
            entry = lists_ref[zslot, slot, tile, place] + (slot - slots[0]) * tiles_here
            entry = jnp.where(live, entry, 0)
            picked.append(rows_ref[pl.ds(pl.multiple_of(entry * TILE, TILE), TILE), :])
            picked_norm.append(norms_ref[pl.ds(jnp.where(live, entry, dummy), 1), :])
        inner = lax.dot_general(
            frame_tile,
            jnp.concatenate(picked, axis=0),
            (((1,), (1,)), ((), ())),
            preferred_element_type=jnp.float32,
        )
        for step in range(unroll):
            part = picked_norm[step] - inner[:, step * TILE : (step + 1) * TILE]
            two = jnp.minimum(two, jnp.maximum(one, part))
            one = jnp.minimum(one, part)
        return one, two

    empty = jnp.full((TILE, TILE), big_value, jnp.float32)
    return lax.fori_loop(0, (number + unroll - 1) // unroll, block, (empty, empty))


def near_kernel(
    lists_ref, norms_in, own_group, near_group, own_frames, frames_1, frames_2,
    out_ref, rows_buf, frames_buf, norms_buf, sems,
):
    tile_rows = own_group.shape[0]
    tiles_here = tile_rows // TILE
    quarter = own_frames.shape[0]
    quarter_tiles = quarter // TILE
    copies = [
        pltpu.make_async_copy(own_group, rows_buf.at[pl.ds(0, tile_rows)], sems.at[0]),
        pltpu.make_async_copy(near_group, rows_buf.at[pl.ds(tile_rows, tile_rows)], sems.at[1]),
    ]
    for index, ref in enumerate((own_frames, frames_1, frames_2)):
        copies.append(
            pltpu.make_async_copy(
                ref, frames_buf.at[pl.ds(index * quarter, quarter)], sems.at[2 + index]
            )
        )
    for copy in copies:
        copy.start()
    dummy = 2 * tiles_here
    norms_buf[pl.ds(0, tiles_here), :] = norms_in[0]
    norms_buf[pl.ds(tiles_here, tiles_here), :] = norms_in[1]
    norms_buf[pl.ds(dummy, 1), :] = jnp.full((1, TILE), big_value, jnp.float32)
    out_ref[...] = jnp.full(out_ref.shape, big_value, jnp.float32)
    for copy in copies:
        copy.wait()

    def one_tile(index, _):
        zslot = index // quarter_tiles
        tile = index - zslot * quarter_tiles
        frame_tile = frames_buf[pl.ds(pl.multiple_of(index * TILE, TILE), TILE), :]
        one, two = search_tile(
            frame_tile, (0, 1), zslot, tile, lists_ref, rows_buf, norms_buf, dummy, tiles_here
        )
        one, two = row_pair(one, two)
        squares = frame_tile.astype(jnp.float32)
        out_ref[0, pl.ds(index, 1), :] = one
        out_ref[1, pl.ds(index, 1), :] = two
        out_ref[2, pl.ds(index, 1), :] = column_of(squares * squares)
        return 0

    lax.fori_loop(0, 3 * quarter_tiles, one_tile, 0)


def far_kernel(
    where_ref, lists_ref, norms_in, before_ref, own_group, near_group, far_a, far_b, far_c,
    last_a, last_b, last_c, own_frames, frames_1, frames_2, frames_3a, frames_3b,
    out_ref, rows_buf, frames_buf, norms_buf, found_buf, sems,
):
    tile_rows = own_group.shape[0]
    tiles_here = tile_rows // TILE
    groups = norms_in.shape[0]
    quarter = own_frames.shape[0]
    quarter_tiles = quarter // TILE
    width = own_frames.shape[1]
    members = frames_buf.shape[0] // quarter
    member = where_ref[0]
    slab = where_ref[2]
    side = far_a.shape[0]
    middle = far_b.shape[0]
    near_side = slab * (tile_rows - side)
    other_side = (1 - slab) * (tile_rows - side)

    copies = []

    def bring(source, target, start, rows):
        copies.append(
            pltpu.make_async_copy(
                source, target.at[pl.ds(pl.multiple_of(start, TILE), rows)], sems.at[len(copies)]
            )
        )

    for slot, (first_piece, second_piece, third_piece) in (
        (2, (far_a, far_b, far_c)),
        (3, (last_a, last_b, last_c)),
    ):
        bring(first_piece, rows_buf, slot * tile_rows + near_side, side)
        bring(second_piece, rows_buf, slot * tile_rows + side, middle)
        bring(third_piece, rows_buf, slot * tile_rows + other_side, side)
    bring(own_frames, frames_buf, 0, quarter)
    bring(frames_1, frames_buf, quarter, quarter)
    bring(frames_2, frames_buf, 2 * quarter, quarter)
    early = len(copies)
    bring(own_group, rows_buf, 0, tile_rows)
    bring(near_group, rows_buf, tile_rows, tile_rows)
    for copy in copies[:early]:
        copy.start()
    inner_member = jnp.logical_and(member > 0, member < members - 1)
    last_sem = sems.at[len(copies)]
    last_target = frames_buf.at[pl.ds(3 * quarter, quarter)]

    @pl.when(inner_member)
    def _():
        pltpu.make_async_copy(frames_3a, last_target, last_sem).start()

    @pl.when(jnp.logical_not(inner_member))
    def _():
        pltpu.make_async_copy(frames_3b, last_target, last_sem).start()

    for copy in copies[early:]:
        copy.start()

    dummy = groups * tiles_here
    for slot in range(groups):
        norms_buf[pl.ds(slot * tiles_here, tiles_here), :] = norms_in[slot]
    norms_buf[pl.ds(dummy, 1), :] = jnp.full((1, TILE), big_value, jnp.float32)
    found_buf[...] = before_ref[...]
    for copy in copies[:early]:
        copy.wait()

    far_rows = rows_buf.at[pl.ds(2 * tile_rows, 2 * tile_rows)]
    far_norms = norms_buf.at[pl.ds(2 * tiles_here, 2 * tiles_here + 8)]

    def one_tile(index, _):
        zslot = index // quarter_tiles
        tile = index - zslot * quarter_tiles
        frame_tile = frames_buf[pl.ds(pl.multiple_of(index * TILE, TILE), TILE), :]
        one, two = search_tile(
            frame_tile, (2, 3), zslot, tile, lists_ref, far_rows, far_norms, 2 * tiles_here, tiles_here
        )
        one, two = row_pair(one, two)
        one, two = fold_two(
            one, two, found_buf[0, pl.ds(index, 1), :], found_buf[1, pl.ds(index, 1), :]
        )
        found_buf[0, pl.ds(index, 1), :] = one
        found_buf[1, pl.ds(index, 1), :] = two
        return 0

    lax.fori_loop(0, 3 * quarter_tiles, one_tile, 0)
    pltpu.make_async_copy(frames_3a, last_target, last_sem).wait()
    for copy in copies[early:]:
        copy.wait()

    def last_tile(tile, _):
        index = 3 * quarter_tiles + tile
        frame_tile = frames_buf[pl.ds(pl.multiple_of(index * TILE, TILE), TILE), :]
        one, two = search_tile(
            frame_tile, tuple(range(groups)), 3, tile, lists_ref, rows_buf, norms_buf, dummy, tiles_here
        )
        one, two = row_pair(one, two)
        squares = frame_tile.astype(jnp.float32)
        found_buf[0, pl.ds(index, 1), :] = one
        found_buf[1, pl.ds(index, 1), :] = two
        found_buf[2, pl.ds(index, 1), :] = column_of(squares * squares)
        return 0

    lax.fori_loop(0, quarter_tiles, last_tile, 0)
    norm = found_buf[2]
    found_buf[0] = (norm + 2.0 * found_buf[0]) / width
    found_buf[1] = (norm + 2.0 * found_buf[1]) / width
    for index in range(members * quarter_tiles):
        block_of = jnp.bitwise_xor(member, index // quarter_tiles)
        row = block_of * quarter_tiles + index % quarter_tiles
        out_ref[0, pl.ds(row, 1), :] = found_buf[0, index : index + 1, :]
        out_ref[1, pl.ds(row, 1), :] = found_buf[1, index : index + 1, :]


def pick_kernel(where_ref, plan_ref, part_0, part_1, part_2, part_3, first_ref, second_ref, every):
    member = where_ref[0]
    piece = where_ref[1]
    blocks = first_ref.shape[0]
    parts = (part_0, part_1, part_2, part_3)
    quarter_tiles = blocks // len(parts)
    rows = part_0.shape[1]
    for slot, part in enumerate(parts):
        every[:, slot * rows : (slot + 1) * rows, :] = part[...]
    for place in range(blocks):
        tile = plan_ref[member * blocks + place]
        block_of = tile // blocks
        inside = tile - block_of * blocks
        part = inside // quarter_tiles
        row = jnp.bitwise_xor(part, piece) * rows + block_of * quarter_tiles + (inside - part * quarter_tiles)
        first_ref[pl.ds(place, 1), :] = every[0, pl.ds(row, 1), :]
        second_ref[pl.ds(place, 1), :] = every[1, pl.ds(row, 1), :]


def exchanged(number, distance):
    return [(at, at ^ distance) for at in range(number)]


def gathered_frames(frames, medoids, tile_ids, tile_counts, plan):
    width = frames.shape[1]
    blocks = frames.shape[0] // TILE
    members = lax.axis_size("frames")
    groups = lax.axis_size("medoids")
    member = lax.axis_index("frames")
    piece = lax.axis_index("medoids")
    slab = lax.axis_index("slab")
    rows = medoids[0]
    tile_rows = rows.shape[0]
    quarter_tiles = blocks // groups
    quarter = quarter_tiles * TILE
    side = tile_rows // TILE // 3 * TILE

    mine = lax.dynamic_slice_in_dim(frames, piece * quarter, quarter)
    frames_2 = lax.ppermute(mine, "frames", exchanged(members, 2))
    frames_1 = lax.ppermute(mine, "frames", exchanged(members, 1))
    frames_3a = lax.ppermute(mine, "frames", [(1, 2), (2, 1)])
    frames_3b = lax.ppermute(frames_2, "frames", [(2, 3), (1, 0)])

    edge = lax.dynamic_slice_in_dim(rows, slab * (tile_rows - side), side)
    far_a = lax.ppermute(edge, "medoids", exchanged(groups, 2))
    far_b = lax.ppermute(rows[side : tile_rows - side], "medoids", exchanged(groups, 2))
    far_c = lax.ppermute(far_a, "slab", exchanged(2, 1))
    near_group = lax.ppermute(rows, "medoids", exchanged(groups, 1))
    last_a = lax.ppermute(far_a, "medoids", exchanged(groups, 1))
    last_b = lax.ppermute(far_b, "medoids", exchanged(groups, 1))
    last_c = lax.ppermute(far_c, "medoids", exchanged(groups, 1))

    where = jnp.stack([member, piece, slab]).astype(jnp.int32)
    hbm = pl.BlockSpec(memory_space=pl.ANY)
    scalar = pl.BlockSpec(memory_space=pltpu.SMEM)
    vector = pl.BlockSpec(memory_space=pltpu.VMEM)
    tiles_here = tile_rows // TILE
    lanes = TILE // members
    listed, norms = pl.pallas_call(
        functools.partial(prepare_kernel, members),
        out_shape=(
            jax.ShapeDtypeStruct((blocks, members * lanes), jnp.int32),
            jax.ShapeDtypeStruct((tiles_here, TILE), jnp.float32),
        ),
        in_specs=[scalar, scalar, scalar, vector],
        out_specs=(scalar, vector),
        name="prepare",
    )(where, tile_ids[0], tile_counts, rows)
    packed = jnp.concatenate([listed.astype(jnp.float32), norms], axis=0)
    pair = jnp.stack([packed, lax.ppermute(packed, "medoids", exchanged(groups, 1))])
    far_pair = lax.ppermute(pair, "medoids", exchanged(groups, 2))
    packed = jnp.concatenate([pair, far_pair], axis=0)
    norms = packed[:, blocks:]
    lists = lax.dynamic_slice_in_dim(packed, piece * quarter_tiles, quarter_tiles, axis=1)
    lists = lists.astype(jnp.int32).reshape(groups, quarter_tiles, members, lanes)
    lists = jnp.stack(
        [lists[:, :, 0]]
        + [lax.ppermute(lists[:, :, at], "frames", exchanged(members, at)) for at in (1, 2, 3)]
    )

    total_tiles = members * quarter_tiles
    before = pl.pallas_call(
        near_kernel,
        out_shape=jax.ShapeDtypeStruct((3, total_tiles, TILE), jnp.float32),
        in_specs=[scalar, vector] + [hbm] * 5,
        out_specs=vector,
        scratch_shapes=[
            pltpu.VMEM((2 * tile_rows, width), jnp.bfloat16),
            pltpu.VMEM((3 * quarter, width), jnp.bfloat16),
            pltpu.VMEM((2 * tiles_here + 8, TILE), jnp.float32),
            pltpu.SemaphoreType.DMA((5,)),
        ],
        name="near_search",
    )(lists, norms, rows, near_group, mine, frames_1, frames_2)
    found = pl.pallas_call(
        far_kernel,
        out_shape=jax.ShapeDtypeStruct((2, total_tiles, TILE), jnp.float32),
        in_specs=[scalar, scalar, vector, vector] + [hbm] * 13,
        out_specs=vector,
        scratch_shapes=[
            pltpu.VMEM((groups * tile_rows, width), jnp.bfloat16),
            pltpu.VMEM((members * quarter, width), jnp.bfloat16),
            pltpu.VMEM((groups * tiles_here + 8, TILE), jnp.float32),
            pltpu.VMEM((3, total_tiles, TILE), jnp.float32),
            pltpu.SemaphoreType.DMA((16,)),
        ],
        name="far_search",
    )(
        where, lists, norms, before, rows, near_group, far_a, far_b, far_c, last_a, last_b, last_c,
        mine, frames_1, frames_2, frames_3a, frames_3b,
    )

    one, two = found[0], found[1]
    for at in (1, 2, 3):
        other = lax.ppermute(found, "frames", exchanged(members, at))
        one, two = fold_two(one, two, other[0], other[1])
    merged = jnp.stack([one, two])
    parts = [merged] + [lax.ppermute(merged, "medoids", exchanged(groups, at)) for at in (1, 2, 3)]
    first, second = pl.pallas_call(
        pick_kernel,
        out_shape=(jax.ShapeDtypeStruct((blocks, TILE), jnp.float32),) * 2,
        in_specs=[scalar, scalar] + [vector] * 4,
        out_specs=(vector, vector),
        scratch_shapes=[pltpu.VMEM((2, groups * members * quarter_tiles, TILE), jnp.float32)],
        name="pick",
    )(where, plan, *parts)
    return (first.reshape(-1), second.reshape(-1))


def solution(mesh):
    placed = (
        P(("slab", "frames"), None),
        P("medoids", "frames", None),
        P("medoids", ("slab", "frames"), None),
        P("medoids", ("slab", "frames")),
        P("slab"),
    )

    def per_device(frames, medoids, tile_ids, tile_counts, plan):
        blocks = frames.shape[0] // TILE
        quarters = mesh.shape["frames"] == 4 and mesh.shape["medoids"] == 4 and mesh.shape["slab"] == 2
        if quarters and blocks % 4 == 0 and medoids.shape[1] // TILE >= 3:
            return gathered_frames(frames, medoids, tile_ids, tile_counts, plan)
        return gathered_medoids(frames, medoids, tile_ids, tile_counts, plan)

    return jax.shard_map(
        per_device,
        mesh=mesh,
        in_specs=placed,
        out_specs=(P(("slab", "frames")), P(("slab", "frames"))),
        check_vma=False,
    )
```

profile of v0, /device:TPU:0, one launch (start us, length us, event | category | flops | bytes accessed | tf_op | source)
XLA Modules:
  0.0 111.8 jit_solution(15423842863703960085)
XLA Ops:
  0.6 0.0 copy-start
  0.6 0.6 collective-permute-start.5
  1.2 2.0 %dynamic-slice_bitcast_fusion = bf16[640,512]{1,0:T(8,128)(2,1)} fusion(bf16[1,2048,512]{2,1,0:T(8,128)(2,1)} %param.6, s32[]{:T(128)S(6)} %select_n.11), kind=kLoop, calls=%fused_computation.1 | loop fusion | bytes 1310724 | tf_op jit(solution)/shard_map/dynamic_slice | solution.py:415
  3.2 2.6 %collective-permute-start.8 = (bf16[640,512]{1,0:T(8,128)(2,1)}, bf16[640,512]{1,0:T(8,128)(2,1)}, u32[]{:S(2)}, u32[]{:S(2)}) collective-permute-start(bf16[640,512]{1,0:T(8,128)(2,1)} %dynamic-slice_bitcast_fusion), channel_id=1, source_target_pairs={{0,2},{1,3},{2,0},{3,1},{4,6},{5,7},{6,4},{7,5},{8,10},{9,11},{10,... | collective-permute-start | bytes 1966088 | tf_op jit(solution)/shard_map/ppermute | solution.py:416
  5.8 0.6 pad_add_fusion.1.where_ref
  6.4 7.0 %prepare.1 = (s32[16,128]{1,0:T(8,128)}, f32[16,128]{1,0:T(8,128)}) custom-call(s32[3]{0:T(128)} %pad_add_fusion.1.where_ref, s32[16,24]{1,0:T(8,128)} %bitcast.36, s32[1,16]{1,0:T(1,128)} %counts_ref.1, bf16[2048,512]{1,0:T(8,128)(2,1)} %bitcast.30), custom_call_target="tpu_custom_call" | custom-call | tf_op jit(solution)/shard_map/prepare/pallas_call | solution.py:430
  13.4 0.7 convert_element_type.6
  14.1 0.7 fusion.3
  14.8 0.5 collective-permute-start
  15.3 2.1 %slice_bitcast_fusion = bf16[768,512]{1,0:T(8,128)(2,1)} fusion(bf16[1,2048,512]{2,1,0:T(8,128)(2,1)} %param.6), kind=kLoop, calls=%fused_computation | loop fusion | bytes 1572864 | tf_op jit(solution)/shard_map/slice | solution.py:417
  17.4 1.2 %collective-permute-start.9 = (bf16[768,512]{1,0:T(8,128)(2,1)}, bf16[768,512]{1,0:T(8,128)(2,1)}, u32[]{:S(2)}, u32[]{:S(2)}) collective-permute-start(bf16[768,512]{1,0:T(8,128)(2,1)} %slice_bitcast_fusion), channel_id=1, source_target_pairs={{0,2},{1,3},{2,0},{3,1},{4,6},{5,7},{6,4},{7,5},{8,10},{9,11},{10,... | collective-permute-start | bytes 2359304 | tf_op jit(solution)/shard_map/ppermute | solution.py:417
  18.6 0.0 collective-permute-done
  18.6 0.9 collective-permute-start.1
  19.5 0.0 copy-done
  19.5 0.0 copy-start.1
  19.5 0.8 collective-permute-start.7
  20.4 18.5 %collective-permute-done.1 = f32[2,32,128]{2,1,0:T(8,128)S(1)} collective-permute-done((f32[2,32,128]{2,1,0:T(8,128)S(1)}, f32[2,32,128]{2,1,0:T(8,128)S(1)}, u32[]{:S(2)}, u32[]{:S(2)}) %collective-permute-start.1) | collective-permute-done | bytes 32800 | tf_op jit(solution)/shard_map/ppermute | solution.py:442
  38.8 0.0 collective-permute-done.8.far_a
  38.8 1.9 %collective-permute-start.10 = (bf16[640,512]{1,0:T(8,128)(2,1)}, bf16[640,512]{1,0:T(8,128)(2,1)}, u32[]{:S(2)}, u32[]{:S(2)}) collective-permute-start(bf16[640,512]{1,0:T(8,128)(2,1)} %collective-permute-done.8.far_a), channel_id=1, source_target_pairs={{0,16},{16,0},{1,17},{17,1},{2,18},{18,2},{3,19},{19,3},{4,20},{20... | collective-permute-start | bytes 1966088 | tf_op jit(solution)/shard_map/ppermute | solution.py:418
  40.7 0.1 reshape.15
  40.8 2.6 %collective-permute-start.3 = (s32[4,4,32]{2,1,0:T(4,128)S(1)}, s32[4,4,32]{2,1,0:T(4,128)S(1)}, u32[]{:S(2)}, u32[]{:S(2)}) collective-permute-start(s32[4,4,32]{2,1,0:T(4,128)S(1)} %bitcast.42), channel_id=1, source_target_pairs={{0,8},{4,12},{8,0},{12,4},{1,9},{5,13},{9,1},{13,5},{2,10},{6,14},... | collective-permute-start | bytes 6152 | tf_op jit(solution)/shard_map/ppermute | solution.py:449
  43.5 2.0 %collective-permute-done.3 = s32[4,4,32]{2,1,0:T(4,128)S(1)} collective-permute-done((s32[4,4,32]{2,1,0:T(4,128)S(1)}, s32[4,4,32]{2,1,0:T(4,128)S(1)}, u32[]{:S(2)}, u32[]{:S(2)}) %collective-permute-start.3) | collective-permute-done | bytes 2080 | tf_op jit(solution)/shard_map/ppermute | solution.py:449
  45.4 1.5 %collective-permute-start.2 = (s32[4,4,32]{2,1,0:T(4,128)S(1)}, s32[4,4,32]{2,1,0:T(4,128)S(1)}, u32[]{:S(2)}, u32[]{:S(2)}) collective-permute-start(s32[4,4,32]{2,1,0:T(4,128)S(1)} %bitcast.41), channel_id=1, source_target_pairs={{0,4},{4,0},{8,12},{12,8},{1,5},{5,1},{9,13},{13,9},{2,6},{6,2},{1... | collective-permute-start | bytes 6152 | tf_op jit(solution)/shard_map/ppermute | solution.py:449
  47.0 2.1 %collective-permute-done.2 = s32[4,4,32]{2,1,0:T(4,128)S(1)} collective-permute-done((s32[4,4,32]{2,1,0:T(4,128)S(1)}, s32[4,4,32]{2,1,0:T(4,128)S(1)}, u32[]{:S(2)}, u32[]{:S(2)}) %collective-permute-start.2) | collective-permute-done | bytes 2080 | tf_op jit(solution)/shard_map/ppermute | solution.py:449
  49.1 3.6 %collective-permute-start.4 = (s32[4,4,32]{2,1,0:T(4,128)S(1)}, s32[4,4,32]{2,1,0:T(4,128)S(1)}, u32[]{:S(2)}, u32[]{:S(2)}) collective-permute-start(s32[4,4,32]{2,1,0:T(4,128)S(1)} %bitcast.40), channel_id=1, source_target_pairs={{0,12},{4,8},{8,4},{12,0},{1,13},{5,9},{9,5},{13,1},{2,14},{6,10},... | collective-permute-start | bytes 6152 | tf_op jit(solution)/shard_map/ppermute | solution.py:449
  52.7 2.0 %collective-permute-done.4 = s32[4,4,32]{2,1,0:T(4,128)S(1)} collective-permute-done((s32[4,4,32]{2,1,0:T(4,128)S(1)}, s32[4,4,32]{2,1,0:T(4,128)S(1)}, u32[]{:S(2)}, u32[]{:S(2)}) %collective-permute-start.4) | collective-permute-done | bytes 2080 | tf_op jit(solution)/shard_map/ppermute | solution.py:449
  54.7 0.0 collective-permute-start.6
  54.7 0.0 collective-permute-done.9.far_b
  54.7 0.0 collective-permute-start.12
  54.7 0.0 collective-permute-done.7.frames_2
  54.7 0.0 copy-start.2
  54.7 0.5 collective-permute-start.11
  55.2 0.5 collective-permute-done.10.far_c
  55.7 0.0 collective-permute-start.13
  55.7 9.2 %collective-permute-done.6.frames_1 = bf16[512,512]{1,0:T(8,128)(2,1)S(1)} collective-permute-done((bf16[512,512]{1,0:T(8,128)(2,1)S(1)}, bf16[512,512]{1,0:T(8,128)(2,1)S(1)}, u32[]{:S(2)}, u32[]{:S(2)}) %collective-permute-start.6) | collective-permute-done | bytes 524320 | tf_op jit(solution)/shard_map/ppermute | solution.py:411
  64.9 1.5 %collective-permute-start.14 = (bf16[512,512]{1,0:T(8,128)(2,1)S(1)}, bf16[512,512]{1,0:T(8,128)(2,1)}, u32[]{:S(2)}, u32[]{:S(2)}) collective-permute-start(bf16[512,512]{1,0:T(8,128)(2,1)S(1)} %constant_dynamic-slice_fusion.own_frames), channel_id=1, source_target_pairs={{4,8},{8,4},{5,9},{9,5},{6,10},{10,6},{7,11},{11,7},{20,24},{24,20... | collective-permute-start | bytes 1572872 | tf_op jit(solution)/shard_map/ppermute | solution.py:412
  66.4 0.0 collective-permute-done.5.near_group
  66.4 1.3 %collective-permute-start.15 = (bf16[512,512]{1,0:T(8,128)(2,1)S(1)}, bf16[512,512]{1,0:T(8,128)(2,1)}, u32[]{:S(2)}, u32[]{:S(2)}) collective-permute-start(bf16[512,512]{1,0:T(8,128)(2,1)S(1)} %collective-permute-done.7.frames_2), channel_id=1, source_target_pairs={{8,12},{4,0},{9,13},{5,1},{10,14},{6,2},{11,15},{7,3},{24,28},{20,... | collective-permute-start | bytes 1572872 | tf_op jit(solution)/shard_map/ppermute | solution.py:413
  67.7 0.6 slice.64.norms_in
  68.3 0.6 pad_add_fusion.lists_ref
  69.0 13.1 %near_search.1.before_ref = f32[3,16,128]{2,1,0:T(8,128)} custom-call(s32[4,4,4,32]{3,2,1,0:T(4,128)} %pad_add_fusion.lists_ref, f32[4,16,128]{2,1,0:T(8,128)} %slice.64.norms_in, bf16[2048,512]{1,0:T(8,128)(2,1)} %bitcast.31, bf16[2048,512]{1,0:T(8,128)(2,1)} %collective-permute-done.5.near_group, bf16[512,512]{1,0:T(8,128)(2,1)} %copy-done.1, ...), custom_call_target="tpu_custom_call" | custom-call | tf_op jit(solution)/shard_map/near_search/pallas_call | solution.py:453
  82.1 0.0 collective-permute-done.14.frames_3a
  82.1 0.0 collective-permute-done.15.frames_3b
  82.1 0.0 collective-permute-done.11.last_a
  82.1 0.0 collective-permute-done.12.last_b
  82.2 0.0 collective-permute-done.13.last_c
  82.2 13.1 %far_search.1 = f32[2,16,128]{2,1,0:T(8,128)} custom-call(s32[3]{0:T(128)} %pad_add_fusion.1.where_ref, s32[4,4,4,32]{3,2,1,0:T(4,128)} %pad_add_fusion.lists_ref, f32[4,16,128]{2,1,0:T(8,128)} %slice.64.norms_in, f32[3,16,128]{2,1,0:T(8,128)} %near_search.1.before_ref, bf16[2048,512]{1,0:T(8,128)(2,1)} %bitcast.32, ...), custom_call_target="tpu_custom_call" | custom-call | tf_op jit(solution)/shard_map/far_search/pallas_call | solution.py:466
  95.3 2.8 %collective-permute-start.18 = (f32[2,16,128]{2,1,0:T(8,128)}, f32[2,16,128]{2,1,0:T(8,128)S(1)}, u32[]{:S(2)}, u32[]{:S(2)}) collective-permute-start(f32[2,16,128]{2,1,0:T(8,128)} %far_search.1), channel_id=1, source_target_pairs={{0,12},{4,8},{8,4},{12,0},{1,13},{5,9},{9,5},{13,1},{2,14},{6,10},... | collective-permute-start | bytes 49160 | tf_op jit(solution)/shard_map/ppermute | solution.py:486
  98.0 2.3 %collective-permute-start.17 = (f32[2,16,128]{2,1,0:T(8,128)}, f32[2,16,128]{2,1,0:T(8,128)S(1)}, u32[]{:S(2)}, u32[]{:S(2)}) collective-permute-start(f32[2,16,128]{2,1,0:T(8,128)} %far_search.1), channel_id=1, source_target_pairs={{0,8},{4,12},{8,0},{12,4},{1,9},{5,13},{9,1},{13,5},{2,10},{6,14},... | collective-permute-start | bytes 49160 | tf_op jit(solution)/shard_map/ppermute | solution.py:486
  100.4 0.3 collective-permute-start.16
  100.7 0.4 collective-permute-done.18
  101.1 1.8 %collective-permute-done.17 = f32[2,16,128]{2,1,0:T(8,128)S(1)} collective-permute-done((f32[2,16,128]{2,1,0:T(8,128)}, f32[2,16,128]{2,1,0:T(8,128)S(1)}, u32[]{:S(2)}, u32[]{:S(2)}) %collective-permute-start.17) | collective-permute-done | bytes 16416 | tf_op jit(solution)/shard_map/ppermute | solution.py:486
  102.9 1.4 %collective-permute-done.16 = f32[2,16,128]{2,1,0:T(8,128)S(1)} collective-permute-done((f32[2,16,128]{2,1,0:T(8,128)}, f32[2,16,128]{2,1,0:T(8,128)S(1)}, u32[]{:S(2)}, u32[]{:S(2)}) %collective-permute-start.16) | collective-permute-done | bytes 16416 | tf_op jit(solution)/shard_map/ppermute | solution.py:486
  104.3 0.7 slice_minimum_fusion.3
  105.1 0.0 copy-start.4
  105.1 0.1 collective-permute-start.21
  105.2 0.7 collective-permute-start.20
  105.8 1.2 %collective-permute-start.19 = (f32[2,16,128]{2,1,0:T(8,128)S(1)}, f32[2,16,128]{2,1,0:T(8,128)S(1)}, u32[]{:S(2)}, u32[]{:S(2)}) collective-permute-start(f32[2,16,128]{2,1,0:T(8,128)S(1)} %pad_maximum_fusion.3.part_0), channel_id=1, source_target_pairs={{0,1},{1,0},{2,3},{3,2},{4,5},{5,4},{6,7},{7,6},{8,9},{9,8},{10,11... | collective-permute-start | bytes 49160 | tf_op jit(solution)/shard_map/ppermute | solution.py:489
  107.0 1.3 %collective-permute-done.21.part_3 = f32[2,16,128]{2,1,0:T(8,128)S(1)} collective-permute-done((f32[2,16,128]{2,1,0:T(8,128)S(1)}, f32[2,16,128]{2,1,0:T(8,128)S(1)}, u32[]{:S(2)}, u32[]{:S(2)}) %collective-permute-start.21) | collective-permute-done | bytes 16416 | tf_op jit(solution)/shard_map/ppermute | solution.py:489
  108.3 0.7 collective-permute-done.20.part_2
  109.0 0.0 collective-permute-done.19.part_1
  109.0 0.6 copy-done.6
  109.6 0.6 copy-done.7
  110.2 1.6 %pick.1 = (f32[16,128]{1,0:T(8,128)}, f32[16,128]{1,0:T(8,128)}) custom-call(s32[3]{0:T(128)} %pad_add_fusion.1.where_ref, s32[64]{0:T(128)} %plan_ref.1, f32[2,16,128]{2,1,0:T(8,128)} %copy-done.4, f32[2,16,128]{2,1,0:T(8,128)} %copy-done.7, f32[2,16,128]{2,1,0:T(8,128)} %copy-done.6, f32[2,16,128]{2,1,0:T(8,128)} %copy-done.5), custom_call_target="tpu_custom_call" | custom-call | tf_op jit(solution)/shard_map/pick/pallas_call | solution.py:490
  (15 shorter events, 0.1 us)
Async XLA Ops:
  0.6 18.8 %copy-start = (bf16[2048,512]{1,0:T(8,128)(2,1)S(1)}, bf16[2048,512]{1,0:T(8,128)(2,1)}, u32[]{:S(2)}) copy-start(bf16[2048,512]{1,0:T(8,128)(2,1)} %param.5) | copy-start | bytes 6291460
  0.6 65.8 %collective-permute-start.5 = (bf16[2048,512]{1,0:T(8,128)(2,1)}, bf16[2048,512]{1,0:T(8,128)(2,1)}, u32[]{:S(2)}, u32[]{:S(2)}) collective-permute-start(bf16[2048,512]{1,0:T(8,128)(2,1)} %bitcast.29), channel_id=1, source_target_pairs={{0,1},{1,0},{2,3},{3,2},{4,5},{5,4},{6,7},{7,6},{8,9},{9,8},{10,11... | collective-permute-start | bytes 6291464 | tf_op jit(solution)/shard_map/ppermute | solution.py:419
  3.2 35.6 %collective-permute-start.8 = (bf16[640,512]{1,0:T(8,128)(2,1)}, bf16[640,512]{1,0:T(8,128)(2,1)}, u32[]{:S(2)}, u32[]{:S(2)}) collective-permute-start(bf16[640,512]{1,0:T(8,128)(2,1)} %dynamic-slice_bitcast_fusion), channel_id=1, source_target_pairs={{0,2},{1,3},{2,0},{3,1},{4,6},{5,7},{6,4},{7,5},{8,10},{9,11},{10,... | collective-permute-start | bytes 1966088 | tf_op jit(solution)/shard_map/ppermute | solution.py:416
  14.8 3.8 %collective-permute-start = (f32[32,128]{1,0:T(8,128)S(1)}, f32[32,128]{1,0:T(8,128)S(1)}, u32[]{:S(2)}, u32[]{:S(2)}) collective-permute-start(f32[32,128]{1,0:T(8,128)S(1)} %get-tuple-element.17), channel_id=1, source_target_pairs={{0,1},{1,0},{2,3},{3,2},{4,5},{5,4},{6,7},{7,6},{8,9},{9,8},{10,11... | collective-permute-start | bytes 49160 | tf_op jit(solution)/shard_map/ppermute | solution.py:441
  17.4 37.2 %collective-permute-start.9 = (bf16[768,512]{1,0:T(8,128)(2,1)}, bf16[768,512]{1,0:T(8,128)(2,1)}, u32[]{:S(2)}, u32[]{:S(2)}) collective-permute-start(bf16[768,512]{1,0:T(8,128)(2,1)} %slice_bitcast_fusion), channel_id=1, source_target_pairs={{0,2},{1,3},{2,0},{3,1},{4,6},{5,7},{6,4},{7,5},{8,10},{9,11},{10,... | collective-permute-start | bytes 2359304 | tf_op jit(solution)/shard_map/ppermute | solution.py:417
  18.6 20.2 %collective-permute-start.1 = (f32[2,32,128]{2,1,0:T(8,128)S(1)}, f32[2,32,128]{2,1,0:T(8,128)S(1)}, u32[]{:S(2)}, u32[]{:S(2)}) collective-permute-start(f32[2,32,128]{2,1,0:T(8,128)S(1)} %pad_maximum_fusion.1), channel_id=1, source_target_pairs={{0,2},{1,3},{2,0},{3,1},{4,6},{5,7},{6,4},{7,5},{8,10},{9,11},{10,... | collective-permute-start | bytes 98312 | tf_op jit(solution)/shard_map/ppermute | solution.py:442
  19.5 49.5 %copy-start.1 = (bf16[512,512]{1,0:T(8,128)(2,1)}, bf16[512,512]{1,0:T(8,128)(2,1)S(1)}, u32[]{:S(2)}) copy-start(bf16[512,512]{1,0:T(8,128)(2,1)S(1)} %constant_dynamic-slice_fusion.own_frames) | copy-start | bytes 1572868
  19.5 35.2 %collective-permute-start.7 = (bf16[512,512]{1,0:T(8,128)(2,1)S(1)}, bf16[512,512]{1,0:T(8,128)(2,1)S(1)}, u32[]{:S(2)}, u32[]{:S(2)}) collective-permute-start(bf16[512,512]{1,0:T(8,128)(2,1)S(1)} %constant_dynamic-slice_fusion.own_frames), channel_id=1, source_target_pairs={{0,8},{4,12},{8,0},{12,4},{1,9},{5,13},{9,1},{13,5},{2,10},{6,14},... | collective-permute-start | bytes 1572872 | tf_op jit(solution)/shard_map/ppermute | solution.py:410
  38.8 16.9 %collective-permute-start.10 = (bf16[640,512]{1,0:T(8,128)(2,1)}, bf16[640,512]{1,0:T(8,128)(2,1)}, u32[]{:S(2)}, u32[]{:S(2)}) collective-permute-start(bf16[640,512]{1,0:T(8,128)(2,1)} %collective-permute-done.8.far_a), channel_id=1, source_target_pairs={{0,16},{16,0},{1,17},{17,1},{2,18},{18,2},{3,19},{19,3},{4,20},{20... | collective-permute-start | bytes 1966088 | tf_op jit(solution)/shard_map/ppermute | solution.py:418
  40.8 4.6 %collective-permute-start.3 = (s32[4,4,32]{2,1,0:T(4,128)S(1)}, s32[4,4,32]{2,1,0:T(4,128)S(1)}, u32[]{:S(2)}, u32[]{:S(2)}) collective-permute-start(s32[4,4,32]{2,1,0:T(4,128)S(1)} %bitcast.42), channel_id=1, source_target_pairs={{0,8},{4,12},{8,0},{12,4},{1,9},{5,13},{9,1},{13,5},{2,10},{6,14},... | collective-permute-start | bytes 6152 | tf_op jit(solution)/shard_map/ppermute | solution.py:449
  45.4 3.7 %collective-permute-start.2 = (s32[4,4,32]{2,1,0:T(4,128)S(1)}, s32[4,4,32]{2,1,0:T(4,128)S(1)}, u32[]{:S(2)}, u32[]{:S(2)}) collective-permute-start(s32[4,4,32]{2,1,0:T(4,128)S(1)} %bitcast.41), channel_id=1, source_target_pairs={{0,4},{4,0},{8,12},{12,8},{1,5},{5,1},{9,13},{13,9},{2,6},{6,2},{1... | collective-permute-start | bytes 6152 | tf_op jit(solution)/shard_map/ppermute | solution.py:449
  49.1 5.6 %collective-permute-start.4 = (s32[4,4,32]{2,1,0:T(4,128)S(1)}, s32[4,4,32]{2,1,0:T(4,128)S(1)}, u32[]{:S(2)}, u32[]{:S(2)}) collective-permute-start(s32[4,4,32]{2,1,0:T(4,128)S(1)} %bitcast.40), channel_id=1, source_target_pairs={{0,12},{4,8},{8,4},{12,0},{1,13},{5,9},{9,5},{13,1},{2,14},{6,10},... | collective-permute-start | bytes 6152 | tf_op jit(solution)/shard_map/ppermute | solution.py:449
  54.7 10.3 %collective-permute-start.6 = (bf16[512,512]{1,0:T(8,128)(2,1)S(1)}, bf16[512,512]{1,0:T(8,128)(2,1)S(1)}, u32[]{:S(2)}, u32[]{:S(2)}) collective-permute-start(bf16[512,512]{1,0:T(8,128)(2,1)S(1)} %constant_dynamic-slice_fusion.own_frames), channel_id=1, source_target_pairs={{0,4},{4,0},{8,12},{12,8},{1,5},{5,1},{9,13},{13,9},{2,6},{6,2},{1... | collective-permute-start | bytes 1572872 | tf_op jit(solution)/shard_map/ppermute | solution.py:411
  54.7 27.5 %collective-permute-start.12 = (bf16[768,512]{1,0:T(8,128)(2,1)}, bf16[768,512]{1,0:T(8,128)(2,1)}, u32[]{:S(2)}, u32[]{:S(2)}) collective-permute-start(bf16[768,512]{1,0:T(8,128)(2,1)} %collective-permute-done.9.far_b), channel_id=1, source_target_pairs={{0,1},{1,0},{2,3},{3,2},{4,5},{5,4},{6,7},{7,6},{8,9},{9,8},{10,11... | collective-permute-start | bytes 2359304 | tf_op jit(solution)/shard_map/ppermute | solution.py:421
  54.7 14.3 %copy-start.2 = (bf16[512,512]{1,0:T(8,128)(2,1)}, bf16[512,512]{1,0:T(8,128)(2,1)S(1)}, u32[]{:S(2)}) copy-start(bf16[512,512]{1,0:T(8,128)(2,1)S(1)} %collective-permute-done.7.frames_2) | copy-start | bytes 1572868
  54.7 27.4 %collective-permute-start.11 = (bf16[640,512]{1,0:T(8,128)(2,1)}, bf16[640,512]{1,0:T(8,128)(2,1)}, u32[]{:S(2)}, u32[]{:S(2)}) collective-permute-start(bf16[640,512]{1,0:T(8,128)(2,1)} %collective-permute-done.8.far_a), channel_id=1, source_target_pairs={{0,1},{1,0},{2,3},{3,2},{4,5},{5,4},{6,7},{7,6},{8,9},{9,8},{10,11... | collective-permute-start | bytes 1966088 | tf_op jit(solution)/shard_map/ppermute | solution.py:420
  55.7 26.5 %collective-permute-start.13 = (bf16[640,512]{1,0:T(8,128)(2,1)}, bf16[640,512]{1,0:T(8,128)(2,1)}, u32[]{:S(2)}, u32[]{:S(2)}) collective-permute-start(bf16[640,512]{1,0:T(8,128)(2,1)} %collective-permute-done.10.far_c), channel_id=1, source_target_pairs={{0,1},{1,0},{2,3},{3,2},{4,5},{5,4},{6,7},{7,6},{8,9},{9,8},{10,11... | collective-permute-start | bytes 1966088 | tf_op jit(solution)/shard_map/ppermute | solution.py:422
  64.9 1.5 %copy-start.3 = (bf16[512,512]{1,0:T(8,128)(2,1)}, bf16[512,512]{1,0:T(8,128)(2,1)S(1)}, u32[]{:S(2)}) copy-start(bf16[512,512]{1,0:T(8,128)(2,1)S(1)} %collective-permute-done.6.frames_1) | copy-start | bytes 1572868
  64.9 17.2 %collective-permute-start.14 = (bf16[512,512]{1,0:T(8,128)(2,1)S(1)}, bf16[512,512]{1,0:T(8,128)(2,1)}, u32[]{:S(2)}, u32[]{:S(2)}) collective-permute-start(bf16[512,512]{1,0:T(8,128)(2,1)S(1)} %constant_dynamic-slice_fusion.own_frames), channel_id=1, source_target_pairs={{4,8},{8,4},{5,9},{9,5},{6,10},{10,6},{7,11},{11,7},{20,24},{24,20... | collective-permute-start | bytes 1572872 | tf_op jit(solution)/shard_map/ppermute | solution.py:412
  66.4 15.7 %collective-permute-start.15 = (bf16[512,512]{1,0:T(8,128)(2,1)S(1)}, bf16[512,512]{1,0:T(8,128)(2,1)}, u32[]{:S(2)}, u32[]{:S(2)}) collective-permute-start(bf16[512,512]{1,0:T(8,128)(2,1)S(1)} %collective-permute-done.7.frames_2), channel_id=1, source_target_pairs={{8,12},{4,0},{9,13},{5,1},{10,14},{6,2},{11,15},{7,3},{24,28},{20,... | collective-permute-start | bytes 1572872 | tf_op jit(solution)/shard_map/ppermute | solution.py:413
  95.3 5.8 %collective-permute-start.18 = (f32[2,16,128]{2,1,0:T(8,128)}, f32[2,16,128]{2,1,0:T(8,128)S(1)}, u32[]{:S(2)}, u32[]{:S(2)}) collective-permute-start(f32[2,16,128]{2,1,0:T(8,128)} %far_search.1), channel_id=1, source_target_pairs={{0,12},{4,8},{8,4},{12,0},{1,13},{5,9},{9,5},{13,1},{2,14},{6,10},... | collective-permute-start | bytes 49160 | tf_op jit(solution)/shard_map/ppermute | solution.py:486
  98.0 4.8 %collective-permute-start.17 = (f32[2,16,128]{2,1,0:T(8,128)}, f32[2,16,128]{2,1,0:T(8,128)S(1)}, u32[]{:S(2)}, u32[]{:S(2)}) collective-permute-start(f32[2,16,128]{2,1,0:T(8,128)} %far_search.1), channel_id=1, source_target_pairs={{0,8},{4,12},{8,0},{12,4},{1,9},{5,13},{9,1},{13,5},{2,10},{6,14},... | collective-permute-start | bytes 49160 | tf_op jit(solution)/shard_map/ppermute | solution.py:486
  100.4 3.9 %collective-permute-start.16 = (f32[2,16,128]{2,1,0:T(8,128)}, f32[2,16,128]{2,1,0:T(8,128)S(1)}, u32[]{:S(2)}, u32[]{:S(2)}) collective-permute-start(f32[2,16,128]{2,1,0:T(8,128)} %far_search.1), channel_id=1, source_target_pairs={{0,4},{4,0},{8,12},{12,8},{1,5},{5,1},{9,13},{13,9},{2,6},{6,2},{1... | collective-permute-start | bytes 49160 | tf_op jit(solution)/shard_map/ppermute | solution.py:486
  105.1 3.9 %copy-start.4 = (f32[2,16,128]{2,1,0:T(8,128)}, f32[2,16,128]{2,1,0:T(8,128)S(1)}, u32[]{:S(2)}) copy-start(f32[2,16,128]{2,1,0:T(8,128)S(1)} %pad_maximum_fusion.3.part_0) | copy-start | bytes 49156
  105.1 3.2 %collective-permute-start.21 = (f32[2,16,128]{2,1,0:T(8,128)S(1)}, f32[2,16,128]{2,1,0:T(8,128)S(1)}, u32[]{:S(2)}, u32[]{:S(2)}) collective-permute-start(f32[2,16,128]{2,1,0:T(8,128)S(1)} %pad_maximum_fusion.3.part_0), channel_id=1, source_target_pairs={{0,3},{1,2},{2,1},{3,0},{4,7},{5,6},{6,5},{7,4},{8,11},{9,10},{10,... | collective-permute-start | bytes 49160 | tf_op jit(solution)/shard_map/ppermute | solution.py:489
  105.2 3.8 %collective-permute-start.20 = (f32[2,16,128]{2,1,0:T(8,128)S(1)}, f32[2,16,128]{2,1,0:T(8,128)S(1)}, u32[]{:S(2)}, u32[]{:S(2)}) collective-permute-start(f32[2,16,128]{2,1,0:T(8,128)S(1)} %pad_maximum_fusion.3.part_0), channel_id=1, source_target_pairs={{0,2},{1,3},{2,0},{3,1},{4,6},{5,7},{6,4},{7,5},{8,10},{9,11},{10,... | collective-permute-start | bytes 49160 | tf_op jit(solution)/shard_map/ppermute | solution.py:489
  105.8 3.1 %collective-permute-start.19 = (f32[2,16,128]{2,1,0:T(8,128)S(1)}, f32[2,16,128]{2,1,0:T(8,128)S(1)}, u32[]{:S(2)}, u32[]{:S(2)}) collective-permute-start(f32[2,16,128]{2,1,0:T(8,128)S(1)} %pad_maximum_fusion.3.part_0), channel_id=1, source_target_pairs={{0,1},{1,0},{2,3},{3,2},{4,5},{5,4},{6,7},{7,6},{8,9},{9,8},{10,11... | collective-permute-start | bytes 49160 | tf_op jit(solution)/shard_map/ppermute | solution.py:489
  108.3 0.7 copy-start.5
  109.0 0.6 copy-start.6
  109.6 0.6 copy-start.7
where the time goes:
time: 113 us; the launch traced here: 112 us
  waiting for transfers between devices  39.9 us (35%)
  Pallas kernels  34.8 us (31%)
  starting transfers between devices  26.7 us (24%)
  local copies, waits for them, and re-layouts  6.08 us (5%)
  other arithmetic  3.37 us (3%)
    ppermute x1, waiting for transfers between devices, gathered_frames(): far_pair = lax.ppermute(pair, 'medoids', exchanged(groups, 2))  18.5 us
    pallas_call x1, Pallas kernels, gathered_frames(): pl.pallas_call(near_kernel, out_shape=jax.ShapeDtypeStruct((3, total_tile...  13.1 us
    pallas_call x1, Pallas kernels, gathered_frames(): pl.pallas_call(far_kernel, out_shape=jax.ShapeDtypeStruct((2, total_tiles...  13.1 us
    ppermute x1, waiting for transfers between devices, gathered_frames(): frames_1 = lax.ppermute(mine, 'frames', exchanged(members, 1))  9.21 us
    ppermute x3, starting transfers between devices, gathered_frames(): lax.ppermute(lists[:, :, at], 'frames', exchanged(members, at))  7.75 us
    pallas_call x1, Pallas kernels, gathered_frames(): pl.pallas_call(functools.partial(prepare_kernel, members), out_shape=(jax...  6.99 us
    ppermute x3, waiting for transfers between devices, gathered_frames(): lax.ppermute(lists[:, :, at], 'frames', exchanged(members, at))  6.07 us
    ppermute x3, starting transfers between devices, gathered_frames(): other = lax.ppermute(found, 'frames', exchanged(members, at))  5.38 us
  transfers between devices with their start and end apart: 22, of which 11 were waited for; matrix products, arithmetic and copies ran while one was open for 7% of the time, Pallas kernels for 18%

commit v1 on v0

--- a/solution.py
+++ b/solution.py
@@ -14,6 +14,9 @@
 big_value = 1e30
 per_block = 8
 unroll = 4
+together = 2
+small_vmem = 8 << 20
+large_vmem = 24 << 20
 
 
 def fold_two(left_one, left_two, right_one, right_two):
@@ -139,81 +142,125 @@
     return one[0:1], two[0:1]
 
 
-def prepare_kernel(members, where_ref, ids_ref, counts_ref, group_ref, lists_ref, norms_ref):
-    tiles_here = group_ref.shape[0] // TILE
+def split_kernel(members, where_ref, ids_ref, counts_ref, lists_ref):
+    tiles_here = where_ref[3]
     lanes = lists_ref.shape[1] // members
     member = where_ref[0]
 
     def split(tile, _):
-        def take(at, numbers):
+        for shard in range(members):
+            lists_ref[tile, shard * lanes + lanes - 1] = 0
+
+        def take(at, _):
             entry = ids_ref[tile, at]
-            owner = entry // tiles_here
-            distance = jnp.bitwise_xor(owner, member)
-            place = jnp.int32(0)
-            for shard in range(members):
-                place = jnp.where(distance == shard, numbers[shard], place)
-            lists_ref[tile, distance * lanes + place] = entry - owner * tiles_here
-            return tuple(
-                numbers[shard] + (distance == shard).astype(jnp.int32) for shard in range(members)
+            owner = jnp.int32(0)
+            for shard in range(1, members):
+                owner = owner + (entry >= shard * tiles_here).astype(jnp.int32)
+            start = jnp.bitwise_xor(owner, member) * lanes
+            place = lists_ref[tile, start + lanes - 1]
+            lists_ref[tile, start + place] = entry - owner * tiles_here
+            lists_ref[tile, start + lanes - 1] = place + 1
+            return 0
+
+        return lax.fori_loop(0, counts_ref[0, tile], take, 0)
+
+    lax.fori_loop(0, ids_ref.shape[0], split, 0)
+
+
+def norms_kernel(scale, *refs):
+    norms_ref = refs[-1]
+    row = 0
+    for ref in refs[:-1]:
+        for tile in range(ref.shape[0] // TILE):
+            rows = ref[tile * TILE : (tile + 1) * TILE, :].astype(jnp.float32)
+            norms_ref[row : row + 1, :] = scale * column_of(rows * rows)
+            row += 1
+
+
+def search(
+    tiles, slots, first_tile, quarter_tiles, tiles_here, lists_ref, rows_ref, norms_ref,
+    frames_ref, one_ref, two_ref, table_ref,
+):
+    last_lane = lists_ref.shape[3] - 1
+    dummy = len(slots) * tiles_here
+    shift = 16
+
+    def place_of(index):
+        zslot = index // quarter_tiles
+        return zslot, index - zslot * quarter_tiles
+
+    def ends_of(index):
+        zslot, tile = place_of(index)
+        ends, number = [], jnp.int32(0)
+        for slot in slots:
+            number = number + lists_ref[zslot, slot, tile, last_lane]
+            ends.append(number)
+        return ends
+
+    def blocks_of(at, written):
+        blocks = (ends_of(first_tile + at)[-1] + unroll - 1) // unroll
+
+        def put(block, _):
+            table_ref[written + block] = (block << shift) + at
+            return 0
+
+        lax.fori_loop(0, blocks, put, 0)
+        return written + blocks
+
+    written = lax.fori_loop(0, tiles, blocks_of, jnp.int32(0))
+    for extra in range(together - 1):
+        table_ref[written + extra] = jnp.int32(1 << (shift + 8))
+    size = tiles * TILE
+    one_ref[0:size, :] = jnp.full((size, TILE), big_value, jnp.float32)
+    two_ref[0:size, :] = jnp.full((size, TILE), big_value, jnp.float32)
+
+    def step(at_step, _):
+        results = []
+        for member in range(together):
+            code = table_ref[at_step * together + member]
+            at = jnp.bitwise_and(code, (1 << shift) - 1)
+            block = code >> shift
+            index = first_tile + at
+            zslot, tile = place_of(index)
+            ends = ends_of(index)
+            picked, picked_norm = [], []
+            for lane in range(unroll):
+                place = block * unroll + lane
+                live = place < ends[-1]
+                slot, start = jnp.int32(0), jnp.int32(0)
+                for number in range(1, len(slots)):
+                    beyond = place >= ends[number - 1]
+                    slot = jnp.where(beyond, number, slot)
+                    start = jnp.where(beyond, ends[number - 1], start)
+                place = jnp.where(live, place - start, 0)
+                entry = lists_ref[zslot, slots[0] + slot, tile, place] + slot * tiles_here
+                row = jnp.where(live, entry, 0) * TILE
+                picked.append(rows_ref[pl.ds(pl.multiple_of(row, TILE), TILE), :])
+                picked_norm.append(norms_ref[pl.ds(jnp.where(live, entry, dummy), 1), :])
+            inner = lax.dot_general(
+                frames_ref[pl.ds(pl.multiple_of(index * TILE, TILE), TILE), :],
+                jnp.concatenate(picked, axis=0),
+                (((1,), (1,)), ((), ())),
+                preferred_element_type=jnp.float32,
             )
-
-        numbers = lax.fori_loop(0, counts_ref[0, tile], take, (jnp.int32(0),) * members)
-        for shard in range(members):
-            lists_ref[tile, shard * lanes + lanes - 1] = numbers[shard]
+            results.append((at, picked_norm, inner))
+        for at, picked_norm, inner in results:
+            rows = pl.ds(pl.multiple_of(at * TILE, TILE), TILE)
+            one, two = one_ref[rows, :], two_ref[rows, :]
+            for lane in range(unroll):
+                part = picked_norm[lane] - inner[:, lane * TILE : (lane + 1) * TILE]
+                two = jnp.minimum(two, jnp.maximum(one, part))
+                one = jnp.minimum(one, part)
+            one_ref[rows, :] = one
+            two_ref[rows, :] = two
         return 0
 
-    lax.fori_loop(0, ids_ref.shape[0], split, 0)
-
-    for tile in range(tiles_here):
-        rows = group_ref[tile * TILE : (tile + 1) * TILE, :].astype(jnp.float32)
-        norms_ref[tile : tile + 1, :] = 0.5 * column_of(rows * rows)
-
-
-def search_tile(frame_tile, slots, zslot, tile, lists_ref, rows_ref, norms_ref, dummy, base):
-    last_lane = lists_ref.shape[3] - 1
-    tiles_here = base
-    ends = []
-    number = jnp.int32(0)
-    for slot in slots:
-        number = number + lists_ref[zslot, slot, tile, last_lane]
-        ends.append(number)
-
-    def block(at, carry):
-        one, two = carry
-        picked, picked_norm = [], []
-        for step in range(unroll):
-            place = at * unroll + step
-            live = place < number
-            slot = jnp.int32(slots[0])
-            start = jnp.int32(0)
-            for index in range(1, len(slots)):
-                beyond = place >= ends[index - 1]
-                slot = jnp.where(beyond, slots[index], slot)
-                start = jnp.where(beyond, ends[index - 1], start)
-            place = jnp.where(live, place - start, 0)
-            entry = lists_ref[zslot, slot, tile, place] + (slot - slots[0]) * tiles_here
-            entry = jnp.where(live, entry, 0)
-            picked.append(rows_ref[pl.ds(pl.multiple_of(entry * TILE, TILE), TILE), :])
-            picked_norm.append(norms_ref[pl.ds(jnp.where(live, entry, dummy), 1), :])
-        inner = lax.dot_general(
-            frame_tile,
-            jnp.concatenate(picked, axis=0),
-            (((1,), (1,)), ((), ())),
-            preferred_element_type=jnp.float32,
-        )
-        for step in range(unroll):
-            part = picked_norm[step] - inner[:, step * TILE : (step + 1) * TILE]
-            two = jnp.minimum(two, jnp.maximum(one, part))
-            one = jnp.minimum(one, part)
-        return one, two
-
-    empty = jnp.full((TILE, TILE), big_value, jnp.float32)
-    return lax.fori_loop(0, (number + unroll - 1) // unroll, block, (empty, empty))
+    lax.fori_loop(0, (written + together - 1) // together, step, 0)
 
 
 def near_kernel(
     lists_ref, norms_in, own_group, near_group, own_frames, frames_1, frames_2,
-    out_ref, rows_buf, frames_buf, norms_buf, sems,
+    out_ref, rows_buf, frames_buf, norms_buf, one_buf, two_buf, table_ref, sems,
 ):
     tile_rows = own_group.shape[0]
     tiles_here = tile_rows // TILE
@@ -231,35 +278,26 @@
         )
     for copy in copies:
         copy.start()
-    dummy = 2 * tiles_here
     norms_buf[pl.ds(0, tiles_here), :] = norms_in[0]
     norms_buf[pl.ds(tiles_here, tiles_here), :] = norms_in[1]
-    norms_buf[pl.ds(dummy, 1), :] = jnp.full((1, TILE), big_value, jnp.float32)
-    out_ref[...] = jnp.full(out_ref.shape, big_value, jnp.float32)
+    norms_buf[pl.ds(2 * tiles_here, 1), :] = jnp.full((1, TILE), big_value, jnp.float32)
     for copy in copies:
         copy.wait()
-
-    def one_tile(index, _):
-        zslot = index // quarter_tiles
-        tile = index - zslot * quarter_tiles
-        frame_tile = frames_buf[pl.ds(pl.multiple_of(index * TILE, TILE), TILE), :]
-        one, two = search_tile(
-            frame_tile, (0, 1), zslot, tile, lists_ref, rows_buf, norms_buf, dummy, tiles_here
-        )
-        one, two = row_pair(one, two)
-        squares = frame_tile.astype(jnp.float32)
-        out_ref[0, pl.ds(index, 1), :] = one
-        out_ref[1, pl.ds(index, 1), :] = two
-        out_ref[2, pl.ds(index, 1), :] = column_of(squares * squares)
-        return 0
-
-    lax.fori_loop(0, 3 * quarter_tiles, one_tile, 0)
+    tiles = 3 * quarter_tiles
+    search(
+        tiles, (0, 1), 0, quarter_tiles, tiles_here, lists_ref, rows_buf, norms_buf,
+        frames_buf, one_buf, two_buf, table_ref,
+    )
+    for index in range(tiles):
+        one, two = row_pair(one_buf[pl.ds(index * TILE, TILE), :], two_buf[pl.ds(index * TILE, TILE), :])
+        out_ref[0, index : index + 1, :] = one
+        out_ref[1, index : index + 1, :] = two
 
 
 def far_kernel(
-    where_ref, lists_ref, norms_in, before_ref, own_group, near_group, far_a, far_b, far_c,
-    last_a, last_b, last_c, own_frames, frames_1, frames_2, frames_3a, frames_3b,
-    out_ref, rows_buf, frames_buf, norms_buf, found_buf, sems,
+    where_ref, lists_ref, norms_in, before_ref, frame_norms, own_group, near_group,
+    far_a, far_b, far_c, last_a, last_b, last_c, own_frames, frames_1, frames_2, frames_3a, frames_3b,
+    out_ref, rows_buf, frames_buf, norms_buf, one_buf, two_buf, table_ref, sems,
 ):
     tile_rows = own_group.shape[0]
     tiles_here = tile_rows // TILE
@@ -318,55 +356,41 @@
     for slot in range(groups):
         norms_buf[pl.ds(slot * tiles_here, tiles_here), :] = norms_in[slot]
     norms_buf[pl.ds(dummy, 1), :] = jnp.full((1, TILE), big_value, jnp.float32)
-    found_buf[...] = before_ref[...]
     for copy in copies[:early]:
         copy.wait()
 
-    far_rows = rows_buf.at[pl.ds(2 * tile_rows, 2 * tile_rows)]
-    far_norms = norms_buf.at[pl.ds(2 * tiles_here, 2 * tiles_here + 8)]
-
-    def one_tile(index, _):
-        zslot = index // quarter_tiles
-        tile = index - zslot * quarter_tiles
-        frame_tile = frames_buf[pl.ds(pl.multiple_of(index * TILE, TILE), TILE), :]
-        one, two = search_tile(
-            frame_tile, (2, 3), zslot, tile, lists_ref, far_rows, far_norms, 2 * tiles_here, tiles_here
+    def finish(index, at, before_one, before_two, frame_norm):
+        rows = pl.ds(at * TILE, TILE)
+        one, two = row_pair(one_buf[rows, :], two_buf[rows, :])
+        if before_one is not None:
+            one, two = fold_two(one, two, before_one, before_two)
+        block_of = jnp.bitwise_xor(member, index // quarter_tiles)
+        row = block_of * quarter_tiles + index % quarter_tiles
+        out_ref[0, pl.ds(row, 1), :] = (frame_norm + 2.0 * one) / width
+        out_ref[1, pl.ds(row, 1), :] = (frame_norm + 2.0 * two) / width
+
+    early_tiles = 3 * quarter_tiles
+    search(
+        early_tiles, (2, 3), 0, quarter_tiles, tiles_here, lists_ref,
+        rows_buf.at[pl.ds(2 * tile_rows, 2 * tile_rows)],
+        norms_buf.at[pl.ds(2 * tiles_here, 2 * tiles_here + 8)],
+        frames_buf, one_buf, two_buf, table_ref,
+    )
+    for index in range(early_tiles):
+        finish(
+            index, index, before_ref[0, index : index + 1, :], before_ref[1, index : index + 1, :],
+            frame_norms[index : index + 1, :],
         )
-        one, two = row_pair(one, two)
-        one, two = fold_two(
-            one, two, found_buf[0, pl.ds(index, 1), :], found_buf[1, pl.ds(index, 1), :]
-        )
-        found_buf[0, pl.ds(index, 1), :] = one
-        found_buf[1, pl.ds(index, 1), :] = two
-        return 0
-
-    lax.fori_loop(0, 3 * quarter_tiles, one_tile, 0)
     pltpu.make_async_copy(frames_3a, last_target, last_sem).wait()
     for copy in copies[early:]:
         copy.wait()
-
-    def last_tile(tile, _):
-        index = 3 * quarter_tiles + tile
-        frame_tile = frames_buf[pl.ds(pl.multiple_of(index * TILE, TILE), TILE), :]
-        one, two = search_tile(
-            frame_tile, tuple(range(groups)), 3, tile, lists_ref, rows_buf, norms_buf, dummy, tiles_here
-        )
-        one, two = row_pair(one, two)
-        squares = frame_tile.astype(jnp.float32)
-        found_buf[0, pl.ds(index, 1), :] = one
-        found_buf[1, pl.ds(index, 1), :] = two
-        found_buf[2, pl.ds(index, 1), :] = column_of(squares * squares)
-        return 0
-
-    lax.fori_loop(0, quarter_tiles, last_tile, 0)
-    norm = found_buf[2]
-    found_buf[0] = (norm + 2.0 * found_buf[0]) / width
-    found_buf[1] = (norm + 2.0 * found_buf[1]) / width
-    for index in range(members * quarter_tiles):
-        block_of = jnp.bitwise_xor(member, index // quarter_tiles)
-        row = block_of * quarter_tiles + index % quarter_tiles
-        out_ref[0, pl.ds(row, 1), :] = found_buf[0, index : index + 1, :]
-        out_ref[1, pl.ds(row, 1), :] = found_buf[1, index : index + 1, :]
+    search(
+        quarter_tiles, tuple(range(groups)), early_tiles, quarter_tiles, tiles_here, lists_ref,
+        rows_buf, norms_buf, frames_buf, one_buf, two_buf, table_ref,
+    )
+    for tile in range(quarter_tiles):
+        rows = frames_buf[pl.ds((early_tiles + tile) * TILE, TILE), :].astype(jnp.float32)
+        finish(early_tiles + tile, tile, None, None, column_of(rows * rows))
 
 
 def pick_kernel(where_ref, plan_ref, part_0, part_1, part_2, part_3, first_ref, second_ref, every):
@@ -421,64 +445,88 @@
     last_b = lax.ppermute(far_b, "medoids", exchanged(groups, 1))
     last_c = lax.ppermute(far_c, "medoids", exchanged(groups, 1))
 
-    where = jnp.stack([member, piece, slab]).astype(jnp.int32)
+    tiles_here = tile_rows // TILE
+    where = jnp.stack([member, piece, slab, jnp.int32(tiles_here)]).astype(jnp.int32)
     hbm = pl.BlockSpec(memory_space=pl.ANY)
     scalar = pl.BlockSpec(memory_space=pltpu.SMEM)
     vector = pl.BlockSpec(memory_space=pltpu.VMEM)
-    tiles_here = tile_rows // TILE
     lanes = TILE // members
-    listed, norms = pl.pallas_call(
-        functools.partial(prepare_kernel, members),
-        out_shape=(
-            jax.ShapeDtypeStruct((blocks, members * lanes), jnp.int32),
-            jax.ShapeDtypeStruct((tiles_here, TILE), jnp.float32),
-        ),
-        in_specs=[scalar, scalar, scalar, vector],
-        out_specs=(scalar, vector),
-        name="prepare",
-    )(where, tile_ids[0], tile_counts, rows)
-    packed = jnp.concatenate([listed.astype(jnp.float32), norms], axis=0)
-    pair = jnp.stack([packed, lax.ppermute(packed, "medoids", exchanged(groups, 1))])
+    listed = pl.pallas_call(
+        functools.partial(split_kernel, members),
+        out_shape=jax.ShapeDtypeStruct((blocks, members * lanes), jnp.int32),
+        in_specs=[scalar] * 3,
+        out_specs=scalar,
+        compiler_params=pltpu.CompilerParams(vmem_limit_bytes=small_vmem),
+        name="split",
+    )(where, tile_ids[0], tile_counts)
+    pair = jnp.stack([listed, lax.ppermute(listed, "medoids", exchanged(groups, 1))])
     far_pair = lax.ppermute(pair, "medoids", exchanged(groups, 2))
-    packed = jnp.concatenate([pair, far_pair], axis=0)
-    norms = packed[:, blocks:]
-    lists = lax.dynamic_slice_in_dim(packed, piece * quarter_tiles, quarter_tiles, axis=1)
-    lists = lists.astype(jnp.int32).reshape(groups, quarter_tiles, members, lanes)
+    lists = jnp.concatenate([pair, far_pair], axis=0)
+    lists = lax.dynamic_slice_in_dim(lists, piece * quarter_tiles, quarter_tiles, axis=1)
+    lists = lists.reshape(groups, quarter_tiles, members, lanes)
     lists = jnp.stack(
         [lists[:, :, 0]]
         + [lax.ppermute(lists[:, :, at], "frames", exchanged(members, at)) for at in (1, 2, 3)]
     )
+    norms = pl.pallas_call(
+        functools.partial(norms_kernel, 0.5),
+        out_shape=jax.ShapeDtypeStruct((tiles_here, TILE), jnp.float32),
+        in_specs=[vector],
+        out_specs=vector,
+        compiler_params=pltpu.CompilerParams(vmem_limit_bytes=small_vmem),
+        name="medoid_norms",
+    )(rows)
+    norm_pair = jnp.stack([norms, lax.ppermute(norms, "medoids", exchanged(groups, 1))])
+    norm_far = lax.ppermute(norm_pair, "medoids", exchanged(groups, 2))
+    norms = jnp.concatenate([norm_pair, norm_far], axis=0)
+    frame_norms = pl.pallas_call(
+        functools.partial(norms_kernel, 1.0),
+        out_shape=jax.ShapeDtypeStruct((3 * quarter_tiles, TILE), jnp.float32),
+        in_specs=[vector] * 3,
+        out_specs=vector,
+        compiler_params=pltpu.CompilerParams(vmem_limit_bytes=small_vmem),
+        name="frame_norms",
+    )(mine, frames_1, frames_2)
 
     total_tiles = members * quarter_tiles
+    early_tiles = 3 * quarter_tiles
+    table_size = early_tiles * (groups * tile_ids.shape[2] // unroll + 1) + together
     before = pl.pallas_call(
         near_kernel,
-        out_shape=jax.ShapeDtypeStruct((3, total_tiles, TILE), jnp.float32),
+        out_shape=jax.ShapeDtypeStruct((2, early_tiles, TILE), jnp.float32),
         in_specs=[scalar, vector] + [hbm] * 5,
         out_specs=vector,
         scratch_shapes=[
             pltpu.VMEM((2 * tile_rows, width), jnp.bfloat16),
             pltpu.VMEM((3 * quarter, width), jnp.bfloat16),
             pltpu.VMEM((2 * tiles_here + 8, TILE), jnp.float32),
+            pltpu.VMEM((3 * quarter, TILE), jnp.float32),
+            pltpu.VMEM((3 * quarter, TILE), jnp.float32),
+            pltpu.SMEM((table_size,), jnp.int32),
             pltpu.SemaphoreType.DMA((5,)),
         ],
+        compiler_params=pltpu.CompilerParams(vmem_limit_bytes=large_vmem),
         name="near_search",
-    )(lists, norms, rows, near_group, mine, frames_1, frames_2)
+    )(lists, norm_pair, rows, near_group, mine, frames_1, frames_2)
     found = pl.pallas_call(
         far_kernel,
         out_shape=jax.ShapeDtypeStruct((2, total_tiles, TILE), jnp.float32),
-        in_specs=[scalar, scalar, vector, vector] + [hbm] * 13,
+        in_specs=[scalar, scalar, vector, vector, vector] + [hbm] * 13,
         out_specs=vector,
         scratch_shapes=[
             pltpu.VMEM((groups * tile_rows, width), jnp.bfloat16),
             pltpu.VMEM((members * quarter, width), jnp.bfloat16),
             pltpu.VMEM((groups * tiles_here + 8, TILE), jnp.float32),
-            pltpu.VMEM((3, total_tiles, TILE), jnp.float32),
+            pltpu.VMEM((3 * quarter, TILE), jnp.float32),
+            pltpu.VMEM((3 * quarter, TILE), jnp.float32),
+            pltpu.SMEM((table_size,), jnp.int32),
             pltpu.SemaphoreType.DMA((16,)),
         ],
+        compiler_params=pltpu.CompilerParams(vmem_limit_bytes=large_vmem),
         name="far_search",
     )(
-        where, lists, norms, before, rows, near_group, far_a, far_b, far_c, last_a, last_b, last_c,
-        mine, frames_1, frames_2, frames_3a, frames_3b,
+        where, lists, norms, before, frame_norms, rows, near_group,
+        far_a, far_b, far_c, last_a, last_b, last_c, mine, frames_1, frames_2, frames_3a, frames_3b,
     )
 
     one, two = found[0], found[1]
@@ -493,6 +541,7 @@
         in_specs=[scalar, scalar] + [vector] * 4,
         out_specs=(vector, vector),
         scratch_shapes=[pltpu.VMEM((2, groups * members * quarter_tiles, TILE), jnp.float32)],
+        compiler_params=pltpu.CompilerParams(vmem_limit_bytes=small_vmem),
         name="pick",
     )(where, plan, *parts)
     return (first.reshape(-1), second.reshape(-1))

time: 113 us -> 104 us (0.920); the launches traced: 112 us -> 104 us
  Pallas kernels: 34.8 us -> 24.4 us
  other arithmetic: 3.37 us -> 0.12 us
  waiting for transfers between devices: 39.9 us -> 42.4 us
  starting transfers between devices: 26.7 us -> 29 us
  local copies, waits for them, and re-layouts: 6.08 us -> 7.47 us
    pallas_call x2 -> x4, Pallas kernels: 20.1 us -> 14.7 us  [the longest x1 8.58 us: gathered_frames(): pl.pallas_call(near_kernel, out_shape=jax.ShapeDtypeStruct((2, early_tile...]
    pallas_call x1, Pallas kernels: 13.1 us -> 8.41 us  [gathered_frames(): pl.pallas_call(far_kernel, out_shape=jax.ShapeDtypeStruct((2, total_tiles...]
    ppermute x1, waiting for transfers between devices: 18.5 us -> 21.4 us  [gathered_frames(): far_pair = lax.ppermute(pair, 'medoids', exchanged(groups, 2))]
    unnamed x16 -> x12, local copies, waits for them, and re-layouts: 1.2 us -> 3.26 us
    ppermute x1 -> x3, starting transfers between devices: 0.53 us -> 2.24 us  [the longest x1 1.74 us: gathered_frames(): norm_far = lax.ppermute(norm_pair, 'medoids', exchanged(groups, 2))]
    another operation x3, other arithmetic: 1.3 us -> 0.08 us  [the longest x1 0.08 us: gathered_frames(): jnp.stack([member, piece, slab, jnp.int32(tiles_here)]).astype(jnp.int32)]
  transfers between devices with their start and end apart: 22 -> 24, of which waited for: 11 -> 11; matrix products, arithmetic and copies ran while one was open for 7% -> 4% of each run, Pallas kernels for 18% -> 14%
where the time goes in v1:
time: 104 us
  waiting for transfers between devices  42.4 us (41%)
  starting transfers between devices  29 us (28%)
  Pallas kernels  24.4 us (23%)
  local copies, waits for them, and re-layouts  7.47 us (7%)
    ppermute x1, waiting for transfers between devices, gathered_frames(): far_pair = lax.ppermute(pair, 'medoids', exchanged(groups, 2))  21.4 us
    ppermute x1, waiting for transfers between devices, gathered_frames(): frames_1 = lax.ppermute(mine, 'frames', exchanged(members, 1))  8.76 us
    pallas_call x1, Pallas kernels, gathered_frames(): pl.pallas_call(near_kernel, out_shape=jax.ShapeDtypeStruct((2, early_tile...  8.58 us
    ppermute x3, starting transfers between devices, gathered_frames(): lax.ppermute(lists[:, :, at], 'frames', exchanged(members, at))  8.52 us
    pallas_call x1, Pallas kernels, gathered_frames(): pl.pallas_call(far_kernel, out_shape=jax.ShapeDtypeStruct((2, total_tiles...  8.41 us
    ppermute x3, starting transfers between devices, gathered_frames(): other = lax.ppermute(found, 'frames', exchanged(members, at))  5.54 us
    ppermute x3, waiting for transfers between devices, gathered_frames(): lax.ppermute(lists[:, :, at], 'frames', exchanged(members, at))  5.26 us
    pallas_call x1, Pallas kernels, gathered_frames(): pl.pallas_call(functools.partial(split_kernel, members), out_shape=jax.Sh...  5.21 us
  transfers between devices with their start and end apart: 24, of which 11 were waited for; matrix products, arithmetic and copies ran while one was open for 4% of the time, Pallas kernels for 14%

profile of v1, /device:TPU:0, one launch (start us, length us, event | category | flops | bytes accessed | tf_op | source)
XLA Modules:
  0.0 104.2 jit_solution(11632427064009148663)
XLA Ops:
  0.6 0.0 copy-start
  0.7 0.6 collective-permute-start.7
  1.2 1.6 %copy-done.1 = bf16[1,2048,512]{2,1,0:T(8,128)(2,1)S(1)} copy-done((bf16[1,2048,512]{2,1,0:T(8,128)(2,1)S(1)}, bf16[1,2048,512]{2,1,0:T(8,128)(2,1)}, u32[]{:S(2)}) %copy-start.1) | copy-done | bytes 2097176
  2.9 0.5 medoid_norms.1
  3.4 0.2 collective-permute-start.5
  3.5 2.0 %dynamic-slice_bitcast_fusion = bf16[640,512]{1,0:T(8,128)(2,1)} fusion(bf16[1,2048,512]{2,1,0:T(8,128)(2,1)} %param.6, s32[]{:T(128)S(6)} %select_n.11), kind=kLoop, calls=%fused_computation.1 | loop fusion | bytes 1310724 | tf_op jit(solution)/shard_map/dynamic_slice | solution.py:439
  5.5 2.8 %collective-permute-start.10 = (bf16[640,512]{1,0:T(8,128)(2,1)}, bf16[640,512]{1,0:T(8,128)(2,1)}, u32[]{:S(2)}, u32[]{:S(2)}) collective-permute-start(bf16[640,512]{1,0:T(8,128)(2,1)} %dynamic-slice_bitcast_fusion), channel_id=1, source_target_pairs={{0,2},{1,3},{2,0},{3,1},{4,6},{5,7},{6,4},{7,5},{8,10},{9,11},{10,... | collective-permute-start | bytes 1966088 | tf_op jit(solution)/shard_map/ppermute | solution.py:440
  8.3 0.1 pad_add_fusion.2.where_ref
  8.4 0.0 copy-done.3
  8.4 5.2 %split.1 = s32[16,128]{1,0:T(8,128)S(1)} custom-call(s32[4]{0:T(128)S(1)} %pad_add_fusion.2.where_ref, s32[16,24]{1,0:T(8,128)S(1)} %bitcast.38, s32[1,16]{1,0:T(1,128)S(1)} %copy-done.5), custom_call_target="tpu_custom_call" | custom-call | tf_op jit(solution)/shard_map/split/pallas_call | solution.py:454
  13.6 0.3 collective-permute-start
  14.0 1.3 %collective-permute-start.9 = (bf16[512,512]{1,0:T(8,128)(2,1)S(1)}, bf16[512,512]{1,0:T(8,128)(2,1)S(1)}, u32[]{:S(2)}, u32[]{:S(2)}) collective-permute-start(bf16[512,512]{1,0:T(8,128)(2,1)S(1)} %constant_dynamic-slice_fusion.own_frames.refs_0_), channel_id=1, source_target_pairs={{0,8},{4,12},{8,0},{12,4},{1,9},{5,13},{9,1},{13,5},{2,10},{6,14},... | collective-permute-start | bytes 1572872 | tf_op jit(solution)/shard_map/ppermute | solution.py:434
  15.3 2.1 %slice_bitcast_fusion = bf16[768,512]{1,0:T(8,128)(2,1)} fusion(bf16[1,2048,512]{2,1,0:T(8,128)(2,1)} %param.6), kind=kLoop, calls=%fused_computation | loop fusion | bytes 1572864 | tf_op jit(solution)/shard_map/slice | solution.py:441
  17.4 0.0 collective-permute-done
  17.4 0.6 collective-permute-start.11
  18.0 0.0 collective-permute-done.5
  18.0 1.5 %collective-permute-start.1 = (s32[2,16,128]{2,1,0:T(8,128)S(1)}, s32[2,16,128]{2,1,0:T(8,128)S(1)}, u32[]{:S(2)}, u32[]{:S(2)}) collective-permute-start(s32[2,16,128]{2,1,0:T(8,128)S(1)} %pad_add_fusion.1), channel_id=1, source_target_pairs={{0,2},{1,3},{2,0},{3,1},{4,6},{5,7},{6,4},{7,5},{8,10},{9,11},{10,... | collective-permute-start | bytes 49160 | tf_op jit(solution)/shard_map/ppermute | solution.py:463
  19.4 21.4 %collective-permute-done.1 = s32[2,16,128]{2,1,0:T(8,128)S(1)} collective-permute-done((s32[2,16,128]{2,1,0:T(8,128)S(1)}, s32[2,16,128]{2,1,0:T(8,128)S(1)}, u32[]{:S(2)}, u32[]{:S(2)}) %collective-permute-start.1) | collective-permute-done | bytes 16416 | tf_op jit(solution)/shard_map/ppermute | solution.py:463
  40.8 1.7 %collective-permute-start.6 = (f32[2,16,128]{2,1,0:T(8,128)S(1)}, f32[2,16,128]{2,1,0:T(8,128)S(1)}, u32[]{:S(2)}, u32[]{:S(2)}) collective-permute-start(f32[2,16,128]{2,1,0:T(8,128)S(1)} %pad_maximum_fusion.1.norms_in), channel_id=1, source_target_pairs={{0,2},{1,3},{2,0},{3,1},{4,6},{5,7},{6,4},{7,5},{8,10},{9,11},{10,... | collective-permute-start | bytes 49160 | tf_op jit(solution)/shard_map/ppermute | solution.py:480
  42.5 0.0 collective-permute-done.10.far_a
  42.5 1.5 %collective-permute-start.12 = (bf16[640,512]{1,0:T(8,128)(2,1)}, bf16[640,512]{1,0:T(8,128)(2,1)}, u32[]{:S(2)}, u32[]{:S(2)}) collective-permute-start(bf16[640,512]{1,0:T(8,128)(2,1)} %collective-permute-done.10.far_a), channel_id=1, source_target_pairs={{0,16},{16,0},{1,17},{17,1},{2,18},{18,2},{3,19},{19,3},{4,20},{20... | collective-permute-start | bytes 1966088 | tf_op jit(solution)/shard_map/ppermute | solution.py:442
  44.1 0.1 reshape.15
  44.2 0.3 collective-permute-done.6
  44.5 2.8 %collective-permute-start.3 = (s32[4,4,32]{2,1,0:T(4,128)S(1)}, s32[4,4,32]{2,1,0:T(4,128)S(1)}, u32[]{:S(2)}, u32[]{:S(2)}) collective-permute-start(s32[4,4,32]{2,1,0:T(4,128)S(1)} %bitcast.49), channel_id=1, source_target_pairs={{0,8},{4,12},{8,0},{12,4},{1,9},{5,13},{9,1},{13,5},{2,10},{6,14},... | collective-permute-start | bytes 6152 | tf_op jit(solution)/shard_map/ppermute | solution.py:469
  47.4 1.7 %collective-permute-done.3 = s32[4,4,32]{2,1,0:T(4,128)S(1)} collective-permute-done((s32[4,4,32]{2,1,0:T(4,128)S(1)}, s32[4,4,32]{2,1,0:T(4,128)S(1)}, u32[]{:S(2)}, u32[]{:S(2)}) %collective-permute-start.3) | collective-permute-done | bytes 2080 | tf_op jit(solution)/shard_map/ppermute | solution.py:469
  49.1 1.8 %collective-permute-start.2 = (s32[4,4,32]{2,1,0:T(4,128)S(1)}, s32[4,4,32]{2,1,0:T(4,128)S(1)}, u32[]{:S(2)}, u32[]{:S(2)}) collective-permute-start(s32[4,4,32]{2,1,0:T(4,128)S(1)} %bitcast.48), channel_id=1, source_target_pairs={{0,4},{4,0},{8,12},{12,8},{1,5},{5,1},{9,13},{13,9},{2,6},{6,2},{1... | collective-permute-start | bytes 6152 | tf_op jit(solution)/shard_map/ppermute | solution.py:469
  50.9 1.8 %collective-permute-done.2 = s32[4,4,32]{2,1,0:T(4,128)S(1)} collective-permute-done((s32[4,4,32]{2,1,0:T(4,128)S(1)}, s32[4,4,32]{2,1,0:T(4,128)S(1)}, u32[]{:S(2)}, u32[]{:S(2)}) %collective-permute-start.2) | collective-permute-done | bytes 2080 | tf_op jit(solution)/shard_map/ppermute | solution.py:469
  52.7 3.9 %collective-permute-start.4 = (s32[4,4,32]{2,1,0:T(4,128)S(1)}, s32[4,4,32]{2,1,0:T(4,128)S(1)}, u32[]{:S(2)}, u32[]{:S(2)}) collective-permute-start(s32[4,4,32]{2,1,0:T(4,128)S(1)} %bitcast.47), channel_id=1, source_target_pairs={{0,12},{4,8},{8,4},{12,0},{1,13},{5,9},{9,5},{13,1},{2,14},{6,10},... | collective-permute-start | bytes 6152 | tf_op jit(solution)/shard_map/ppermute | solution.py:469
  56.6 1.7 %collective-permute-done.4 = s32[4,4,32]{2,1,0:T(4,128)S(1)} collective-permute-done((s32[4,4,32]{2,1,0:T(4,128)S(1)}, s32[4,4,32]{2,1,0:T(4,128)S(1)}, u32[]{:S(2)}, u32[]{:S(2)}) %collective-permute-start.4) | collective-permute-done | bytes 2080 | tf_op jit(solution)/shard_map/ppermute | solution.py:469
  58.3 0.0 collective-permute-start.8
  58.3 0.0 collective-permute-done.11.far_b
  58.3 0.0 collective-permute-start.14
  58.3 0.0 collective-permute-done.9.frames_2.refs_2_
  58.3 0.5 collective-permute-start.13
  58.8 0.0 collective-permute-done.12.far_c
  58.8 0.1 collective-permute-start.15
  58.9 8.8 %collective-permute-done.8.frames_1.refs_1_ = bf16[512,512]{1,0:T(8,128)(2,1)S(1)} collective-permute-done((bf16[512,512]{1,0:T(8,128)(2,1)S(1)}, bf16[512,512]{1,0:T(8,128)(2,1)S(1)}, u32[]{:S(2)}, u32[]{:S(2)}) %collective-permute-start.8) | collective-permute-done | bytes 524320 | tf_op jit(solution)/shard_map/ppermute | solution.py:435
  67.7 0.7 collective-permute-start.16
  68.4 0.0 collective-permute-done.7.near_group
  68.4 1.3 %collective-permute-start.17 = (bf16[512,512]{1,0:T(8,128)(2,1)S(1)}, bf16[512,512]{1,0:T(8,128)(2,1)S(1)}, u32[]{:S(2)}, u32[]{:S(2)}) collective-permute-start(bf16[512,512]{1,0:T(8,128)(2,1)S(1)} %collective-permute-done.9.frames_2.refs_2_), channel_id=1, source_target_pairs={{8,12},{4,0},{9,13},{5,1},{10,14},{6,2},{11,15},{7,3},{24,28},{20,... | collective-permute-start | bytes 1572872 | tf_op jit(solution)/shard_map/ppermute | solution.py:437
  69.7 0.4 frame_norms.1
  70.1 0.0 copy-start.2
  70.1 1.6 %copy-done.2 = bf16[1,2048,512]{2,1,0:T(8,128)(2,1)S(1)} copy-done((bf16[1,2048,512]{2,1,0:T(8,128)(2,1)S(1)}, bf16[1,2048,512]{2,1,0:T(8,128)(2,1)}, u32[]{:S(2)}) %copy-start.2) | copy-done | bytes 2097176
  71.7 8.6 %near_search.1.before_ref = f32[2,12,128]{2,1,0:T(8,128)S(1)} custom-call(s32[4,4,4,32]{3,2,1,0:T(4,128)S(1)} %pad_add_fusion.lists_ref, f32[2,16,128]{2,1,0:T(8,128)S(1)} %pad_maximum_fusion.1.norms_in, bf16[2048,512]{1,0:T(8,128)(2,1)S(1)} %bitcast.32, bf16[2048,512]{1,0:T(8,128)(2,1)} %collective-permute-done.7.near_group, ...), custom_call_target="tpu_custom_call" | custom-call | tf_op jit(solution)/shard_map/near_search/pallas_call | solution.py:494
  80.3 0.0 copy-start.4
  80.3 0.0 collective-permute-done.16.frames_3a
  80.3 0.7 collective-permute-done.17.frames_3b
  81.0 0.0 collective-permute-done.13.last_a
  81.0 0.0 collective-permute-done.14.last_b
  81.0 0.0 collective-permute-done.15.last_c
  81.0 8.4 %far_search.1 = f32[2,16,128]{2,1,0:T(8,128)S(1)} custom-call(s32[4]{0:T(128)S(1)} %pad_add_fusion.2.where_ref, s32[4,4,4,32]{3,2,1,0:T(4,128)S(1)} %pad_add_fusion.lists_ref, f32[4,16,128]{2,1,0:T(8,128)S(1)} %pad_maximum_fusion.norms_in, f32[2,12,128]{2,1,0:T(8,128)S(1)} %near_search.1.before_ref, f32[12,128]{1,0:T(8,128)S(1)} %frame_norms.1, ...), custom_call_target="tpu_custom_call" | custom-call | tf_op jit(solution)/shard_map/far_search/pallas_call | solution.py:511
  89.4 4.9 %collective-permute-start.20 = (f32[2,16,128]{2,1,0:T(8,128)S(1)}, f32[2,16,128]{2,1,0:T(8,128)S(1)}, u32[]{:S(2)}, u32[]{:S(2)}) collective-permute-start(f32[2,16,128]{2,1,0:T(8,128)S(1)} %far_search.1), channel_id=1, source_target_pairs={{0,12},{4,8},{8,4},{12,0},{1,13},{5,9},{9,5},{13,1},{2,14},{6,10},... | collective-permute-start | bytes 49160 | tf_op jit(solution)/shard_map/ppermute | solution.py:534
  94.3 0.2 collective-permute-start.19
  94.5 0.5 collective-permute-start.18
  94.9 1.1 %collective-permute-done.20 = f32[2,16,128]{2,1,0:T(8,128)S(1)} collective-permute-done((f32[2,16,128]{2,1,0:T(8,128)S(1)}, f32[2,16,128]{2,1,0:T(8,128)S(1)}, u32[]{:S(2)}, u32[]{:S(2)}) %collective-permute-start.20) | collective-permute-done | bytes 16416 | tf_op jit(solution)/shard_map/ppermute | solution.py:534
  96.0 2.9 %collective-permute-done.19 = f32[2,16,128]{2,1,0:T(8,128)S(1)} collective-permute-done((f32[2,16,128]{2,1,0:T(8,128)S(1)}, f32[2,16,128]{2,1,0:T(8,128)S(1)}, u32[]{:S(2)}, u32[]{:S(2)}) %collective-permute-start.19) | collective-permute-done | bytes 16416 | tf_op jit(solution)/shard_map/ppermute | solution.py:534
  98.9 0.0 collective-permute-done.18
  99.0 0.1 collective-permute-start.23
  99.0 0.6 collective-permute-start.22
  99.6 1.2 %collective-permute-start.21 = (f32[2,16,128]{2,1,0:T(8,128)S(1)}, f32[2,16,128]{2,1,0:T(8,128)S(1)}, u32[]{:S(2)}, u32[]{:S(2)}) collective-permute-start(f32[2,16,128]{2,1,0:T(8,128)S(1)} %pad_maximum_fusion.2.part_0), channel_id=1, source_target_pairs={{0,1},{1,0},{2,3},{3,2},{4,5},{5,4},{6,7},{7,6},{8,9},{9,8},{10,11... | collective-permute-start | bytes 49160 | tf_op jit(solution)/shard_map/ppermute | solution.py:537
  100.9 1.3 %collective-permute-done.23.part_3 = f32[2,16,128]{2,1,0:T(8,128)S(1)} collective-permute-done((f32[2,16,128]{2,1,0:T(8,128)S(1)}, f32[2,16,128]{2,1,0:T(8,128)S(1)}, u32[]{:S(2)}, u32[]{:S(2)}) %collective-permute-start.23) | collective-permute-done | bytes 16416 | tf_op jit(solution)/shard_map/ppermute | solution.py:537
  102.2 0.7 collective-permute-done.22.part_2
  102.8 0.0 collective-permute-done.21.part_1
  102.9 1.3 %pick.1 = (f32[16,128]{1,0:T(8,128)}, f32[16,128]{1,0:T(8,128)}) custom-call(s32[4]{0:T(128)S(1)} %pad_add_fusion.2.where_ref, s32[64]{0:T(128)S(1)} %copy-done.4, f32[2,16,128]{2,1,0:T(8,128)S(1)} %pad_maximum_fusion.2.part_0, f32[2,16,128]{2,1,0:T(8,128)S(1)} %collective-permute-done.21.part_1, f32[2,16,128]{2,1,0:T(8,128)S(1)} %collective-permute-done.22.part_2, ...), custom_call_target="tpu_custom_call" | custom-call | tf_op jit(solution)/shard_map/pick/pallas_call | solution.py:538
  (15 shorter events, 0.1 us)
Async XLA Ops:
  0.6 13.3 %copy-start = (bf16[2048,512]{1,0:T(8,128)(2,1)S(1)}, bf16[2048,512]{1,0:T(8,128)(2,1)}, u32[]{:S(2)}) copy-start(bf16[2048,512]{1,0:T(8,128)(2,1)} %param.5) | copy-start | bytes 6291460
  0.6 7.8 %copy-start.5 = (s32[1,16]{1,0:T(1,128)S(1)}, s32[1,16]{1,0:T(1,128)}, u32[]{:S(2)}) copy-start(s32[1,16]{1,0:T(1,128)} %counts_ref.1) | copy-start | bytes 196
  0.7 67.7 %collective-permute-start.7 = (bf16[2048,512]{1,0:T(8,128)(2,1)}, bf16[2048,512]{1,0:T(8,128)(2,1)}, u32[]{:S(2)}, u32[]{:S(2)}) collective-permute-start(bf16[2048,512]{1,0:T(8,128)(2,1)} %bitcast.30), channel_id=1, source_target_pairs={{0,1},{1,0},{2,3},{3,2},{4,5},{5,4},{6,7},{7,6},{8,9},{9,8},{10,11... | collective-permute-start | bytes 6291464 | tf_op jit(solution)/shard_map/ppermute | solution.py:443
  1.2 1.6 %copy-start.1 = (bf16[1,2048,512]{2,1,0:T(8,128)(2,1)S(1)}, bf16[1,2048,512]{2,1,0:T(8,128)(2,1)}, u32[]{:S(2)}) copy-start(bf16[1,2048,512]{2,1,0:T(8,128)(2,1)} %param.6) | copy-start | bytes 6291460
  2.9 5.5 %copy-start.3 = (s32[1,16,24]{2,1,0:T(8,128)S(1)}, s32[1,16,24]{2,1,0:T(8,128)}, u32[]{:S(2)}) copy-start(s32[1,16,24]{2,1,0:T(8,128)} %param.7) | copy-start | bytes 4612
  3.4 14.6 %collective-permute-start.5 = (f32[16,128]{1,0:T(8,128)S(1)}, f32[16,128]{1,0:T(8,128)S(1)}, u32[]{:S(2)}, u32[]{:S(2)}) collective-permute-start(f32[16,128]{1,0:T(8,128)S(1)} %medoid_norms.1), channel_id=1, source_target_pairs={{0,1},{1,0},{2,3},{3,2},{4,5},{5,4},{6,7},{7,6},{8,9},{9,8},{10,11... | collective-permute-start | bytes 24584 | tf_op jit(solution)/shard_map/ppermute | solution.py:479
  5.5 37.0 %collective-permute-start.10 = (bf16[640,512]{1,0:T(8,128)(2,1)}, bf16[640,512]{1,0:T(8,128)(2,1)}, u32[]{:S(2)}, u32[]{:S(2)}) collective-permute-start(bf16[640,512]{1,0:T(8,128)(2,1)} %dynamic-slice_bitcast_fusion), channel_id=1, source_target_pairs={{0,2},{1,3},{2,0},{3,1},{4,6},{5,7},{6,4},{7,5},{8,10},{9,11},{10,... | collective-permute-start | bytes 1966088 | tf_op jit(solution)/shard_map/ppermute | solution.py:440
  13.6 3.8 %collective-permute-start = (s32[16,128]{1,0:T(8,128)S(1)}, s32[16,128]{1,0:T(8,128)S(1)}, u32[]{:S(2)}, u32[]{:S(2)}) collective-permute-start(s32[16,128]{1,0:T(8,128)S(1)} %split.1), channel_id=1, source_target_pairs={{0,1},{1,0},{2,3},{3,2},{4,5},{5,4},{6,7},{7,6},{8,9},{9,8},{10,11... | collective-permute-start | bytes 24584 | tf_op jit(solution)/shard_map/ppermute | solution.py:462
  14.0 44.3 %collective-permute-start.9 = (bf16[512,512]{1,0:T(8,128)(2,1)S(1)}, bf16[512,512]{1,0:T(8,128)(2,1)S(1)}, u32[]{:S(2)}, u32[]{:S(2)}) collective-permute-start(bf16[512,512]{1,0:T(8,128)(2,1)S(1)} %constant_dynamic-slice_fusion.own_frames.refs_0_), channel_id=1, source_target_pairs={{0,8},{4,12},{8,0},{12,4},{1,9},{5,13},{9,1},{13,5},{2,10},{6,14},... | collective-permute-start | bytes 1572872 | tf_op jit(solution)/shard_map/ppermute | solution.py:434
  17.4 40.9 %collective-permute-start.11 = (bf16[768,512]{1,0:T(8,128)(2,1)}, bf16[768,512]{1,0:T(8,128)(2,1)}, u32[]{:S(2)}, u32[]{:S(2)}) collective-permute-start(bf16[768,512]{1,0:T(8,128)(2,1)} %slice_bitcast_fusion), channel_id=1, source_target_pairs={{0,2},{1,3},{2,0},{3,1},{4,6},{5,7},{6,4},{7,5},{8,10},{9,11},{10,... | collective-permute-start | bytes 2359304 | tf_op jit(solution)/shard_map/ppermute | solution.py:441
  18.0 22.8 %collective-permute-start.1 = (s32[2,16,128]{2,1,0:T(8,128)S(1)}, s32[2,16,128]{2,1,0:T(8,128)S(1)}, u32[]{:S(2)}, u32[]{:S(2)}) collective-permute-start(s32[2,16,128]{2,1,0:T(8,128)S(1)} %pad_add_fusion.1), channel_id=1, source_target_pairs={{0,2},{1,3},{2,0},{3,1},{4,6},{5,7},{6,4},{7,5},{8,10},{9,11},{10,... | collective-permute-start | bytes 49160 | tf_op jit(solution)/shard_map/ppermute | solution.py:463
  40.8 3.7 %collective-permute-start.6 = (f32[2,16,128]{2,1,0:T(8,128)S(1)}, f32[2,16,128]{2,1,0:T(8,128)S(1)}, u32[]{:S(2)}, u32[]{:S(2)}) collective-permute-start(f32[2,16,128]{2,1,0:T(8,128)S(1)} %pad_maximum_fusion.1.norms_in), channel_id=1, source_target_pairs={{0,2},{1,3},{2,0},{3,1},{4,6},{5,7},{6,4},{7,5},{8,10},{9,11},{10,... | collective-permute-start | bytes 49160 | tf_op jit(solution)/shard_map/ppermute | solution.py:480
  42.5 16.3 %collective-permute-start.12 = (bf16[640,512]{1,0:T(8,128)(2,1)}, bf16[640,512]{1,0:T(8,128)(2,1)}, u32[]{:S(2)}, u32[]{:S(2)}) collective-permute-start(bf16[640,512]{1,0:T(8,128)(2,1)} %collective-permute-done.10.far_a), channel_id=1, source_target_pairs={{0,16},{16,0},{1,17},{17,1},{2,18},{18,2},{3,19},{19,3},{4,20},{20... | collective-permute-start | bytes 1966088 | tf_op jit(solution)/shard_map/ppermute | solution.py:442
  44.5 4.5 %collective-permute-start.3 = (s32[4,4,32]{2,1,0:T(4,128)S(1)}, s32[4,4,32]{2,1,0:T(4,128)S(1)}, u32[]{:S(2)}, u32[]{:S(2)}) collective-permute-start(s32[4,4,32]{2,1,0:T(4,128)S(1)} %bitcast.49), channel_id=1, source_target_pairs={{0,8},{4,12},{8,0},{12,4},{1,9},{5,13},{9,1},{13,5},{2,10},{6,14},... | collective-permute-start | bytes 6152 | tf_op jit(solution)/shard_map/ppermute | solution.py:469
  49.1 3.7 %collective-permute-start.2 = (s32[4,4,32]{2,1,0:T(4,128)S(1)}, s32[4,4,32]{2,1,0:T(4,128)S(1)}, u32[]{:S(2)}, u32[]{:S(2)}) collective-permute-start(s32[4,4,32]{2,1,0:T(4,128)S(1)} %bitcast.48), channel_id=1, source_target_pairs={{0,4},{4,0},{8,12},{12,8},{1,5},{5,1},{9,13},{13,9},{2,6},{6,2},{1... | collective-permute-start | bytes 6152 | tf_op jit(solution)/shard_map/ppermute | solution.py:469
  52.7 5.6 %collective-permute-start.4 = (s32[4,4,32]{2,1,0:T(4,128)S(1)}, s32[4,4,32]{2,1,0:T(4,128)S(1)}, u32[]{:S(2)}, u32[]{:S(2)}) collective-permute-start(s32[4,4,32]{2,1,0:T(4,128)S(1)} %bitcast.47), channel_id=1, source_target_pairs={{0,12},{4,8},{8,4},{12,0},{1,13},{5,9},{9,5},{13,1},{2,14},{6,10},... | collective-permute-start | bytes 6152 | tf_op jit(solution)/shard_map/ppermute | solution.py:469
  58.3 9.4 %collective-permute-start.8 = (bf16[512,512]{1,0:T(8,128)(2,1)S(1)}, bf16[512,512]{1,0:T(8,128)(2,1)S(1)}, u32[]{:S(2)}, u32[]{:S(2)}) collective-permute-start(bf16[512,512]{1,0:T(8,128)(2,1)S(1)} %constant_dynamic-slice_fusion.own_frames.refs_0_), channel_id=1, source_target_pairs={{0,4},{4,0},{8,12},{12,8},{1,5},{5,1},{9,13},{13,9},{2,6},{6,2},{1... | collective-permute-start | bytes 1572872 | tf_op jit(solution)/shard_map/ppermute | solution.py:435
  58.3 22.7 %collective-permute-start.14 = (bf16[768,512]{1,0:T(8,128)(2,1)}, bf16[768,512]{1,0:T(8,128)(2,1)S(1)}, u32[]{:S(2)}, u32[]{:S(2)}) collective-permute-start(bf16[768,512]{1,0:T(8,128)(2,1)} %collective-permute-done.11.far_b), channel_id=1, source_target_pairs={{0,1},{1,0},{2,3},{3,2},{4,5},{5,4},{6,7},{7,6},{8,9},{9,8},{10,11... | collective-permute-start | bytes 2359304 | tf_op jit(solution)/shard_map/ppermute | solution.py:445
  58.3 22.6 %collective-permute-start.13 = (bf16[640,512]{1,0:T(8,128)(2,1)}, bf16[640,512]{1,0:T(8,128)(2,1)S(1)}, u32[]{:S(2)}, u32[]{:S(2)}) collective-permute-start(bf16[640,512]{1,0:T(8,128)(2,1)} %collective-permute-done.10.far_a), channel_id=1, source_target_pairs={{0,1},{1,0},{2,3},{3,2},{4,5},{5,4},{6,7},{7,6},{8,9},{9,8},{10,11... | collective-permute-start | bytes 1966088 | tf_op jit(solution)/shard_map/ppermute | solution.py:444
  58.8 22.1 %collective-permute-start.15 = (bf16[640,512]{1,0:T(8,128)(2,1)}, bf16[640,512]{1,0:T(8,128)(2,1)S(1)}, u32[]{:S(2)}, u32[]{:S(2)}) collective-permute-start(bf16[640,512]{1,0:T(8,128)(2,1)} %collective-permute-done.12.far_c), channel_id=1, source_target_pairs={{0,1},{1,0},{2,3},{3,2},{4,5},{5,4},{6,7},{7,6},{8,9},{9,8},{10,11... | collective-permute-start | bytes 1966088 | tf_op jit(solution)/shard_map/ppermute | solution.py:446
  67.7 12.6 %collective-permute-start.16 = (bf16[512,512]{1,0:T(8,128)(2,1)S(1)}, bf16[512,512]{1,0:T(8,128)(2,1)S(1)}, u32[]{:S(2)}, u32[]{:S(2)}) collective-permute-start(bf16[512,512]{1,0:T(8,128)(2,1)S(1)} %constant_dynamic-slice_fusion.own_frames.refs_0_), channel_id=1, source_target_pairs={{4,8},{8,4},{5,9},{9,5},{6,10},{10,6},{7,11},{11,7},{20,24},{24,20... | collective-permute-start | bytes 1572872 | tf_op jit(solution)/shard_map/ppermute | solution.py:436
  68.4 12.6 %collective-permute-start.17 = (bf16[512,512]{1,0:T(8,128)(2,1)S(1)}, bf16[512,512]{1,0:T(8,128)(2,1)S(1)}, u32[]{:S(2)}, u32[]{:S(2)}) collective-permute-start(bf16[512,512]{1,0:T(8,128)(2,1)S(1)} %collective-permute-done.9.frames_2.refs_2_), channel_id=1, source_target_pairs={{8,12},{4,0},{9,13},{5,1},{10,14},{6,2},{11,15},{7,3},{24,28},{20,... | collective-permute-start | bytes 1572872 | tf_op jit(solution)/shard_map/ppermute | solution.py:437
  70.1 1.6 %copy-start.2 = (bf16[1,2048,512]{2,1,0:T(8,128)(2,1)S(1)}, bf16[1,2048,512]{2,1,0:T(8,128)(2,1)}, u32[]{:S(2)}) copy-start(bf16[1,2048,512]{2,1,0:T(8,128)(2,1)} %param.6) | copy-start | bytes 6291460
  80.3 22.6 %copy-start.4 = (s32[64]{0:T(128)S(1)}, s32[64]{0:T(128)}, u32[]{:S(2)}) copy-start(s32[64]{0:T(128)} %plan_ref.1) | copy-start | bytes 772
  89.4 6.6 %collective-permute-start.20 = (f32[2,16,128]{2,1,0:T(8,128)S(1)}, f32[2,16,128]{2,1,0:T(8,128)S(1)}, u32[]{:S(2)}, u32[]{:S(2)}) collective-permute-start(f32[2,16,128]{2,1,0:T(8,128)S(1)} %far_search.1), channel_id=1, source_target_pairs={{0,12},{4,8},{8,4},{12,0},{1,13},{5,9},{9,5},{13,1},{2,14},{6,10},... | collective-permute-start | bytes 49160 | tf_op jit(solution)/shard_map/ppermute | solution.py:534
  94.3 4.6 %collective-permute-start.19 = (f32[2,16,128]{2,1,0:T(8,128)S(1)}, f32[2,16,128]{2,1,0:T(8,128)S(1)}, u32[]{:S(2)}, u32[]{:S(2)}) collective-permute-start(f32[2,16,128]{2,1,0:T(8,128)S(1)} %far_search.1), channel_id=1, source_target_pairs={{0,8},{4,12},{8,0},{12,4},{1,9},{5,13},{9,1},{13,5},{2,10},{6,14},... | collective-permute-start | bytes 49160 | tf_op jit(solution)/shard_map/ppermute | solution.py:534
  94.5 4.5 %collective-permute-start.18 = (f32[2,16,128]{2,1,0:T(8,128)S(1)}, f32[2,16,128]{2,1,0:T(8,128)S(1)}, u32[]{:S(2)}, u32[]{:S(2)}) collective-permute-start(f32[2,16,128]{2,1,0:T(8,128)S(1)} %far_search.1), channel_id=1, source_target_pairs={{0,4},{4,0},{8,12},{12,8},{1,5},{5,1},{9,13},{13,9},{2,6},{6,2},{1... | collective-permute-start | bytes 49160 | tf_op jit(solution)/shard_map/ppermute | solution.py:534
  99.0 3.2 %collective-permute-start.23 = (f32[2,16,128]{2,1,0:T(8,128)S(1)}, f32[2,16,128]{2,1,0:T(8,128)S(1)}, u32[]{:S(2)}, u32[]{:S(2)}) collective-permute-start(f32[2,16,128]{2,1,0:T(8,128)S(1)} %pad_maximum_fusion.2.part_0), channel_id=1, source_target_pairs={{0,3},{1,2},{2,1},{3,0},{4,7},{5,6},{6,5},{7,4},{8,11},{9,10},{10,... | collective-permute-start | bytes 49160 | tf_op jit(solution)/shard_map/ppermute | solution.py:537
  99.0 3.8 %collective-permute-start.22 = (f32[2,16,128]{2,1,0:T(8,128)S(1)}, f32[2,16,128]{2,1,0:T(8,128)S(1)}, u32[]{:S(2)}, u32[]{:S(2)}) collective-permute-start(f32[2,16,128]{2,1,0:T(8,128)S(1)} %pad_maximum_fusion.2.part_0), channel_id=1, source_target_pairs={{0,2},{1,3},{2,0},{3,1},{4,6},{5,7},{6,4},{7,5},{8,10},{9,11},{10,... | collective-permute-start | bytes 49160 | tf_op jit(solution)/shard_map/ppermute | solution.py:537
  99.6 3.2 %collective-permute-start.21 = (f32[2,16,128]{2,1,0:T(8,128)S(1)}, f32[2,16,128]{2,1,0:T(8,128)S(1)}, u32[]{:S(2)}, u32[]{:S(2)}) collective-permute-start(f32[2,16,128]{2,1,0:T(8,128)S(1)} %pad_maximum_fusion.2.part_0), channel_id=1, source_target_pairs={{0,1},{1,0},{2,3},{3,2},{4,5},{5,4},{6,7},{7,6},{8,9},{9,8},{10,11... | collective-permute-start | bytes 49160 | tf_op jit(solution)/shard_map/ppermute | solution.py:537

commit v2 on v1

--- a/solution.py
+++ b/solution.py
@@ -13,10 +13,11 @@
 
 big_value = 1e30
 per_block = 8
-unroll = 4
-together = 2
+unroll = 2
+together = 6
 small_vmem = 8 << 20
 large_vmem = 24 << 20
+whole_vmem = 61 << 20
 
 
 def fold_two(left_one, left_two, right_one, right_two):
@@ -142,29 +143,52 @@
     return one[0:1], two[0:1]
 
 
-def split_kernel(members, where_ref, ids_ref, counts_ref, lists_ref):
-    tiles_here = where_ref[3]
+def cut_kernel(frames_ref, group_ref, mine_ref, edge_ref, middle_ref, sems):
+    quarter = mine_ref.shape[0]
+    side = edge_ref.shape[0]
+    piece = pl.multiple_of(lax.axis_index("medoids") * quarter, TILE)
+    end = pl.multiple_of(lax.axis_index("slab") * (group_ref.shape[0] - side), TILE)
+    copies = (
+        pltpu.make_async_copy(frames_ref.at[pl.ds(piece, quarter)], mine_ref, sems.at[0]),
+        pltpu.make_async_copy(group_ref.at[pl.ds(end, side)], edge_ref, sems.at[1]),
+        pltpu.make_async_copy(
+            group_ref.at[pl.ds(side, middle_ref.shape[0])], middle_ref, sems.at[2]
+        ),
+    )
+    for copy in copies:
+        copy.start()
+    for copy in copies:
+        copy.wait()
+
+
+def split_kernel(members, tiles_here, ids_ref, lists_ref):
+    member = lax.axis_index("frames")
+    rows, columns = ids_ref.shape
     lanes = lists_ref.shape[1] // members
-    member = where_ref[0]
-
-    def split(tile, _):
-        for shard in range(members):
-            lists_ref[tile, shard * lanes + lanes - 1] = 0
-
-        def take(at, _):
-            entry = ids_ref[tile, at]
-            owner = jnp.int32(0)
-            for shard in range(1, members):
-                owner = owner + (entry >= shard * tiles_here).astype(jnp.int32)
-            start = jnp.bitwise_xor(owner, member) * lanes
-            place = lists_ref[tile, start + lanes - 1]
-            lists_ref[tile, start + place] = entry - owner * tiles_here
-            lists_ref[tile, start + lanes - 1] = place + 1
-            return 0
-
-        return lax.fori_loop(0, counts_ref[0, tile], take, 0)
-
-    lax.fori_loop(0, ids_ref.shape[0], split, 0)
+    shape = (rows, members * lanes)
+    lane = lax.broadcasted_iota(jnp.int32, shape, 1)
+    distance = lane // lanes
+    within = lane - distance * lanes
+    shard = jnp.bitwise_xor(distance, member)
+    low = shard * tiles_here
+    count = jnp.broadcast_to(ids_ref[:, columns - 1 : columns], shape)
+    taken = jnp.zeros(shape, jnp.int32)
+    lists = jnp.zeros(shape, jnp.int32)
+    for at in range(columns - 1):
+        entry = jnp.broadcast_to(ids_ref[:, at : at + 1], shape) - low
+        here = (entry >= 0) & (entry < tiles_here) & (at < count)
+        lists = jnp.where(here & (within == taken), entry, lists)
+        taken = taken + here.astype(jnp.int32)
+    lists_ref[...] = jnp.where(within == lanes - 1, taken, lists)
+
+
+def route_kernel(own_ref, near_ref, far_ref, out_ref):
+    quarter_tiles = out_ref.shape[0] // 4
+    start = lax.axis_index("medoids") * quarter_tiles
+    for slot, ref in enumerate((own_ref, near_ref, far_ref.at[0], far_ref.at[1])):
+        for tile in range(quarter_tiles):
+            row = slot * quarter_tiles + tile
+            out_ref[row : row + 1, :] = ref[pl.ds(start + tile, 1), :]
 
 
 def norms_kernel(scale, *refs):
@@ -181,9 +205,12 @@
     tiles, slots, first_tile, quarter_tiles, tiles_here, lists_ref, rows_ref, norms_ref,
     frames_ref, one_ref, two_ref, table_ref,
 ):
-    last_lane = lists_ref.shape[3] - 1
+    lanes = lists_ref.shape[2] // lists_ref.shape[0]
     dummy = len(slots) * tiles_here
     shift = 16
+
+    def listed(zslot, slot, tile, place):
+        return lists_ref[zslot, slot * quarter_tiles + tile, zslot * lanes + place]
 
     def place_of(index):
         zslot = index // quarter_tiles
@@ -193,7 +220,7 @@
         zslot, tile = place_of(index)
         ends, number = [], jnp.int32(0)
         for slot in slots:
-            number = number + lists_ref[zslot, slot, tile, last_lane]
+            number = number + listed(zslot, slot, tile, lanes - 1)
             ends.append(number)
         return ends
 
@@ -233,7 +260,7 @@
                     slot = jnp.where(beyond, number, slot)
                     start = jnp.where(beyond, ends[number - 1], start)
                 place = jnp.where(live, place - start, 0)
-                entry = lists_ref[zslot, slots[0] + slot, tile, place] + slot * tiles_here
+                entry = listed(zslot, slots[0] + slot, tile, place) + slot * tiles_here
                 row = jnp.where(live, entry, 0) * TILE
                 picked.append(rows_ref[pl.ds(pl.multiple_of(row, TILE), TILE), :])
                 picked_norm.append(norms_ref[pl.ds(jnp.where(live, entry, dummy), 1), :])
@@ -259,8 +286,9 @@
 
 
 def near_kernel(
-    lists_ref, norms_in, own_group, near_group, own_frames, frames_1, frames_2,
-    out_ref, rows_buf, frames_buf, norms_buf, one_buf, two_buf, table_ref, sems,
+    lists_0, lists_1, lists_2, lists_3, norms_own, norms_near, own_group, near_group,
+    own_frames, frames_1, frames_2,
+    out_ref, lists_ref, rows_buf, frames_buf, norms_buf, one_buf, two_buf, table_ref, sems,
 ):
     tile_rows = own_group.shape[0]
     tiles_here = tile_rows // TILE
@@ -276,10 +304,12 @@
                 ref, frames_buf.at[pl.ds(index * quarter, quarter)], sems.at[2 + index]
             )
         )
+    for index, ref in enumerate((lists_0, lists_1, lists_2, lists_3)):
+        copies.append(pltpu.make_async_copy(ref, lists_ref.at[index], sems.at[5 + index]))
     for copy in copies:
         copy.start()
-    norms_buf[pl.ds(0, tiles_here), :] = norms_in[0]
-    norms_buf[pl.ds(tiles_here, tiles_here), :] = norms_in[1]
+    norms_buf[pl.ds(0, tiles_here), :] = norms_own[...]
+    norms_buf[pl.ds(tiles_here, tiles_here), :] = norms_near[...]
     norms_buf[pl.ds(2 * tiles_here, 1), :] = jnp.full((1, TILE), big_value, jnp.float32)
     for copy in copies:
         copy.wait()
@@ -295,19 +325,20 @@
 
 
 def far_kernel(
-    where_ref, lists_ref, norms_in, before_ref, frame_norms, own_group, near_group,
-    far_a, far_b, far_c, last_a, last_b, last_c, own_frames, frames_1, frames_2, frames_3a, frames_3b,
-    out_ref, rows_buf, frames_buf, norms_buf, one_buf, two_buf, table_ref, sems,
+    lists_0, lists_1, lists_2, lists_3, norms_own, norms_near, norms_far, before_ref, frame_norms,
+    own_group, near_group, far_a, far_b, far_c, last_a, last_b, last_c,
+    own_frames, frames_1, frames_2, frames_3a, frames_3b,
+    out_ref, lists_ref, rows_buf, frames_buf, norms_buf, one_buf, two_buf, table_ref, sems,
 ):
     tile_rows = own_group.shape[0]
     tiles_here = tile_rows // TILE
-    groups = norms_in.shape[0]
+    groups = 2 + norms_far.shape[0]
     quarter = own_frames.shape[0]
     quarter_tiles = quarter // TILE
     width = own_frames.shape[1]
     members = frames_buf.shape[0] // quarter
-    member = where_ref[0]
-    slab = where_ref[2]
+    member = lax.axis_index("frames")
+    slab = lax.axis_index("slab")
     side = far_a.shape[0]
     middle = far_b.shape[0]
     near_side = slab * (tile_rows - side)
@@ -332,6 +363,8 @@
     bring(own_frames, frames_buf, 0, quarter)
     bring(frames_1, frames_buf, quarter, quarter)
     bring(frames_2, frames_buf, 2 * quarter, quarter)
+    for index, ref in enumerate((lists_0, lists_1, lists_2, lists_3)):
+        copies.append(pltpu.make_async_copy(ref, lists_ref.at[index], sems.at[len(copies)]))
     early = len(copies)
     bring(own_group, rows_buf, 0, tile_rows)
     bring(near_group, rows_buf, tile_rows, tile_rows)
@@ -353,8 +386,8 @@
         copy.start()
 
     dummy = groups * tiles_here
-    for slot in range(groups):
-        norms_buf[pl.ds(slot * tiles_here, tiles_here), :] = norms_in[slot]
+    for slot, norms in enumerate((norms_own, norms_near, norms_far.at[0], norms_far.at[1])):
+        norms_buf[pl.ds(slot * tiles_here, tiles_here), :] = norms[...]
     norms_buf[pl.ds(dummy, 1), :] = jnp.full((1, TILE), big_value, jnp.float32)
     for copy in copies[:early]:
         copy.wait()
@@ -393,9 +426,9 @@
         finish(early_tiles + tile, tile, None, None, column_of(rows * rows))
 
 
-def pick_kernel(where_ref, plan_ref, part_0, part_1, part_2, part_3, first_ref, second_ref, every):
-    member = where_ref[0]
-    piece = where_ref[1]
+def pick_kernel(plan_ref, part_0, part_1, part_2, part_3, first_ref, second_ref, every):
+    member = lax.axis_index("frames")
+    piece = lax.axis_index("medoids")
     blocks = first_ref.shape[0]
     parts = (part_0, part_1, part_2, part_3)
     quarter_tiles = blocks // len(parts)
@@ -421,24 +454,37 @@
     blocks = frames.shape[0] // TILE
     members = lax.axis_size("frames")
     groups = lax.axis_size("medoids")
-    member = lax.axis_index("frames")
-    piece = lax.axis_index("medoids")
-    slab = lax.axis_index("slab")
     rows = medoids[0]
     tile_rows = rows.shape[0]
     quarter_tiles = blocks // groups
     quarter = quarter_tiles * TILE
     side = tile_rows // TILE // 3 * TILE
 
-    mine = lax.dynamic_slice_in_dim(frames, piece * quarter, quarter)
+    hbm = pl.BlockSpec(memory_space=pl.ANY)
+    scalar = pl.BlockSpec(memory_space=pltpu.SMEM)
+    vector = pl.BlockSpec(memory_space=pltpu.VMEM)
+    small = pltpu.CompilerParams(vmem_limit_bytes=small_vmem)
+    large = pltpu.CompilerParams(vmem_limit_bytes=large_vmem)
+    mine, edge, inside_rows = pl.pallas_call(
+        cut_kernel,
+        out_shape=(
+            jax.ShapeDtypeStruct((quarter, width), frames.dtype),
+            jax.ShapeDtypeStruct((side, width), rows.dtype),
+            jax.ShapeDtypeStruct((tile_rows - 2 * side, width), rows.dtype),
+        ),
+        in_specs=[hbm, hbm],
+        out_specs=(vector, vector, vector),
+        scratch_shapes=[pltpu.SemaphoreType.DMA((3,))],
+        compiler_params=pltpu.CompilerParams(vmem_limit_bytes=whole_vmem),
+        name="cut",
+    )(frames, rows)
     frames_2 = lax.ppermute(mine, "frames", exchanged(members, 2))
     frames_1 = lax.ppermute(mine, "frames", exchanged(members, 1))
     frames_3a = lax.ppermute(mine, "frames", [(1, 2), (2, 1)])
     frames_3b = lax.ppermute(frames_2, "frames", [(2, 3), (1, 0)])
 
-    edge = lax.dynamic_slice_in_dim(rows, slab * (tile_rows - side), side)
     far_a = lax.ppermute(edge, "medoids", exchanged(groups, 2))
-    far_b = lax.ppermute(rows[side : tile_rows - side], "medoids", exchanged(groups, 2))
+    far_b = lax.ppermute(inside_rows, "medoids", exchanged(groups, 2))
     far_c = lax.ppermute(far_a, "slab", exchanged(2, 1))
     near_group = lax.ppermute(rows, "medoids", exchanged(groups, 1))
     last_a = lax.ppermute(far_a, "medoids", exchanged(groups, 1))
@@ -446,45 +492,41 @@
     last_c = lax.ppermute(far_c, "medoids", exchanged(groups, 1))
 
     tiles_here = tile_rows // TILE
-    where = jnp.stack([member, piece, slab, jnp.int32(tiles_here)]).astype(jnp.int32)
-    hbm = pl.BlockSpec(memory_space=pl.ANY)
-    scalar = pl.BlockSpec(memory_space=pltpu.SMEM)
-    vector = pl.BlockSpec(memory_space=pltpu.VMEM)
-    lanes = TILE // members
     listed = pl.pallas_call(
-        functools.partial(split_kernel, members),
-        out_shape=jax.ShapeDtypeStruct((blocks, members * lanes), jnp.int32),
-        in_specs=[scalar] * 3,
-        out_specs=scalar,
-        compiler_params=pltpu.CompilerParams(vmem_limit_bytes=small_vmem),
+        functools.partial(split_kernel, members, tiles_here),
+        out_shape=jax.ShapeDtypeStruct((blocks, TILE), jnp.int32),
+        in_specs=[vector],
+        out_specs=vector,
+        compiler_params=small,
         name="split",
-    )(where, tile_ids[0], tile_counts)
-    pair = jnp.stack([listed, lax.ppermute(listed, "medoids", exchanged(groups, 1))])
-    far_pair = lax.ppermute(pair, "medoids", exchanged(groups, 2))
-    lists = jnp.concatenate([pair, far_pair], axis=0)
-    lists = lax.dynamic_slice_in_dim(lists, piece * quarter_tiles, quarter_tiles, axis=1)
-    lists = lists.reshape(groups, quarter_tiles, members, lanes)
-    lists = jnp.stack(
-        [lists[:, :, 0]]
-        + [lax.ppermute(lists[:, :, at], "frames", exchanged(members, at)) for at in (1, 2, 3)]
-    )
+    )(jnp.concatenate([tile_ids[0], tile_counts[0][:, None]], axis=1))
+    near_listed = lax.ppermute(listed, "medoids", exchanged(groups, 1))
+    far_listed = lax.ppermute(jnp.stack([listed, near_listed]), "medoids", exchanged(groups, 2))
+    lists = pl.pallas_call(
+        route_kernel,
+        out_shape=jax.ShapeDtypeStruct((groups * quarter_tiles, TILE), jnp.int32),
+        in_specs=[vector] * 3,
+        out_specs=vector,
+        compiler_params=small,
+        name="route",
+    )(listed, near_listed, far_listed)
+    lists = [lists] + [lax.ppermute(lists, "frames", exchanged(members, at)) for at in (1, 2, 3)]
     norms = pl.pallas_call(
         functools.partial(norms_kernel, 0.5),
         out_shape=jax.ShapeDtypeStruct((tiles_here, TILE), jnp.float32),
         in_specs=[vector],
         out_specs=vector,
-        compiler_params=pltpu.CompilerParams(vmem_limit_bytes=small_vmem),
+        compiler_params=small,
         name="medoid_norms",
     )(rows)
-    norm_pair = jnp.stack([norms, lax.ppermute(norms, "medoids", exchanged(groups, 1))])
-    norm_far = lax.ppermute(norm_pair, "medoids", exchanged(groups, 2))
-    norms = jnp.concatenate([norm_pair, norm_far], axis=0)
+    norm_near = lax.ppermute(norms, "medoids", exchanged(groups, 1))
+    norm_far = lax.ppermute(jnp.stack([norms, norm_near]), "medoids", exchanged(groups, 2))
     frame_norms = pl.pallas_call(
         functools.partial(norms_kernel, 1.0),
         out_shape=jax.ShapeDtypeStruct((3 * quarter_tiles, TILE), jnp.float32),
         in_specs=[vector] * 3,
         out_specs=vector,
-        compiler_params=pltpu.CompilerParams(vmem_limit_bytes=small_vmem),
+        compiler_params=small,
         name="frame_norms",
     )(mine, frames_1, frames_2)
 
@@ -494,38 +536,40 @@
     before = pl.pallas_call(
         near_kernel,
         out_shape=jax.ShapeDtypeStruct((2, early_tiles, TILE), jnp.float32),
-        in_specs=[scalar, vector] + [hbm] * 5,
+        in_specs=[hbm] * 4 + [vector] * 2 + [hbm] * 5,
         out_specs=vector,
         scratch_shapes=[
+            pltpu.SMEM((members, groups * quarter_tiles, TILE), jnp.int32),
             pltpu.VMEM((2 * tile_rows, width), jnp.bfloat16),
             pltpu.VMEM((3 * quarter, width), jnp.bfloat16),
             pltpu.VMEM((2 * tiles_here + 8, TILE), jnp.float32),
             pltpu.VMEM((3 * quarter, TILE), jnp.float32),
             pltpu.VMEM((3 * quarter, TILE), jnp.float32),
             pltpu.SMEM((table_size,), jnp.int32),
-            pltpu.SemaphoreType.DMA((5,)),
+            pltpu.SemaphoreType.DMA((9,)),
         ],
-        compiler_params=pltpu.CompilerParams(vmem_limit_bytes=large_vmem),
+        compiler_params=large,
         name="near_search",
-    )(lists, norm_pair, rows, near_group, mine, frames_1, frames_2)
+    )(*lists, norms, norm_near, rows, near_group, mine, frames_1, frames_2)
     found = pl.pallas_call(
         far_kernel,
         out_shape=jax.ShapeDtypeStruct((2, total_tiles, TILE), jnp.float32),
-        in_specs=[scalar, scalar, vector, vector, vector] + [hbm] * 13,
+        in_specs=[hbm] * 4 + [vector] * 5 + [hbm] * 13,
         out_specs=vector,
         scratch_shapes=[
+            pltpu.SMEM((members, groups * quarter_tiles, TILE), jnp.int32),
             pltpu.VMEM((groups * tile_rows, width), jnp.bfloat16),
             pltpu.VMEM((members * quarter, width), jnp.bfloat16),
             pltpu.VMEM((groups * tiles_here + 8, TILE), jnp.float32),
             pltpu.VMEM((3 * quarter, TILE), jnp.float32),
             pltpu.VMEM((3 * quarter, TILE), jnp.float32),
             pltpu.SMEM((table_size,), jnp.int32),
-            pltpu.SemaphoreType.DMA((16,)),
+            pltpu.SemaphoreType.DMA((20,)),
         ],
-        compiler_params=pltpu.CompilerParams(vmem_limit_bytes=large_vmem),
+        compiler_params=large,
         name="far_search",
     )(
-        where, lists, norms, before, frame_norms, rows, near_group,
+        *lists, norms, norm_near, norm_far, before, frame_norms, rows, near_group,
         far_a, far_b, far_c, last_a, last_b, last_c, mine, frames_1, frames_2, frames_3a, frames_3b,
     )
 
@@ -538,12 +582,12 @@
     first, second = pl.pallas_call(
         pick_kernel,
         out_shape=(jax.ShapeDtypeStruct((blocks, TILE), jnp.float32),) * 2,
-        in_specs=[scalar, scalar] + [vector] * 4,
+        in_specs=[scalar] + [vector] * 4,
         out_specs=(vector, vector),
         scratch_shapes=[pltpu.VMEM((2, groups * members * quarter_tiles, TILE), jnp.float32)],
-        compiler_params=pltpu.CompilerParams(vmem_limit_bytes=small_vmem),
+        compiler_params=small,
         name="pick",
-    )(where, plan, *parts)
+    )(plan, *parts)
     return (first.reshape(-1), second.reshape(-1))
 
 

time: 104 us -> 102 us (0.981)
  waiting for transfers between devices: 42.4 us -> 51.4 us
  local copies, waits for them, and re-layouts: 7.47 us -> 0.11 us
  Pallas kernels: 24.4 us -> 19 us
  starting transfers between devices: 29 us -> 30.1 us
    ppermute x1, waiting for transfers between devices: 0.01 us -> 11.2 us  [gathered_frames(): far_a = lax.ppermute(edge, 'medoids', exchanged(groups, 2))]
    ppermute x8, waiting for transfers between devices: 27 us -> 22.7 us  [the longest x1 13.2 us: gathered_frames(): lax.ppermute(jnp.stack([listed, near_listed]), 'medoids', exchanged(group...]
    ppermute x1, waiting for transfers between devices: 0.67 us -> 4.44 us  [gathered_frames(): frames_3b = lax.ppermute(frames_2, 'frames', [(2, 3), (1, 0)])]
    unnamed x12 -> x10, local copies, waits for them, and re-layouts: 3.26 us -> 0.02 us
    ppermute x8, starting transfers between devices: 12.8 us -> 10.3 us  [the longest x3 6.39 us: gathered_frames(): lax.ppermute(lists, 'frames', exchanged(members, at))]
    pallas_call x1 -> x3, Pallas kernels: 5.21 us -> 3.04 us  [the longest x1 2.88 us: gathered_frames(): pl.pallas_call(cut_kernel, out_shape=(jax.ShapeDtypeStruct((quarter, widt...]
    slice x2 -> x0, local copies, waits for them, and re-layouts: 2.11 us -> none  [the longest x1 2.09 us: gathered_frames(): rows[side:tile_rows - side]]
    dynamic_slice x2 -> x0, local copies, waits for them, and re-layouts: 2.01 us -> none  [the longest x1 1.98 us: gathered_frames(): edge = lax.dynamic_slice_in_dim(rows, slab * (tile_rows - side), side)]
  transfers between devices with their start and end apart: 24 -> 24, of which waited for: 11 -> 13; matrix products, arithmetic and copies ran while one was open for 4% -> 0% of each run, Pallas kernels for 14% -> 11%
where the time goes in v2:
time: 102 us; the launch traced here: 101 us
  waiting for transfers between devices  51.4 us (50%)
  starting transfers between devices  30.1 us (30%)
  Pallas kernels  19 us (19%)
    ppermute x1, waiting for transfers between devices, gathered_frames(): lax.ppermute(jnp.stack([listed, near_listed]), 'medoids', exchanged(group...  13.2 us
    ppermute x1, waiting for transfers between devices, gathered_frames(): far_a = lax.ppermute(edge, 'medoids', exchanged(groups, 2))  11.2 us
    ppermute x3, waiting for transfers between devices, gathered_frames(): lax.ppermute(lists, 'frames', exchanged(members, at))  7.38 us
    ppermute x1, waiting for transfers between devices, gathered_frames(): frames_1 = lax.ppermute(mine, 'frames', exchanged(members, 1))  7.06 us
    pallas_call x1, Pallas kernels, gathered_frames(): pl.pallas_call(near_kernel, out_shape=jax.ShapeDtypeStruct((2, early_tile...  6.92 us
    pallas_call x1, Pallas kernels, gathered_frames(): pl.pallas_call(far_kernel, out_shape=jax.ShapeDtypeStruct((2, total_tiles...  6.82 us
    ppermute x3, starting transfers between devices, gathered_frames(): lax.ppermute(lists, 'frames', exchanged(members, at))  6.39 us
    ppermute x3, starting transfers between devices, gathered_frames(): other = lax.ppermute(found, 'frames', exchanged(members, at))  5.47 us
  transfers between devices with their start and end apart: 24, of which 13 were waited for; matrix products, arithmetic and copies ran while one was open for 0% of the time, Pallas kernels for 11%

profile of v2, /device:TPU:0, one launch (start us, length us, event | category | flops | bytes accessed | tf_op | source)
XLA Modules:
  0.0 101.4 jit_solution(3547669966321925614)
XLA Ops:
  0.6 0.0 copy-start.4
  0.6 0.0 copy-start.3
  0.7 0.0 copy-start
  0.7 0.6 collective-permute-start.7
  1.2 2.9 %cut.1 = (bf16[512,512]{1,0:T(8,128)(2,1)}, bf16[640,512]{1,0:T(8,128)(2,1)}, bf16[768,512]{1,0:T(8,128)(2,1)}) custom-call(bf16[2048,512]{1,0:T(8,128)(2,1)} %frames_ref.1, bf16[2048,512]{1,0:T(8,128)(2,1)} %bitcast.10), custom_call_target="tpu_custom_call" | custom-call | tf_op jit(solution)/shard_map/cut/pallas_call | solution.py:468
  4.1 0.0 copy-start.1
  4.1 2.6 %collective-permute-start.10 = (bf16[640,512]{1,0:T(8,128)(2,1)}, bf16[640,512]{1,0:T(8,128)(2,1)}, u32[]{:S(2)}, u32[]{:S(2)}) collective-permute-start(bf16[640,512]{1,0:T(8,128)(2,1)} %get-tuple-element.8), channel_id=1, source_target_pairs={{0,2},{1,3},{2,0},{3,1},{4,6},{5,7},{6,4},{7,5},{8,10},{9,11},{10,... | collective-permute-start | bytes 1966088 | tf_op jit(solution)/shard_map/ppermute | solution.py:486
  6.7 0.1 collective-permute-start.11
  6.8 0.0 copy-done.4
  6.8 0.1 copy.7
  6.9 0.0 copy-done.3
  6.9 0.1 pad_add_fusion.1.ids_ref
  7.0 0.2 split.1.own_ref
  7.1 0.1 collective-permute-start
  7.3 0.5 medoid_norms.1.norms_own
  7.8 0.5 collective-permute-start.5
  8.3 0.1 collective-permute-done.near_ref
  8.4 3.0 %collective-permute-start.9 = (bf16[512,512]{1,0:T(8,128)(2,1)S(1)}, bf16[512,512]{1,0:T(8,128)(2,1)S(1)}, u32[]{:S(2)}, u32[]{:S(2)}) collective-permute-start(bf16[512,512]{1,0:T(8,128)(2,1)S(1)} %copy-done.1), channel_id=1, source_target_pairs={{0,8},{4,12},{8,0},{12,4},{1,9},{5,13},{9,1},{13,5},{2,10},{6,14},... | collective-permute-start | bytes 1572872 | tf_op jit(solution)/shard_map/ppermute | solution.py:481
  11.4 11.2 %collective-permute-done.10.far_a = bf16[640,512]{1,0:T(8,128)(2,1)} collective-permute-done((bf16[640,512]{1,0:T(8,128)(2,1)}, bf16[640,512]{1,0:T(8,128)(2,1)}, u32[]{:S(2)}, u32[]{:S(2)}) %collective-permute-start.10) | collective-permute-done | bytes 655392 | tf_op jit(solution)/shard_map/ppermute | solution.py:486
  22.6 2.0 %collective-permute-start.12 = (bf16[640,512]{1,0:T(8,128)(2,1)}, bf16[640,512]{1,0:T(8,128)(2,1)S(1)}, u32[]{:S(2)}, u32[]{:S(2)}) collective-permute-start(bf16[640,512]{1,0:T(8,128)(2,1)} %collective-permute-done.10.far_a), channel_id=1, source_target_pairs={{0,16},{16,0},{1,17},{17,1},{2,18},{18,2},{3,19},{19,3},{4,20},{20... | collective-permute-start | bytes 1966088 | tf_op jit(solution)/shard_map/ppermute | solution.py:488
  24.7 0.0 collective-permute-done.5.norms_near
  24.7 1.5 %collective-permute-start.1 = (s32[2,16,128]{2,1,0:T(8,128)S(1)}, s32[2,16,128]{2,1,0:T(8,128)S(1)}, u32[]{:S(2)}, u32[]{:S(2)}) collective-permute-start(s32[2,16,128]{2,1,0:T(8,128)S(1)} %pad_add_fusion), channel_id=1, source_target_pairs={{0,2},{1,3},{2,0},{3,1},{4,6},{5,7},{6,4},{7,5},{8,10},{9,11},{10,... | collective-permute-start | bytes 49160 | tf_op jit(solution)/shard_map/ppermute | solution.py:504
  26.2 13.2 %collective-permute-done.1.far_ref = s32[2,16,128]{2,1,0:T(8,128)S(1)} collective-permute-done((s32[2,16,128]{2,1,0:T(8,128)S(1)}, s32[2,16,128]{2,1,0:T(8,128)S(1)}, u32[]{:S(2)}, u32[]{:S(2)}) %collective-permute-start.1) | collective-permute-done | bytes 16416 | tf_op jit(solution)/shard_map/ppermute | solution.py:504
  39.4 1.7 %collective-permute-start.6 = (f32[2,16,128]{2,1,0:T(8,128)S(1)}, f32[2,16,128]{2,1,0:T(8,128)S(1)}, u32[]{:S(2)}, u32[]{:S(2)}) collective-permute-start(f32[2,16,128]{2,1,0:T(8,128)S(1)} %pad_maximum_fusion), channel_id=1, source_target_pairs={{0,2},{1,3},{2,0},{3,1},{4,6},{5,7},{6,4},{7,5},{8,10},{9,11},{10,... | collective-permute-start | bytes 49160 | tf_op jit(solution)/shard_map/ppermute | solution.py:523
  41.2 2.0 %collective-permute-done.6.norms_far = f32[2,16,128]{2,1,0:T(8,128)S(1)} collective-permute-done((f32[2,16,128]{2,1,0:T(8,128)S(1)}, f32[2,16,128]{2,1,0:T(8,128)S(1)}, u32[]{:S(2)}, u32[]{:S(2)}) %collective-permute-start.6) | collective-permute-done | bytes 16416 | tf_op jit(solution)/shard_map/ppermute | solution.py:523
  43.1 3.8 %collective-permute-start.4 = (s32[16,128]{1,0:T(8,128)S(1)}, s32[16,128]{1,0:T(8,128)S(1)}, u32[]{:S(2)}, u32[]{:S(2)}) collective-permute-start(s32[16,128]{1,0:T(8,128)S(1)} %route.1.lists_0), channel_id=1, source_target_pairs={{0,12},{4,8},{8,4},{12,0},{1,13},{5,9},{9,5},{13,1},{2,14},{6,10},... | collective-permute-start | bytes 24584 | tf_op jit(solution)/shard_map/ppermute | solution.py:513
  47.0 1.6 %collective-permute-done.4.lists_3 = s32[16,128]{1,0:T(8,128)S(1)} collective-permute-done((s32[16,128]{1,0:T(8,128)S(1)}, s32[16,128]{1,0:T(8,128)S(1)}, u32[]{:S(2)}, u32[]{:S(2)}) %collective-permute-start.4) | collective-permute-done | bytes 8224 | tf_op jit(solution)/shard_map/ppermute | solution.py:513
  48.6 1.0 collective-permute-start.3
  49.6 3.5 %collective-permute-done.3.lists_2 = s32[16,128]{1,0:T(8,128)S(1)} collective-permute-done((s32[16,128]{1,0:T(8,128)S(1)}, s32[16,128]{1,0:T(8,128)S(1)}, u32[]{:S(2)}, u32[]{:S(2)}) %collective-permute-start.3) | collective-permute-done | bytes 8224 | tf_op jit(solution)/shard_map/ppermute | solution.py:513
  53.2 1.5 %collective-permute-start.2 = (s32[16,128]{1,0:T(8,128)S(1)}, s32[16,128]{1,0:T(8,128)S(1)}, u32[]{:S(2)}, u32[]{:S(2)}) collective-permute-start(s32[16,128]{1,0:T(8,128)S(1)} %route.1.lists_0), channel_id=1, source_target_pairs={{0,4},{4,0},{8,12},{12,8},{1,5},{5,1},{9,13},{13,9},{2,6},{6,2},{1... | collective-permute-start | bytes 24584 | tf_op jit(solution)/shard_map/ppermute | solution.py:513
  54.7 2.2 %collective-permute-done.2.lists_1 = s32[16,128]{1,0:T(8,128)S(1)} collective-permute-done((s32[16,128]{1,0:T(8,128)S(1)}, s32[16,128]{1,0:T(8,128)S(1)}, u32[]{:S(2)}, u32[]{:S(2)}) %collective-permute-start.2) | collective-permute-done | bytes 8224 | tf_op jit(solution)/shard_map/ppermute | solution.py:513
  56.9 1.5 %collective-permute-start.8 = (bf16[512,512]{1,0:T(8,128)(2,1)S(1)}, bf16[512,512]{1,0:T(8,128)(2,1)S(1)}, u32[]{:S(2)}, u32[]{:S(2)}) collective-permute-start(bf16[512,512]{1,0:T(8,128)(2,1)S(1)} %copy-done.1), channel_id=1, source_target_pairs={{0,4},{4,0},{8,12},{12,8},{1,5},{5,1},{9,13},{13,9},{2,6},{6,2},{1... | collective-permute-start | bytes 1572872 | tf_op jit(solution)/shard_map/ppermute | solution.py:482
  58.4 0.0 collective-permute-done.11.far_b
  58.4 0.0 collective-permute-start.14
  58.5 0.0 collective-permute-done.9.frames_2.refs_2_
  58.5 0.5 collective-permute-start.13
  59.0 0.0 collective-permute-done.12.far_c
  59.0 0.1 collective-permute-start.15
  59.0 7.1 %collective-permute-done.8.frames_1.refs_1_ = bf16[512,512]{1,0:T(8,128)(2,1)S(1)} collective-permute-done((bf16[512,512]{1,0:T(8,128)(2,1)S(1)}, bf16[512,512]{1,0:T(8,128)(2,1)S(1)}, u32[]{:S(2)}, u32[]{:S(2)}) %collective-permute-start.8) | collective-permute-done | bytes 524320 | tf_op jit(solution)/shard_map/ppermute | solution.py:482
  66.1 0.7 collective-permute-start.16
  66.8 0.0 collective-permute-done.7.near_group
  66.8 1.3 %collective-permute-start.17 = (bf16[512,512]{1,0:T(8,128)(2,1)S(1)}, bf16[512,512]{1,0:T(8,128)(2,1)S(1)}, u32[]{:S(2)}, u32[]{:S(2)}) collective-permute-start(bf16[512,512]{1,0:T(8,128)(2,1)S(1)} %collective-permute-done.9.frames_2.refs_2_), channel_id=1, source_target_pairs={{8,12},{4,0},{9,13},{5,1},{10,14},{6,2},{11,15},{7,3},{24,28},{20,... | collective-permute-start | bytes 1572872 | tf_op jit(solution)/shard_map/ppermute | solution.py:484
  68.1 0.4 frame_norms.1
  68.5 6.9 %near_search.1.before_ref = f32[2,12,128]{2,1,0:T(8,128)S(1)} custom-call(s32[16,128]{1,0:T(8,128)S(1)} %route.1.lists_0, s32[16,128]{1,0:T(8,128)S(1)} %collective-permute-done.2.lists_1, s32[16,128]{1,0:T(8,128)S(1)} %collective-permute-done.3.lists_2, s32[16,128]{1,0:T(8,128)S(1)} %collective-permute-done.4.lists_3, f32[16,128]{1,0:T(8,128)S(1)} %medoid_norms.1.norms_own, ...), custom_call_target="tpu_custom_call" | custom-call | tf_op jit(solution)/shard_map/near_search/pallas_call | solution.py:536
  75.4 0.0 copy-start.2
  75.4 0.0 collective-permute-done.16.frames_3a
  75.4 4.4 %collective-permute-done.17.frames_3b = bf16[512,512]{1,0:T(8,128)(2,1)S(1)} collective-permute-done((bf16[512,512]{1,0:T(8,128)(2,1)S(1)}, bf16[512,512]{1,0:T(8,128)(2,1)S(1)}, u32[]{:S(2)}, u32[]{:S(2)}) %collective-permute-start.17) | collective-permute-done | bytes 524320 | tf_op jit(solution)/shard_map/ppermute | solution.py:484
  79.9 0.0 collective-permute-done.13.last_a
  79.9 0.0 collective-permute-done.14.last_b
  79.9 0.0 collective-permute-done.15.last_c
  79.9 6.8 %far_search.1 = f32[2,16,128]{2,1,0:T(8,128)S(1)} custom-call(s32[16,128]{1,0:T(8,128)S(1)} %route.1.lists_0, s32[16,128]{1,0:T(8,128)S(1)} %collective-permute-done.2.lists_1, s32[16,128]{1,0:T(8,128)S(1)} %collective-permute-done.3.lists_2, s32[16,128]{1,0:T(8,128)S(1)} %collective-permute-done.4.lists_3, f32[16,128]{1,0:T(8,128)S(1)} %medoid_norms.1.norms_own, ...), custom_call_target="tpu_custom_call" | custom-call | tf_op jit(solution)/shard_map/far_search/pallas_call | solution.py:554
  86.7 4.8 %collective-permute-start.20 = (f32[2,16,128]{2,1,0:T(8,128)S(1)}, f32[2,16,128]{2,1,0:T(8,128)S(1)}, u32[]{:S(2)}, u32[]{:S(2)}) collective-permute-start(f32[2,16,128]{2,1,0:T(8,128)S(1)} %far_search.1), channel_id=1, source_target_pairs={{0,12},{4,8},{8,4},{12,0},{1,13},{5,9},{9,5},{13,1},{2,14},{6,10},... | collective-permute-start | bytes 49160 | tf_op jit(solution)/shard_map/ppermute | solution.py:578
  91.5 0.0 collective-permute-start.19
  91.5 0.6 collective-permute-start.18
  92.2 1.1 %collective-permute-done.20 = f32[2,16,128]{2,1,0:T(8,128)S(1)} collective-permute-done((f32[2,16,128]{2,1,0:T(8,128)S(1)}, f32[2,16,128]{2,1,0:T(8,128)S(1)}, u32[]{:S(2)}, u32[]{:S(2)}) %collective-permute-start.20) | collective-permute-done | bytes 16416 | tf_op jit(solution)/shard_map/ppermute | solution.py:578
  93.3 2.9 %collective-permute-done.19 = f32[2,16,128]{2,1,0:T(8,128)S(1)} collective-permute-done((f32[2,16,128]{2,1,0:T(8,128)S(1)}, f32[2,16,128]{2,1,0:T(8,128)S(1)}, u32[]{:S(2)}, u32[]{:S(2)}) %collective-permute-start.19) | collective-permute-done | bytes 16416 | tf_op jit(solution)/shard_map/ppermute | solution.py:578
  96.2 0.0 collective-permute-done.18
  96.2 0.1 collective-permute-start.23
  96.3 0.2 collective-permute-start.22
  96.5 1.6 %collective-permute-start.21 = (f32[2,16,128]{2,1,0:T(8,128)S(1)}, f32[2,16,128]{2,1,0:T(8,128)S(1)}, u32[]{:S(2)}, u32[]{:S(2)}) collective-permute-start(f32[2,16,128]{2,1,0:T(8,128)S(1)} %pad_maximum_fusion.1.part_0), channel_id=1, source_target_pairs={{0,1},{1,0},{2,3},{3,2},{4,5},{5,4},{6,7},{7,6},{8,9},{9,8},{10,11... | collective-permute-start | bytes 49160 | tf_op jit(solution)/shard_map/ppermute | solution.py:581
  98.1 1.3 %collective-permute-done.23.part_3 = f32[2,16,128]{2,1,0:T(8,128)S(1)} collective-permute-done((f32[2,16,128]{2,1,0:T(8,128)S(1)}, f32[2,16,128]{2,1,0:T(8,128)S(1)}, u32[]{:S(2)}, u32[]{:S(2)}) %collective-permute-start.23) | collective-permute-done | bytes 16416 | tf_op jit(solution)/shard_map/ppermute | solution.py:581
  99.4 0.7 collective-permute-done.22.part_2
  100.1 0.0 collective-permute-done.21.part_1
  100.1 1.3 %pick.1 = (f32[16,128]{1,0:T(8,128)}, f32[16,128]{1,0:T(8,128)}) custom-call(s32[64]{0:T(128)S(1)} %copy-done.2, f32[2,16,128]{2,1,0:T(8,128)S(1)} %pad_maximum_fusion.1.part_0, f32[2,16,128]{2,1,0:T(8,128)S(1)} %collective-permute-done.21.part_1, f32[2,16,128]{2,1,0:T(8,128)S(1)} %collective-permute-done.22.part_2, ...), custom_call_target="tpu_custom_call" | custom-call | tf_op jit(solution)/shard_map/pick/pallas_call | solution.py:582
  (8 shorter events, 0.0 us)
Async XLA Ops:
  0.6 6.2 %copy-start.4 = (s32[1,16]{1,0:T(1,128)S(1)}, s32[1,16]{1,0:T(1,128)}, u32[]{:S(2)}) copy-start(s32[1,16]{1,0:T(1,128)} %param.8) | copy-start | bytes 196
  0.6 6.3 %copy-start.3 = (s32[1,16,24]{2,1,0:T(8,128)S(1)}, s32[1,16,24]{2,1,0:T(8,128)}, u32[]{:S(2)}) copy-start(s32[1,16,24]{2,1,0:T(8,128)} %param.7) | copy-start | bytes 4612
  0.7 6.6 %copy-start = (bf16[1,2048,512]{2,1,0:T(8,128)(2,1)S(1)}, bf16[1,2048,512]{2,1,0:T(8,128)(2,1)}, u32[]{:S(2)}) copy-start(bf16[1,2048,512]{2,1,0:T(8,128)(2,1)} %param.6) | copy-start | bytes 6291460
  0.7 66.1 %collective-permute-start.7 = (bf16[2048,512]{1,0:T(8,128)(2,1)}, bf16[2048,512]{1,0:T(8,128)(2,1)}, u32[]{:S(2)}, u32[]{:S(2)}) collective-permute-start(bf16[2048,512]{1,0:T(8,128)(2,1)} %bitcast.9), channel_id=1, source_target_pairs={{0,1},{1,0},{2,3},{3,2},{4,5},{5,4},{6,7},{7,6},{8,9},{9,8},{10,11... | collective-permute-start | bytes 6291464 | tf_op jit(solution)/shard_map/ppermute | solution.py:489
  4.1 4.3 %copy-start.1 = (bf16[512,512]{1,0:T(8,128)(2,1)S(1)}, bf16[512,512]{1,0:T(8,128)(2,1)}, u32[]{:S(2)}) copy-start(bf16[512,512]{1,0:T(8,128)(2,1)} %get-tuple-element.7.own_frames.refs_0_) | copy-start | bytes 1572868
  4.1 18.5 %collective-permute-start.10 = (bf16[640,512]{1,0:T(8,128)(2,1)}, bf16[640,512]{1,0:T(8,128)(2,1)}, u32[]{:S(2)}, u32[]{:S(2)}) collective-permute-start(bf16[640,512]{1,0:T(8,128)(2,1)} %get-tuple-element.8), channel_id=1, source_target_pairs={{0,2},{1,3},{2,0},{3,1},{4,6},{5,7},{6,4},{7,5},{8,10},{9,11},{10,... | collective-permute-start | bytes 1966088 | tf_op jit(solution)/shard_map/ppermute | solution.py:486
  6.7 51.7 %collective-permute-start.11 = (bf16[768,512]{1,0:T(8,128)(2,1)}, bf16[768,512]{1,0:T(8,128)(2,1)}, u32[]{:S(2)}, u32[]{:S(2)}) collective-permute-start(bf16[768,512]{1,0:T(8,128)(2,1)} %get-tuple-element.9), channel_id=1, source_target_pairs={{0,2},{1,3},{2,0},{3,1},{4,6},{5,7},{6,4},{7,5},{8,10},{9,11},{10,... | collective-permute-start | bytes 2359304 | tf_op jit(solution)/shard_map/ppermute | solution.py:487
  7.1 1.2 %collective-permute-start = (s32[16,128]{1,0:T(8,128)S(1)}, s32[16,128]{1,0:T(8,128)S(1)}, u32[]{:S(2)}, u32[]{:S(2)}) collective-permute-start(s32[16,128]{1,0:T(8,128)S(1)} %split.1.own_ref), channel_id=1, source_target_pairs={{0,1},{1,0},{2,3},{3,2},{4,5},{5,4},{6,7},{7,6},{8,9},{9,8},{10,11... | collective-permute-start | bytes 24584 | tf_op jit(solution)/shard_map/ppermute | solution.py:503
  7.8 16.9 %collective-permute-start.5 = (f32[16,128]{1,0:T(8,128)S(1)}, f32[16,128]{1,0:T(8,128)S(1)}, u32[]{:S(2)}, u32[]{:S(2)}) collective-permute-start(f32[16,128]{1,0:T(8,128)S(1)} %medoid_norms.1.norms_own), channel_id=1, source_target_pairs={{0,1},{1,0},{2,3},{3,2},{4,5},{5,4},{6,7},{7,6},{8,9},{9,8},{10,11... | collective-permute-start | bytes 24584 | tf_op jit(solution)/shard_map/ppermute | solution.py:522
  8.4 50.1 %collective-permute-start.9 = (bf16[512,512]{1,0:T(8,128)(2,1)S(1)}, bf16[512,512]{1,0:T(8,128)(2,1)S(1)}, u32[]{:S(2)}, u32[]{:S(2)}) collective-permute-start(bf16[512,512]{1,0:T(8,128)(2,1)S(1)} %copy-done.1), channel_id=1, source_target_pairs={{0,8},{4,12},{8,0},{12,4},{1,9},{5,13},{9,1},{13,5},{2,10},{6,14},... | collective-permute-start | bytes 1572872 | tf_op jit(solution)/shard_map/ppermute | solution.py:481
  22.6 36.3 %collective-permute-start.12 = (bf16[640,512]{1,0:T(8,128)(2,1)}, bf16[640,512]{1,0:T(8,128)(2,1)S(1)}, u32[]{:S(2)}, u32[]{:S(2)}) collective-permute-start(bf16[640,512]{1,0:T(8,128)(2,1)} %collective-permute-done.10.far_a), channel_id=1, source_target_pairs={{0,16},{16,0},{1,17},{17,1},{2,18},{18,2},{3,19},{19,3},{4,20},{20... | collective-permute-start | bytes 1966088 | tf_op jit(solution)/shard_map/ppermute | solution.py:488
  24.7 14.7 %collective-permute-start.1 = (s32[2,16,128]{2,1,0:T(8,128)S(1)}, s32[2,16,128]{2,1,0:T(8,128)S(1)}, u32[]{:S(2)}, u32[]{:S(2)}) collective-permute-start(s32[2,16,128]{2,1,0:T(8,128)S(1)} %pad_add_fusion), channel_id=1, source_target_pairs={{0,2},{1,3},{2,0},{3,1},{4,6},{5,7},{6,4},{7,5},{8,10},{9,11},{10,... | collective-permute-start | bytes 49160 | tf_op jit(solution)/shard_map/ppermute | solution.py:504
  39.4 3.7 %collective-permute-start.6 = (f32[2,16,128]{2,1,0:T(8,128)S(1)}, f32[2,16,128]{2,1,0:T(8,128)S(1)}, u32[]{:S(2)}, u32[]{:S(2)}) collective-permute-start(f32[2,16,128]{2,1,0:T(8,128)S(1)} %pad_maximum_fusion), channel_id=1, source_target_pairs={{0,2},{1,3},{2,0},{3,1},{4,6},{5,7},{6,4},{7,5},{8,10},{9,11},{10,... | collective-permute-start | bytes 49160 | tf_op jit(solution)/shard_map/ppermute | solution.py:523
  43.1 5.5 %collective-permute-start.4 = (s32[16,128]{1,0:T(8,128)S(1)}, s32[16,128]{1,0:T(8,128)S(1)}, u32[]{:S(2)}, u32[]{:S(2)}) collective-permute-start(s32[16,128]{1,0:T(8,128)S(1)} %route.1.lists_0), channel_id=1, source_target_pairs={{0,12},{4,8},{8,4},{12,0},{1,13},{5,9},{9,5},{13,1},{2,14},{6,10},... | collective-permute-start | bytes 24584 | tf_op jit(solution)/shard_map/ppermute | solution.py:513
  48.6 4.5 %collective-permute-start.3 = (s32[16,128]{1,0:T(8,128)S(1)}, s32[16,128]{1,0:T(8,128)S(1)}, u32[]{:S(2)}, u32[]{:S(2)}) collective-permute-start(s32[16,128]{1,0:T(8,128)S(1)} %route.1.lists_0), channel_id=1, source_target_pairs={{0,8},{4,12},{8,0},{12,4},{1,9},{5,13},{9,1},{13,5},{2,10},{6,14},... | collective-permute-start | bytes 24584 | tf_op jit(solution)/shard_map/ppermute | solution.py:513
  53.2 3.7 %collective-permute-start.2 = (s32[16,128]{1,0:T(8,128)S(1)}, s32[16,128]{1,0:T(8,128)S(1)}, u32[]{:S(2)}, u32[]{:S(2)}) collective-permute-start(s32[16,128]{1,0:T(8,128)S(1)} %route.1.lists_0), channel_id=1, source_target_pairs={{0,4},{4,0},{8,12},{12,8},{1,5},{5,1},{9,13},{13,9},{2,6},{6,2},{1... | collective-permute-start | bytes 24584 | tf_op jit(solution)/shard_map/ppermute | solution.py:513
  56.9 9.2 %collective-permute-start.8 = (bf16[512,512]{1,0:T(8,128)(2,1)S(1)}, bf16[512,512]{1,0:T(8,128)(2,1)S(1)}, u32[]{:S(2)}, u32[]{:S(2)}) collective-permute-start(bf16[512,512]{1,0:T(8,128)(2,1)S(1)} %copy-done.1), channel_id=1, source_target_pairs={{0,4},{4,0},{8,12},{12,8},{1,5},{5,1},{9,13},{13,9},{2,6},{6,2},{1... | collective-permute-start | bytes 1572872 | tf_op jit(solution)/shard_map/ppermute | solution.py:482
  58.4 21.4 %collective-permute-start.14 = (bf16[768,512]{1,0:T(8,128)(2,1)}, bf16[768,512]{1,0:T(8,128)(2,1)S(1)}, u32[]{:S(2)}, u32[]{:S(2)}) collective-permute-start(bf16[768,512]{1,0:T(8,128)(2,1)} %collective-permute-done.11.far_b), channel_id=1, source_target_pairs={{0,1},{1,0},{2,3},{3,2},{4,5},{5,4},{6,7},{7,6},{8,9},{9,8},{10,11... | collective-permute-start | bytes 2359304 | tf_op jit(solution)/shard_map/ppermute | solution.py:491
  58.5 21.4 %collective-permute-start.13 = (bf16[640,512]{1,0:T(8,128)(2,1)}, bf16[640,512]{1,0:T(8,128)(2,1)S(1)}, u32[]{:S(2)}, u32[]{:S(2)}) collective-permute-start(bf16[640,512]{1,0:T(8,128)(2,1)} %collective-permute-done.10.far_a), channel_id=1, source_target_pairs={{0,1},{1,0},{2,3},{3,2},{4,5},{5,4},{6,7},{7,6},{8,9},{9,8},{10,11... | collective-permute-start | bytes 1966088 | tf_op jit(solution)/shard_map/ppermute | solution.py:490
  59.0 20.9 %collective-permute-start.15 = (bf16[640,512]{1,0:T(8,128)(2,1)S(1)}, bf16[640,512]{1,0:T(8,128)(2,1)S(1)}, u32[]{:S(2)}, u32[]{:S(2)}) collective-permute-start(bf16[640,512]{1,0:T(8,128)(2,1)S(1)} %collective-permute-done.12.far_c), channel_id=1, source_target_pairs={{0,1},{1,0},{2,3},{3,2},{4,5},{5,4},{6,7},{7,6},{8,9},{9,8},{10,11... | collective-permute-start | bytes 1966088 | tf_op jit(solution)/shard_map/ppermute | solution.py:492
  66.1 9.3 %collective-permute-start.16 = (bf16[512,512]{1,0:T(8,128)(2,1)S(1)}, bf16[512,512]{1,0:T(8,128)(2,1)S(1)}, u32[]{:S(2)}, u32[]{:S(2)}) collective-permute-start(bf16[512,512]{1,0:T(8,128)(2,1)S(1)} %copy-done.1), channel_id=1, source_target_pairs={{4,8},{8,4},{5,9},{9,5},{6,10},{10,6},{7,11},{11,7},{20,24},{24,20... | collective-permute-start | bytes 1572872 | tf_op jit(solution)/shard_map/ppermute | solution.py:483
  66.8 13.1 %collective-permute-start.17 = (bf16[512,512]{1,0:T(8,128)(2,1)S(1)}, bf16[512,512]{1,0:T(8,128)(2,1)S(1)}, u32[]{:S(2)}, u32[]{:S(2)}) collective-permute-start(bf16[512,512]{1,0:T(8,128)(2,1)S(1)} %collective-permute-done.9.frames_2.refs_2_), channel_id=1, source_target_pairs={{8,12},{4,0},{9,13},{5,1},{10,14},{6,2},{11,15},{7,3},{24,28},{20,... | collective-permute-start | bytes 1572872 | tf_op jit(solution)/shard_map/ppermute | solution.py:484
  75.4 24.7 %copy-start.2 = (s32[64]{0:T(128)S(1)}, s32[64]{0:T(128)}, u32[]{:S(2)}) copy-start(s32[64]{0:T(128)} %plan_ref.1) | copy-start | bytes 772
  86.7 6.5 %collective-permute-start.20 = (f32[2,16,128]{2,1,0:T(8,128)S(1)}, f32[2,16,128]{2,1,0:T(8,128)S(1)}, u32[]{:S(2)}, u32[]{:S(2)}) collective-permute-start(f32[2,16,128]{2,1,0:T(8,128)S(1)} %far_search.1), channel_id=1, source_target_pairs={{0,12},{4,8},{8,4},{12,0},{1,13},{5,9},{9,5},{13,1},{2,14},{6,10},... | collective-permute-start | bytes 49160 | tf_op jit(solution)/shard_map/ppermute | solution.py:578
  91.5 4.6 %collective-permute-start.19 = (f32[2,16,128]{2,1,0:T(8,128)S(1)}, f32[2,16,128]{2,1,0:T(8,128)S(1)}, u32[]{:S(2)}, u32[]{:S(2)}) collective-permute-start(f32[2,16,128]{2,1,0:T(8,128)S(1)} %far_search.1), channel_id=1, source_target_pairs={{0,8},{4,12},{8,0},{12,4},{1,9},{5,13},{9,1},{13,5},{2,10},{6,14},... | collective-permute-start | bytes 49160 | tf_op jit(solution)/shard_map/ppermute | solution.py:578
  91.5 4.6 %collective-permute-start.18 = (f32[2,16,128]{2,1,0:T(8,128)S(1)}, f32[2,16,128]{2,1,0:T(8,128)S(1)}, u32[]{:S(2)}, u32[]{:S(2)}) collective-permute-start(f32[2,16,128]{2,1,0:T(8,128)S(1)} %far_search.1), channel_id=1, source_target_pairs={{0,4},{4,0},{8,12},{12,8},{1,5},{5,1},{9,13},{13,9},{2,6},{6,2},{1... | collective-permute-start | bytes 49160 | tf_op jit(solution)/shard_map/ppermute | solution.py:578
  96.2 3.2 %collective-permute-start.23 = (f32[2,16,128]{2,1,0:T(8,128)S(1)}, f32[2,16,128]{2,1,0:T(8,128)S(1)}, u32[]{:S(2)}, u32[]{:S(2)}) collective-permute-start(f32[2,16,128]{2,1,0:T(8,128)S(1)} %pad_maximum_fusion.1.part_0), channel_id=1, source_target_pairs={{0,3},{1,2},{2,1},{3,0},{4,7},{5,6},{6,5},{7,4},{8,11},{9,10},{10,... | collective-permute-start | bytes 49160 | tf_op jit(solution)/shard_map/ppermute | solution.py:581
  96.3 3.8 %collective-permute-start.22 = (f32[2,16,128]{2,1,0:T(8,128)S(1)}, f32[2,16,128]{2,1,0:T(8,128)S(1)}, u32[]{:S(2)}, u32[]{:S(2)}) collective-permute-start(f32[2,16,128]{2,1,0:T(8,128)S(1)} %pad_maximum_fusion.1.part_0), channel_id=1, source_target_pairs={{0,2},{1,3},{2,0},{3,1},{4,6},{5,7},{6,4},{7,5},{8,10},{9,11},{10,... | collective-permute-start | bytes 49160 | tf_op jit(solution)/shard_map/ppermute | solution.py:581
  96.5 3.6 %collective-permute-start.21 = (f32[2,16,128]{2,1,0:T(8,128)S(1)}, f32[2,16,128]{2,1,0:T(8,128)S(1)}, u32[]{:S(2)}, u32[]{:S(2)}) collective-permute-start(f32[2,16,128]{2,1,0:T(8,128)S(1)} %pad_maximum_fusion.1.part_0), channel_id=1, source_target_pairs={{0,1},{1,0},{2,3},{3,2},{4,5},{5,4},{6,7},{7,6},{8,9},{9,8},{10,11... | collective-permute-start | bytes 49160 | tf_op jit(solution)/shard_map/ppermute | solution.py:581

commit v3 on v2

--- a/solution.py
+++ b/solution.py
@@ -17,7 +17,7 @@
 together = 6
 small_vmem = 8 << 20
 large_vmem = 24 << 20
-whole_vmem = 61 << 20
+whole_vmem = 125 << 19
 
 
 def fold_two(left_one, left_two, right_one, right_two):
@@ -143,22 +143,25 @@
     return one[0:1], two[0:1]
 
 
-def cut_kernel(frames_ref, group_ref, mine_ref, edge_ref, middle_ref, sems):
-    quarter = mine_ref.shape[0]
-    side = edge_ref.shape[0]
-    piece = pl.multiple_of(lax.axis_index("medoids") * quarter, TILE)
+def cut_first_kernel(frames_ref, group_ref, mine_ref, edge_ref, sems):
+    quarter, side = mine_ref.shape[0], edge_ref.shape[0]
+    start = pl.multiple_of(lax.axis_index("medoids") * quarter, TILE)
     end = pl.multiple_of(lax.axis_index("slab") * (group_ref.shape[0] - side), TILE)
-    copies = (
-        pltpu.make_async_copy(frames_ref.at[pl.ds(piece, quarter)], mine_ref, sems.at[0]),
-        pltpu.make_async_copy(group_ref.at[pl.ds(end, side)], edge_ref, sems.at[1]),
-        pltpu.make_async_copy(
-            group_ref.at[pl.ds(side, middle_ref.shape[0])], middle_ref, sems.at[2]
+    copies = start_all(
+        (
+            (frames_ref.at[pl.ds(start, quarter)], mine_ref),
+            (group_ref.at[pl.ds(end, side)], edge_ref),
         ),
-    )
-    for copy in copies:
-        copy.start()
+        sems,
+    )
     for copy in copies:
         copy.wait()
+
+
+def cut_middle_kernel(side, group_ref, middle_ref, sem):
+    copy = pltpu.make_async_copy(group_ref.at[pl.ds(side, middle_ref.shape[0])], middle_ref, sem)
+    copy.start()
+    copy.wait()
 
 
 def split_kernel(members, tiles_here, ids_ref, lists_ref):
@@ -182,13 +185,22 @@
     lists_ref[...] = jnp.where(within == lanes - 1, taken, lists)
 
 
-def route_kernel(own_ref, near_ref, far_ref, out_ref):
+def route_kernel(own_ref, near_ref, out_ref):
     quarter_tiles = out_ref.shape[0] // 4
-    start = lax.axis_index("medoids") * quarter_tiles
-    for slot, ref in enumerate((own_ref, near_ref, far_ref.at[0], far_ref.at[1])):
-        for tile in range(quarter_tiles):
-            row = slot * quarter_tiles + tile
-            out_ref[row : row + 1, :] = ref[pl.ds(start + tile, 1), :]
+    piece = lax.axis_index("medoids")
+    row = 0
+    for at in (piece, jnp.bitwise_xor(piece, 2)):
+        for ref in (own_ref, near_ref):
+            for tile in range(quarter_tiles):
+                out_ref[row : row + 1, :] = ref[pl.ds(at * quarter_tiles + tile, 1), :]
+                row += 1
+
+
+def stack_kernel(*refs):
+    out_ref = refs[-1]
+    rows = out_ref.shape[1]
+    for index, ref in enumerate(refs[:-1]):
+        out_ref[index] = ref[rows:, :]
 
 
 def norms_kernel(scale, *refs):
@@ -202,15 +214,12 @@
 
 
 def search(
-    tiles, slots, first_tile, quarter_tiles, tiles_here, lists_ref, rows_ref, norms_ref,
+    tiles, slots, first_tile, quarter_tiles, tiles_here, lists, rows_ref, norms_ref,
     frames_ref, one_ref, two_ref, table_ref,
 ):
-    lanes = lists_ref.shape[2] // lists_ref.shape[0]
+    lanes, listed = lists
     dummy = len(slots) * tiles_here
     shift = 16
-
-    def listed(zslot, slot, tile, place):
-        return lists_ref[zslot, slot * quarter_tiles + tile, zslot * lanes + place]
 
     def place_of(index):
         zslot = index // quarter_tiles
@@ -285,47 +294,101 @@
     lax.fori_loop(0, (written + together - 1) // together, step, 0)
 
 
-def near_kernel(
-    lists_0, lists_1, lists_2, lists_3, norms_own, norms_near, own_group, near_group,
-    own_frames, frames_1, frames_2,
-    out_ref, lists_ref, rows_buf, frames_buf, norms_buf, one_buf, two_buf, table_ref, sems,
+def lists_by_distance(lists_ref, quarter_tiles):
+    lanes = lists_ref.shape[2] // lists_ref.shape[0]
+
+    def listed(zslot, slot, tile, place):
+        return lists_ref[zslot, slot * quarter_tiles + tile, zslot * lanes + place]
+
+    return lanes, listed
+
+
+def store_rows(tiles, out_ref, one_buf, two_buf):
+    for index in range(tiles):
+        rows = pl.ds(index * TILE, TILE)
+        one, two = row_pair(one_buf[rows, :], two_buf[rows, :])
+        out_ref[0, index : index + 1, :] = one
+        out_ref[1, index : index + 1, :] = two
+
+
+def start_all(pairs, sems):
+    copies = [
+        pltpu.make_async_copy(source, target, sems.at[index])
+        for index, (source, target) in enumerate(pairs)
+    ]
+    for copy in copies:
+        copy.start()
+    return copies
+
+
+def own_kernel(
+    members, own_listed, near_listed, norms_own, norms_near, own_group, near_group, own_frames,
+    out_ref, lists_ref, rows_buf, norms_buf, one_buf, two_buf, table_ref, sems,
 ):
     tile_rows = own_group.shape[0]
     tiles_here = tile_rows // TILE
-    quarter = own_frames.shape[0]
-    quarter_tiles = quarter // TILE
-    copies = [
-        pltpu.make_async_copy(own_group, rows_buf.at[pl.ds(0, tile_rows)], sems.at[0]),
-        pltpu.make_async_copy(near_group, rows_buf.at[pl.ds(tile_rows, tile_rows)], sems.at[1]),
-    ]
-    for index, ref in enumerate((own_frames, frames_1, frames_2)):
-        copies.append(
-            pltpu.make_async_copy(
-                ref, frames_buf.at[pl.ds(index * quarter, quarter)], sems.at[2 + index]
-            )
-        )
-    for index, ref in enumerate((lists_0, lists_1, lists_2, lists_3)):
-        copies.append(pltpu.make_async_copy(ref, lists_ref.at[index], sems.at[5 + index]))
-    for copy in copies:
-        copy.start()
+    quarter_tiles = own_frames.shape[0] // TILE
+    first = lax.axis_index("medoids") * quarter_tiles
+    copies = start_all(
+        (
+            (own_group, rows_buf.at[pl.ds(0, tile_rows)]),
+            (near_group, rows_buf.at[pl.ds(tile_rows, tile_rows)]),
+            (own_listed, lists_ref.at[0]),
+            (near_listed, lists_ref.at[1]),
+        ),
+        sems,
+    )
     norms_buf[pl.ds(0, tiles_here), :] = norms_own[...]
     norms_buf[pl.ds(tiles_here, tiles_here), :] = norms_near[...]
     norms_buf[pl.ds(2 * tiles_here, 1), :] = jnp.full((1, TILE), big_value, jnp.float32)
     for copy in copies:
         copy.wait()
-    tiles = 3 * quarter_tiles
+
+    def listed(zslot, slot, tile, place):
+        return lists_ref[slot, first + tile, place]
+
     search(
-        tiles, (0, 1), 0, quarter_tiles, tiles_here, lists_ref, rows_buf, norms_buf,
+        quarter_tiles, (0, 1), 0, quarter_tiles, tiles_here, (TILE // members, listed), rows_buf,
+        norms_buf, own_frames, one_buf, two_buf, table_ref,
+    )
+    store_rows(quarter_tiles, out_ref, one_buf, two_buf)
+
+
+def near_kernel(
+    lists_1, lists_2, norms_own, norms_near, own_group, near_group,
+    frames_1, frames_2,
+    out_ref, lists_ref, rows_buf, frames_buf, norms_buf, one_buf, two_buf, table_ref, sems,
+):
+    tile_rows = own_group.shape[0]
+    tiles_here = tile_rows // TILE
+    quarter = frames_1.shape[0]
+    quarter_tiles = quarter // TILE
+    copies = start_all(
+        (
+            (own_group, rows_buf.at[pl.ds(0, tile_rows)]),
+            (near_group, rows_buf.at[pl.ds(tile_rows, tile_rows)]),
+            (frames_1, frames_buf.at[pl.ds(quarter, quarter)]),
+            (frames_2, frames_buf.at[pl.ds(2 * quarter, quarter)]),
+            (lists_1.at[pl.ds(0, 2 * quarter_tiles)], lists_ref.at[1]),
+            (lists_2.at[pl.ds(0, 2 * quarter_tiles)], lists_ref.at[2]),
+        ),
+        sems,
+    )
+    norms_buf[pl.ds(0, tiles_here), :] = norms_own[...]
+    norms_buf[pl.ds(tiles_here, tiles_here), :] = norms_near[...]
+    norms_buf[pl.ds(2 * tiles_here, 1), :] = jnp.full((1, TILE), big_value, jnp.float32)
+    for copy in copies:
+        copy.wait()
+    search(
+        2 * quarter_tiles, (0, 1), quarter_tiles, quarter_tiles, tiles_here,
+        lists_by_distance(lists_ref, quarter_tiles), rows_buf, norms_buf,
         frames_buf, one_buf, two_buf, table_ref,
     )
-    for index in range(tiles):
-        one, two = row_pair(one_buf[pl.ds(index * TILE, TILE), :], two_buf[pl.ds(index * TILE, TILE), :])
-        out_ref[0, index : index + 1, :] = one
-        out_ref[1, index : index + 1, :] = two
+    store_rows(2 * quarter_tiles, out_ref, one_buf, two_buf)
 
 
 def far_kernel(
-    lists_0, lists_1, lists_2, lists_3, norms_own, norms_near, norms_far, before_ref, frame_norms,
+    near_lists, far_lists, norms_own, norms_near, norms_far, before_own, before_near, frame_norms,
     own_group, near_group, far_a, far_b, far_c, last_a, last_b, last_c,
     own_frames, frames_1, frames_2, frames_3a, frames_3b,
     out_ref, lists_ref, rows_buf, frames_buf, norms_buf, one_buf, two_buf, table_ref, sems,
@@ -363,8 +426,14 @@
     bring(own_frames, frames_buf, 0, quarter)
     bring(frames_1, frames_buf, quarter, quarter)
     bring(frames_2, frames_buf, 2 * quarter, quarter)
-    for index, ref in enumerate((lists_0, lists_1, lists_2, lists_3)):
-        copies.append(pltpu.make_async_copy(ref, lists_ref.at[index], sems.at[len(copies)]))
+    pair_rows = 2 * quarter_tiles
+    for index in range(members):
+        target = lists_ref.at[index, pl.ds(pair_rows, pair_rows)]
+        copies.append(pltpu.make_async_copy(far_lists.at[index], target, sems.at[len(copies)]))
+    target = lists_ref.at[members - 1, pl.ds(0, pair_rows)]
+    copies.append(
+        pltpu.make_async_copy(near_lists.at[pl.ds(0, pair_rows)], target, sems.at[len(copies)])
+    )
     early = len(copies)
     bring(own_group, rows_buf, 0, tile_rows)
     bring(near_group, rows_buf, tile_rows, tile_rows)
@@ -403,22 +472,26 @@
         out_ref[1, pl.ds(row, 1), :] = (frame_norm + 2.0 * two) / width
 
     early_tiles = 3 * quarter_tiles
+    lists = lists_by_distance(lists_ref, quarter_tiles)
     search(
-        early_tiles, (2, 3), 0, quarter_tiles, tiles_here, lists_ref,
+        early_tiles, (2, 3), 0, quarter_tiles, tiles_here, lists,
         rows_buf.at[pl.ds(2 * tile_rows, 2 * tile_rows)],
         norms_buf.at[pl.ds(2 * tiles_here, 2 * tiles_here + 8)],
         frames_buf, one_buf, two_buf, table_ref,
     )
     for index in range(early_tiles):
+        before, at = before_own, index
+        if index >= quarter_tiles:
+            before, at = before_near, index - quarter_tiles
         finish(
-            index, index, before_ref[0, index : index + 1, :], before_ref[1, index : index + 1, :],
+            index, index, before[0, at : at + 1, :], before[1, at : at + 1, :],
             frame_norms[index : index + 1, :],
         )
     pltpu.make_async_copy(frames_3a, last_target, last_sem).wait()
     for copy in copies[early:]:
         copy.wait()
     search(
-        quarter_tiles, tuple(range(groups)), early_tiles, quarter_tiles, tiles_here, lists_ref,
+        quarter_tiles, tuple(range(groups)), early_tiles, quarter_tiles, tiles_here, lists,
         rows_buf, norms_buf, frames_buf, one_buf, two_buf, table_ref,
     )
     for tile in range(quarter_tiles):
@@ -465,19 +538,27 @@
     vector = pl.BlockSpec(memory_space=pltpu.VMEM)
     small = pltpu.CompilerParams(vmem_limit_bytes=small_vmem)
     large = pltpu.CompilerParams(vmem_limit_bytes=large_vmem)
-    mine, edge, inside_rows = pl.pallas_call(
-        cut_kernel,
+    mine, edge = pl.pallas_call(
+        cut_first_kernel,
         out_shape=(
             jax.ShapeDtypeStruct((quarter, width), frames.dtype),
             jax.ShapeDtypeStruct((side, width), rows.dtype),
-            jax.ShapeDtypeStruct((tile_rows - 2 * side, width), rows.dtype),
         ),
         in_specs=[hbm, hbm],
-        out_specs=(vector, vector, vector),
-        scratch_shapes=[pltpu.SemaphoreType.DMA((3,))],
+        out_specs=(vector, vector),
+        scratch_shapes=[pltpu.SemaphoreType.DMA((2,))],
         compiler_params=pltpu.CompilerParams(vmem_limit_bytes=whole_vmem),
-        name="cut",
+        name="cut_first",
     )(frames, rows)
+    inside_rows = pl.pallas_call(
+        functools.partial(cut_middle_kernel, side),
+        out_shape=jax.ShapeDtypeStruct((tile_rows - 2 * side, width), rows.dtype),
+        in_specs=[hbm],
+        out_specs=vector,
+        scratch_shapes=[pltpu.SemaphoreType.DMA],
+        compiler_params=small,
+        name="cut_middle",
+    )(rows)
     frames_2 = lax.ppermute(mine, "frames", exchanged(members, 2))
     frames_1 = lax.ppermute(mine, "frames", exchanged(members, 1))
     frames_3a = lax.ppermute(mine, "frames", [(1, 2), (2, 1)])
@@ -501,16 +582,24 @@
         name="split",
     )(jnp.concatenate([tile_ids[0], tile_counts[0][:, None]], axis=1))
     near_listed = lax.ppermute(listed, "medoids", exchanged(groups, 1))
-    far_listed = lax.ppermute(jnp.stack([listed, near_listed]), "medoids", exchanged(groups, 2))
-    lists = pl.pallas_call(
+    routed = pl.pallas_call(
         route_kernel,
-        out_shape=jax.ShapeDtypeStruct((groups * quarter_tiles, TILE), jnp.int32),
-        in_specs=[vector] * 3,
+        out_shape=jax.ShapeDtypeStruct((4 * quarter_tiles, TILE), jnp.int32),
+        in_specs=[vector] * 2,
         out_specs=vector,
         compiler_params=small,
         name="route",
-    )(listed, near_listed, far_listed)
-    lists = [lists] + [lax.ppermute(lists, "frames", exchanged(members, at)) for at in (1, 2, 3)]
+    )(listed, near_listed)
+    near_lists = [lax.ppermute(routed, "frames", exchanged(members, at)) for at in (1, 2, 3)]
+    far_lists = pl.pallas_call(
+        stack_kernel,
+        out_shape=jax.ShapeDtypeStruct((members, 2 * quarter_tiles, TILE), jnp.int32),
+        in_specs=[vector] * 4,
+        out_specs=vector,
+        compiler_params=small,
+        name="stack_far",
+    )(routed, *near_lists)
+    far_lists = lax.ppermute(far_lists, "medoids", exchanged(groups, 2))
     norms = pl.pallas_call(
         functools.partial(norms_kernel, 0.5),
         out_shape=jax.ShapeDtypeStruct((tiles_here, TILE), jnp.float32),
@@ -520,7 +609,8 @@
         name="medoid_norms",
     )(rows)
     norm_near = lax.ppermute(norms, "medoids", exchanged(groups, 1))
-    norm_far = lax.ppermute(jnp.stack([norms, norm_near]), "medoids", exchanged(groups, 2))
+    norm_pair = jnp.stack([norms, norm_near])
+    norm_far = lax.ppermute(norm_pair, "medoids", exchanged(groups, 2))
     frame_norms = pl.pallas_call(
         functools.partial(norms_kernel, 1.0),
         out_shape=jax.ShapeDtypeStruct((3 * quarter_tiles, TILE), jnp.float32),
@@ -533,28 +623,45 @@
     total_tiles = members * quarter_tiles
     early_tiles = 3 * quarter_tiles
     table_size = early_tiles * (groups * tile_ids.shape[2] // unroll + 1) + together
-    before = pl.pallas_call(
+    before_own = pl.pallas_call(
+        functools.partial(own_kernel, members),
+        out_shape=jax.ShapeDtypeStruct((2, quarter_tiles, TILE), jnp.float32),
+        in_specs=[hbm] * 2 + [vector] * 2 + [hbm] * 2 + [vector],
+        out_specs=vector,
+        scratch_shapes=[
+            pltpu.SMEM((2, blocks, TILE), jnp.int32),
+            pltpu.VMEM((2 * tile_rows, width), jnp.bfloat16),
+            pltpu.VMEM((2 * tiles_here + 8, TILE), jnp.float32),
+            pltpu.VMEM((quarter, TILE), jnp.float32),
+            pltpu.VMEM((quarter, TILE), jnp.float32),
+            pltpu.SMEM((table_size,), jnp.int32),
+            pltpu.SemaphoreType.DMA((4,)),
+        ],
+        compiler_params=large,
+        name="own_search",
+    )(listed, near_listed, norms, norm_near, rows, near_group, mine)
+    before_near = pl.pallas_call(
         near_kernel,
-        out_shape=jax.ShapeDtypeStruct((2, early_tiles, TILE), jnp.float32),
-        in_specs=[hbm] * 4 + [vector] * 2 + [hbm] * 5,
+        out_shape=jax.ShapeDtypeStruct((2, 2 * quarter_tiles, TILE), jnp.float32),
+        in_specs=[hbm] * 2 + [vector] * 2 + [hbm] * 4,
         out_specs=vector,
         scratch_shapes=[
-            pltpu.SMEM((members, groups * quarter_tiles, TILE), jnp.int32),
+            pltpu.SMEM((members, 2 * quarter_tiles, TILE), jnp.int32),
             pltpu.VMEM((2 * tile_rows, width), jnp.bfloat16),
             pltpu.VMEM((3 * quarter, width), jnp.bfloat16),
             pltpu.VMEM((2 * tiles_here + 8, TILE), jnp.float32),
-            pltpu.VMEM((3 * quarter, TILE), jnp.float32),
-            pltpu.VMEM((3 * quarter, TILE), jnp.float32),
+            pltpu.VMEM((2 * quarter, TILE), jnp.float32),
+            pltpu.VMEM((2 * quarter, TILE), jnp.float32),
             pltpu.SMEM((table_size,), jnp.int32),
-            pltpu.SemaphoreType.DMA((9,)),
+            pltpu.SemaphoreType.DMA((8,)),
         ],
         compiler_params=large,
         name="near_search",
-    )(*lists, norms, norm_near, rows, near_group, mine, frames_1, frames_2)
+    )(*near_lists[:2], norms, norm_near, rows, near_group, frames_1, frames_2)
     found = pl.pallas_call(
         far_kernel,
         out_shape=jax.ShapeDtypeStruct((2, total_tiles, TILE), jnp.float32),
-        in_specs=[hbm] * 4 + [vector] * 5 + [hbm] * 13,
+        in_specs=[hbm] * 2 + [vector] * 6 + [hbm] * 13,
         out_specs=vector,
         scratch_shapes=[
             pltpu.SMEM((members, groups * quarter_tiles, TILE), jnp.int32),
@@ -569,7 +676,7 @@
         compiler_params=large,
         name="far_search",
     )(
-        *lists, norms, norm_near, norm_far, before, frame_norms, rows, near_group,
+        near_lists[2], far_lists, norms, norm_near, norm_far, before_own, before_near, frame_norms, rows, near_group,
         far_a, far_b, far_c, last_a, last_b, last_c, mine, frames_1, frames_2, frames_3a, frames_3b,
     )
 

time: 102 us -> 110 us (1.078)
  starting transfers between devices: 30.1 us -> 37.9 us
  waiting for transfers between devices: 51.4 us -> 47.9 us
  Pallas kernels: 19 us -> 21.1 us
  local copies, waits for them, and re-layouts: 0.11 us -> 1.7 us
    ppermute x1, starting transfers between devices: 1.53 us -> 11.3 us  [gathered_frames(): frames_1 = lax.ppermute(mine, 'frames', exchanged(members, 1))]
    ppermute x5, waiting for transfers between devices: 22.6 us -> 15 us  [the longest x3 10.5 us: gathered_frames(): lax.ppermute(routed, 'frames', exchanged(members, at))]
    pallas_call x3 -> x6, Pallas kernels: 9.8 us -> 12.1 us  [the longest x1 4.56 us: gathered_frames(): pl.pallas_call(near_kernel, out_shape=jax.ShapeDtypeStruct((2, 2 * quarte...]
    ppermute x1, waiting for transfers between devices: 11.2 us -> 13.2 us  [gathered_frames(): far_a = lax.ppermute(edge, 'medoids', exchanged(groups, 2))]
    unnamed x10 -> x12, local copies, waits for them, and re-layouts: 0.02 us -> 1.61 us
    ppermute x1, waiting for transfers between devices: 7.06 us -> 8.5 us  [gathered_frames(): frames_1 = lax.ppermute(mine, 'frames', exchanged(members, 1))]
  transfers between devices with their start and end apart: 24 -> 24, of which waited for: 13 -> 10; matrix products, arithmetic and copies ran while one was open for 0% -> 0% of each run, Pallas kernels for 11% -> 12%
where the time goes in v3:
time: 110 us
  waiting for transfers between devices  47.9 us (44%)
  starting transfers between devices  37.9 us (34%)
  Pallas kernels  21.1 us (19%)
  local copies, waits for them, and re-layouts  1.7 us (2%)
    ppermute x1, waiting for transfers between devices, gathered_frames(): far_a = lax.ppermute(edge, 'medoids', exchanged(groups, 2))  13.2 us
    ppermute x1, starting transfers between devices, gathered_frames(): frames_1 = lax.ppermute(mine, 'frames', exchanged(members, 1))  11.3 us
    ppermute x3, waiting for transfers between devices, gathered_frames(): lax.ppermute(routed, 'frames', exchanged(members, at))  10.5 us
    ppermute x1, waiting for transfers between devices, gathered_frames(): frames_1 = lax.ppermute(mine, 'frames', exchanged(members, 1))  8.5 us
    ppermute x3, starting transfers between devices, gathered_frames(): lax.ppermute(routed, 'frames', exchanged(members, at))  6.72 us
    pallas_call x1, Pallas kernels, gathered_frames(): pl.pallas_call(far_kernel, out_shape=jax.ShapeDtypeStruct((2, total_tiles...  6.66 us
    ppermute x3, waiting for transfers between devices, gathered_frames(): other = lax.ppermute(found, 'frames', exchanged(members, at))  4.89 us
    pallas_call x1, Pallas kernels, gathered_frames(): pl.pallas_call(near_kernel, out_shape=jax.ShapeDtypeStruct((2, 2 * quarte...  4.56 us
  transfers between devices with their start and end apart: 24, of which 10 were waited for; matrix products, arithmetic and copies ran while one was open for 0% of the time, Pallas kernels for 12%

profile of v3, /device:TPU:0, one launch (start us, length us, event | category | flops | bytes accessed | tf_op | source)
XLA Modules:
  0.0 109.5 jit_solution(17201073797748797644)
XLA Ops:
  0.6 0.6 collective-permute-start.7
  1.2 2.3 %cut_first.1 = (bf16[512,512]{1,0:T(8,128)(2,1)}, bf16[640,512]{1,0:T(8,128)(2,1)}) custom-call(bf16[2048,512]{1,0:T(8,128)(2,1)} %frames_ref.1, bf16[2048,512]{1,0:T(8,128)(2,1)} %bitcast.8), custom_call_target="tpu_custom_call" | custom-call | tf_op jit(solution)/shard_map/cut_first/pallas_call | solution.py:541
  3.5 0.0 copy-start.5
  3.5 2.6 %collective-permute-start.10 = (bf16[640,512]{1,0:T(8,128)(2,1)}, bf16[640,512]{1,0:T(8,128)(2,1)}, u32[]{:S(2)}, u32[]{:S(2)}) collective-permute-start(bf16[640,512]{1,0:T(8,128)(2,1)} %get-tuple-element.7), channel_id=1, source_target_pairs={{0,2},{1,3},{2,0},{3,1},{4,6},{5,7},{6,4},{7,5},{8,10},{9,11},{10,... | collective-permute-start | bytes 1966088 | tf_op jit(solution)/shard_map/ppermute | solution.py:567
  6.1 1.6 %copy-done = bf16[1,2048,512]{2,1,0:T(8,128)(2,1)S(1)} copy-done((bf16[1,2048,512]{2,1,0:T(8,128)(2,1)S(1)}, bf16[1,2048,512]{2,1,0:T(8,128)(2,1)}, u32[]{:S(2)}) %copy-start) | copy-done | bytes 2097176
  7.7 0.9 cut_middle.1
  8.6 0.1 collective-permute-start.11
  8.7 0.1 copy.7
  8.8 13.2 %collective-permute-done.10.far_a = bf16[640,512]{1,0:T(8,128)(2,1)} collective-permute-done((bf16[640,512]{1,0:T(8,128)(2,1)}, bf16[640,512]{1,0:T(8,128)(2,1)}, u32[]{:S(2)}, u32[]{:S(2)}) %collective-permute-start.10) | collective-permute-done | bytes 655392 | tf_op jit(solution)/shard_map/ppermute | solution.py:567
  22.0 2.0 %collective-permute-start.12 = (bf16[640,512]{1,0:T(8,128)(2,1)}, bf16[640,512]{1,0:T(8,128)(2,1)S(1)}, u32[]{:S(2)}, u32[]{:S(2)}) collective-permute-start(bf16[640,512]{1,0:T(8,128)(2,1)} %collective-permute-done.10.far_a), channel_id=1, source_target_pairs={{0,16},{16,0},{1,17},{17,1},{2,18},{18,2},{3,19},{19,3},{4,20},{20... | collective-permute-start | bytes 1966088 | tf_op jit(solution)/shard_map/ppermute | solution.py:569
  24.0 0.1 pad_add_fusion.ids_ref
  24.1 0.2 split.1.own_ref.own_listed
  24.3 0.1 collective-permute-start
  24.3 0.5 medoid_norms.1.norms_own
  24.8 0.6 collective-permute-start.5
  25.4 0.1 collective-permute-done.near_ref.near_listed
  25.5 1.6 %collective-permute-start.2 = (s32[16,128]{1,0:T(8,128)S(1)}, s32[16,128]{1,0:T(8,128)S(1)}, u32[]{:S(2)}, u32[]{:S(2)}) collective-permute-start(s32[16,128]{1,0:T(8,128)S(1)} %route.1.refs_0_), channel_id=1, source_target_pairs={{0,4},{4,0},{8,12},{12,8},{1,5},{5,1},{9,13},{13,9},{2,6},{6,2},{1... | collective-permute-start | bytes 24584 | tf_op jit(solution)/shard_map/ppermute | solution.py:593
  27.1 0.0 collective-permute-done.5.norms_near
  27.1 2.6 %collective-permute-start.3 = (s32[16,128]{1,0:T(8,128)S(1)}, s32[16,128]{1,0:T(8,128)S(1)}, u32[]{:S(2)}, u32[]{:S(2)}) collective-permute-start(s32[16,128]{1,0:T(8,128)S(1)} %route.1.refs_0_), channel_id=1, source_target_pairs={{0,8},{4,12},{8,0},{12,4},{1,9},{5,13},{9,1},{13,5},{2,10},{6,14},... | collective-permute-start | bytes 24584 | tf_op jit(solution)/shard_map/ppermute | solution.py:593
  29.7 0.0 collective-permute-done.2.refs_1_.lists_1
  29.7 0.0 copy-done.2
  29.7 2.1 %collective-permute-start.9 = (bf16[512,512]{1,0:T(8,128)(2,1)S(1)}, bf16[512,512]{1,0:T(8,128)(2,1)S(1)}, u32[]{:S(2)}, u32[]{:S(2)}) collective-permute-start(bf16[512,512]{1,0:T(8,128)(2,1)S(1)} %copy-done.2), channel_id=1, source_target_pairs={{0,8},{4,12},{8,0},{12,4},{1,9},{5,13},{9,1},{13,5},{2,10},{6,14},... | collective-permute-start | bytes 1572872 | tf_op jit(solution)/shard_map/ppermute | solution.py:562
  31.8 0.0 collective-permute-done.3.refs_2_.lists_2
  31.8 2.6 %collective-permute-start.1 = (s32[16,128]{1,0:T(8,128)S(1)}, s32[16,128]{1,0:T(8,128)S(1)}, u32[]{:S(2)}, u32[]{:S(2)}) collective-permute-start(s32[16,128]{1,0:T(8,128)S(1)} %route.1.refs_0_), channel_id=1, source_target_pairs={{0,12},{4,8},{8,4},{12,0},{1,13},{5,9},{9,5},{13,1},{2,14},{6,10},... | collective-permute-start | bytes 24584 | tf_op jit(solution)/shard_map/ppermute | solution.py:593
  34.4 10.5 %collective-permute-done.1.refs_3_.near_lists = s32[16,128]{1,0:T(8,128)S(1)} collective-permute-done((s32[16,128]{1,0:T(8,128)S(1)}, s32[16,128]{1,0:T(8,128)S(1)}, u32[]{:S(2)}, u32[]{:S(2)}) %collective-permute-start.1) | collective-permute-done | bytes 8224 | tf_op jit(solution)/shard_map/ppermute | solution.py:593
  44.9 1.5 %collective-permute-start.6 = (f32[2,16,128]{2,1,0:T(8,128)S(1)}, f32[2,16,128]{2,1,0:T(8,128)S(1)}, u32[]{:S(2)}, u32[]{:S(2)}) collective-permute-start(f32[2,16,128]{2,1,0:T(8,128)S(1)} %pad_maximum_fusion), channel_id=1, source_target_pairs={{0,2},{1,3},{2,0},{3,1},{4,6},{5,7},{6,4},{7,5},{8,10},{9,11},{10,... | collective-permute-start | bytes 49160 | tf_op jit(solution)/shard_map/ppermute | solution.py:613
  46.4 2.2 %collective-permute-done.6.norms_far = f32[2,16,128]{2,1,0:T(8,128)S(1)} collective-permute-done((f32[2,16,128]{2,1,0:T(8,128)S(1)}, f32[2,16,128]{2,1,0:T(8,128)S(1)}, u32[]{:S(2)}, u32[]{:S(2)}) %collective-permute-start.6) | collective-permute-done | bytes 16416 | tf_op jit(solution)/shard_map/ppermute | solution.py:613
  48.6 1.5 %collective-permute-start.4 = (s32[4,8,128]{2,1,0:T(8,128)S(1)}, s32[4,8,128]{2,1,0:T(8,128)S(1)}, u32[]{:S(2)}, u32[]{:S(2)}) collective-permute-start(s32[4,8,128]{2,1,0:T(8,128)S(1)} %stack_far.1), channel_id=1, source_target_pairs={{0,2},{1,3},{2,0},{3,1},{4,6},{5,7},{6,4},{7,5},{8,10},{9,11},{10,... | collective-permute-start | bytes 49160 | tf_op jit(solution)/shard_map/ppermute | solution.py:602
  50.1 2.2 %collective-permute-done.4.far_lists = s32[4,8,128]{2,1,0:T(8,128)S(1)} collective-permute-done((s32[4,8,128]{2,1,0:T(8,128)S(1)}, s32[4,8,128]{2,1,0:T(8,128)S(1)}, u32[]{:S(2)}, u32[]{:S(2)}) %collective-permute-start.4) | collective-permute-done | bytes 16416 | tf_op jit(solution)/shard_map/ppermute | solution.py:602
  52.4 11.3 %collective-permute-start.8 = (bf16[512,512]{1,0:T(8,128)(2,1)S(1)}, bf16[512,512]{1,0:T(8,128)(2,1)S(1)}, u32[]{:S(2)}, u32[]{:S(2)}) collective-permute-start(bf16[512,512]{1,0:T(8,128)(2,1)S(1)} %copy-done.2), channel_id=1, source_target_pairs={{0,4},{4,0},{8,12},{12,8},{1,5},{5,1},{9,13},{13,9},{2,6},{6,2},{1... | collective-permute-start | bytes 1572872 | tf_op jit(solution)/shard_map/ppermute | solution.py:563
  63.6 0.0 collective-permute-done.11.far_b
  63.6 0.0 collective-permute-start.14
  63.6 0.0 collective-permute-done.9.frames_2.refs_2_
  63.7 0.5 collective-permute-start.13
  64.2 0.0 collective-permute-done.12.far_c
  64.2 0.1 collective-permute-start.15
  64.2 8.5 %collective-permute-done.8.frames_1.refs_1_ = bf16[512,512]{1,0:T(8,128)(2,1)S(1)} collective-permute-done((bf16[512,512]{1,0:T(8,128)(2,1)S(1)}, bf16[512,512]{1,0:T(8,128)(2,1)S(1)}, u32[]{:S(2)}, u32[]{:S(2)}) %collective-permute-start.8) | collective-permute-done | bytes 524320 | tf_op jit(solution)/shard_map/ppermute | solution.py:563
  72.7 0.7 collective-permute-start.16
  73.4 0.0 collective-permute-done.7.near_group
  73.4 1.3 %collective-permute-start.17 = (bf16[512,512]{1,0:T(8,128)(2,1)S(1)}, bf16[512,512]{1,0:T(8,128)(2,1)S(1)}, u32[]{:S(2)}, u32[]{:S(2)}) collective-permute-start(bf16[512,512]{1,0:T(8,128)(2,1)S(1)} %collective-permute-done.9.frames_2.refs_2_), channel_id=1, source_target_pairs={{8,12},{4,0},{9,13},{5,1},{10,14},{6,2},{11,15},{7,3},{24,28},{20,... | collective-permute-start | bytes 1572872 | tf_op jit(solution)/shard_map/ppermute | solution.py:565
  74.7 0.4 frame_norms.1
  75.1 4.6 %near_search.1.before_near = f32[2,8,128]{2,1,0:T(8,128)S(1)} custom-call(s32[16,128]{1,0:T(8,128)S(1)} %collective-permute-done.2.refs_1_.lists_1, s32[16,128]{1,0:T(8,128)S(1)} %collective-permute-done.3.refs_2_.lists_2, f32[16,128]{1,0:T(8,128)S(1)} %medoid_norms.1.norms_own, f32[16,128]{1,0:T(8,128)S(1)} %collective-permute-done.5.norms_near, ...), custom_call_target="tpu_custom_call" | custom-call | tf_op jit(solution)/shard_map/near_search/pallas_call | solution.py:643
  79.7 4.3 %own_search.1.before_own = f32[2,4,128]{2,1,0:T(4,128)S(1)} custom-call(s32[16,128]{1,0:T(8,128)S(1)} %split.1.own_ref.own_listed, s32[16,128]{1,0:T(8,128)S(1)} %collective-permute-done.near_ref.near_listed, f32[16,128]{1,0:T(8,128)S(1)} %medoid_norms.1.norms_own, f32[16,128]{1,0:T(8,128)S(1)} %collective-permute-done.5.norms_near, ...), custom_call_target="tpu_custom_call" | custom-call | tf_op jit(solution)/shard_map/own_search/pallas_call | solution.py:626
  84.0 0.0 copy-start.3
  84.0 0.0 collective-permute-done.16.frames_3a
  84.0 4.2 %collective-permute-done.17.frames_3b = bf16[512,512]{1,0:T(8,128)(2,1)S(1)} collective-permute-done((bf16[512,512]{1,0:T(8,128)(2,1)S(1)}, bf16[512,512]{1,0:T(8,128)(2,1)S(1)}, u32[]{:S(2)}, u32[]{:S(2)}) %collective-permute-start.17) | collective-permute-done | bytes 524320 | tf_op jit(solution)/shard_map/ppermute | solution.py:565
  88.2 0.0 collective-permute-done.13.last_a
  88.2 0.0 collective-permute-done.14.last_b
  88.2 0.0 collective-permute-done.15.last_c
  88.2 6.7 %far_search.1 = f32[2,16,128]{2,1,0:T(8,128)S(1)} custom-call(s32[16,128]{1,0:T(8,128)S(1)} %collective-permute-done.1.refs_3_.near_lists, s32[4,8,128]{2,1,0:T(8,128)S(1)} %collective-permute-done.4.far_lists, f32[16,128]{1,0:T(8,128)S(1)} %medoid_norms.1.norms_own, f32[16,128]{1,0:T(8,128)S(1)} %collective-permute-done.5.norms_near, ...), custom_call_target="tpu_custom_call" | custom-call | tf_op jit(solution)/shard_map/far_search/pallas_call | solution.py:661
  94.9 1.6 %collective-permute-start.18 = (f32[2,16,128]{2,1,0:T(8,128)S(1)}, f32[2,16,128]{2,1,0:T(8,128)S(1)}, u32[]{:S(2)}, u32[]{:S(2)}) collective-permute-start(f32[2,16,128]{2,1,0:T(8,128)S(1)} %far_search.1), channel_id=1, source_target_pairs={{0,4},{4,0},{8,12},{12,8},{1,5},{5,1},{9,13},{13,9},{2,6},{6,2},{1... | collective-permute-start | bytes 49160 | tf_op jit(solution)/shard_map/ppermute | solution.py:685
  96.5 2.2 %collective-permute-start.19 = (f32[2,16,128]{2,1,0:T(8,128)S(1)}, f32[2,16,128]{2,1,0:T(8,128)S(1)}, u32[]{:S(2)}, u32[]{:S(2)}) collective-permute-start(f32[2,16,128]{2,1,0:T(8,128)S(1)} %far_search.1), channel_id=1, source_target_pairs={{0,8},{4,12},{8,0},{12,4},{1,9},{5,13},{9,1},{13,5},{2,10},{6,14},... | collective-permute-start | bytes 49160 | tf_op jit(solution)/shard_map/ppermute | solution.py:685
  98.7 0.6 collective-permute-start.20
  99.4 0.0 collective-permute-done.18
  99.4 1.9 %collective-permute-done.19 = f32[2,16,128]{2,1,0:T(8,128)S(1)} collective-permute-done((f32[2,16,128]{2,1,0:T(8,128)S(1)}, f32[2,16,128]{2,1,0:T(8,128)S(1)}, u32[]{:S(2)}, u32[]{:S(2)}) %collective-permute-start.19) | collective-permute-done | bytes 16416 | tf_op jit(solution)/shard_map/ppermute | solution.py:685
  101.3 3.0 %collective-permute-done.20 = f32[2,16,128]{2,1,0:T(8,128)S(1)} collective-permute-done((f32[2,16,128]{2,1,0:T(8,128)S(1)}, f32[2,16,128]{2,1,0:T(8,128)S(1)}, u32[]{:S(2)}, u32[]{:S(2)}) %collective-permute-start.20) | collective-permute-done | bytes 16416 | tf_op jit(solution)/shard_map/ppermute | solution.py:685
  104.3 0.1 collective-permute-start.21
  104.4 0.2 collective-permute-start.22
  104.6 1.6 %collective-permute-start.23 = (f32[2,16,128]{2,1,0:T(8,128)S(1)}, f32[2,16,128]{2,1,0:T(8,128)S(1)}, u32[]{:S(2)}, u32[]{:S(2)}) collective-permute-start(f32[2,16,128]{2,1,0:T(8,128)S(1)} %pad_maximum_fusion.1.part_0), channel_id=1, source_target_pairs={{0,3},{1,2},{2,1},{3,0},{4,7},{5,6},{6,5},{7,4},{8,11},{9,10},{10,... | collective-permute-start | bytes 49160 | tf_op jit(solution)/shard_map/ppermute | solution.py:688
  106.2 0.0 collective-permute-done.21.part_1
  106.2 2.0 %collective-permute-done.22.part_2 = f32[2,16,128]{2,1,0:T(8,128)S(1)} collective-permute-done((f32[2,16,128]{2,1,0:T(8,128)S(1)}, f32[2,16,128]{2,1,0:T(8,128)S(1)}, u32[]{:S(2)}, u32[]{:S(2)}) %collective-permute-start.22) | collective-permute-done | bytes 16416 | tf_op jit(solution)/shard_map/ppermute | solution.py:688
  108.2 0.0 collective-permute-done.23.part_3
  108.2 0.0 copy-done.3
  108.2 1.3 %pick.1 = (f32[16,128]{1,0:T(8,128)}, f32[16,128]{1,0:T(8,128)}) custom-call(s32[64]{0:T(128)S(1)} %copy-done.3, f32[2,16,128]{2,1,0:T(8,128)S(1)} %pad_maximum_fusion.1.part_0, f32[2,16,128]{2,1,0:T(8,128)S(1)} %collective-permute-done.21.part_1, f32[2,16,128]{2,1,0:T(8,128)S(1)} %collective-permute-done.22.part_2, ...), custom_call_target="tpu_custom_call" | custom-call | tf_op jit(solution)/shard_map/pick/pallas_call | solution.py:689
  (12 shorter events, 0.0 us)
Async XLA Ops:
  0.6 72.8 %collective-permute-start.7 = (bf16[2048,512]{1,0:T(8,128)(2,1)}, bf16[2048,512]{1,0:T(8,128)(2,1)}, u32[]{:S(2)}, u32[]{:S(2)}) collective-permute-start(bf16[2048,512]{1,0:T(8,128)(2,1)} %bitcast.7), channel_id=1, source_target_pairs={{0,1},{1,0},{2,3},{3,2},{4,5},{5,4},{6,7},{7,6},{8,9},{9,8},{10,11... | collective-permute-start | bytes 6291464 | tf_op jit(solution)/shard_map/ppermute | solution.py:570
  1.2 22.8 %copy-start.4 = (s32[1,16,24]{2,1,0:T(8,128)S(1)}, s32[1,16,24]{2,1,0:T(8,128)}, u32[]{:S(2)}) copy-start(s32[1,16,24]{2,1,0:T(8,128)} %param.7) | copy-start | bytes 4612
  3.5 5.2 %copy-start.5 = (s32[1,16]{1,0:T(1,128)S(1)}, s32[1,16]{1,0:T(1,128)}, u32[]{:S(2)}) copy-start(s32[1,16]{1,0:T(1,128)} %param.8) | copy-start | bytes 196
  3.5 18.5 %collective-permute-start.10 = (bf16[640,512]{1,0:T(8,128)(2,1)}, bf16[640,512]{1,0:T(8,128)(2,1)}, u32[]{:S(2)}, u32[]{:S(2)}) collective-permute-start(bf16[640,512]{1,0:T(8,128)(2,1)} %get-tuple-element.7), channel_id=1, source_target_pairs={{0,2},{1,3},{2,0},{3,1},{4,6},{5,7},{6,4},{7,5},{8,10},{9,11},{10,... | collective-permute-start | bytes 1966088 | tf_op jit(solution)/shard_map/ppermute | solution.py:567
  6.1 1.6 %copy-start = (bf16[1,2048,512]{2,1,0:T(8,128)(2,1)S(1)}, bf16[1,2048,512]{2,1,0:T(8,128)(2,1)}, u32[]{:S(2)}) copy-start(bf16[1,2048,512]{2,1,0:T(8,128)(2,1)} %param.6) | copy-start | bytes 6291460
  7.7 16.7 %copy-start.1 = (bf16[1,2048,512]{2,1,0:T(8,128)(2,1)S(1)}, bf16[1,2048,512]{2,1,0:T(8,128)(2,1)}, u32[]{:S(2)}) copy-start(bf16[1,2048,512]{2,1,0:T(8,128)(2,1)} %param.6) | copy-start | bytes 6291460
  7.7 22.0 %copy-start.2 = (bf16[512,512]{1,0:T(8,128)(2,1)S(1)}, bf16[512,512]{1,0:T(8,128)(2,1)}, u32[]{:S(2)}) copy-start(bf16[512,512]{1,0:T(8,128)(2,1)} %get-tuple-element.6.own_frames.refs_0_) | copy-start | bytes 1572868
  8.6 55.0 %collective-permute-start.11 = (bf16[768,512]{1,0:T(8,128)(2,1)}, bf16[768,512]{1,0:T(8,128)(2,1)S(1)}, u32[]{:S(2)}, u32[]{:S(2)}) collective-permute-start(bf16[768,512]{1,0:T(8,128)(2,1)} %cut_middle.1), channel_id=1, source_target_pairs={{0,2},{1,3},{2,0},{3,1},{4,6},{5,7},{6,4},{7,5},{8,10},{9,11},{10,... | collective-permute-start | bytes 2359304 | tf_op jit(solution)/shard_map/ppermute | solution.py:568
  22.0 42.2 %collective-permute-start.12 = (bf16[640,512]{1,0:T(8,128)(2,1)}, bf16[640,512]{1,0:T(8,128)(2,1)S(1)}, u32[]{:S(2)}, u32[]{:S(2)}) collective-permute-start(bf16[640,512]{1,0:T(8,128)(2,1)} %collective-permute-done.10.far_a), channel_id=1, source_target_pairs={{0,16},{16,0},{1,17},{17,1},{2,18},{18,2},{3,19},{19,3},{4,20},{20... | collective-permute-start | bytes 1966088 | tf_op jit(solution)/shard_map/ppermute | solution.py:569
  24.3 1.2 %collective-permute-start = (s32[16,128]{1,0:T(8,128)S(1)}, s32[16,128]{1,0:T(8,128)S(1)}, u32[]{:S(2)}, u32[]{:S(2)}) collective-permute-start(s32[16,128]{1,0:T(8,128)S(1)} %split.1.own_ref.own_listed), channel_id=1, source_target_pairs={{0,1},{1,0},{2,3},{3,2},{4,5},{5,4},{6,7},{7,6},{8,9},{9,8},{10,11... | collective-permute-start | bytes 24584 | tf_op jit(solution)/shard_map/ppermute | solution.py:584
  24.8 2.2 %collective-permute-start.5 = (f32[16,128]{1,0:T(8,128)S(1)}, f32[16,128]{1,0:T(8,128)S(1)}, u32[]{:S(2)}, u32[]{:S(2)}) collective-permute-start(f32[16,128]{1,0:T(8,128)S(1)} %medoid_norms.1.norms_own), channel_id=1, source_target_pairs={{0,1},{1,0},{2,3},{3,2},{4,5},{5,4},{6,7},{7,6},{8,9},{9,8},{10,11... | collective-permute-start | bytes 24584 | tf_op jit(solution)/shard_map/ppermute | solution.py:611
  25.5 4.2 %collective-permute-start.2 = (s32[16,128]{1,0:T(8,128)S(1)}, s32[16,128]{1,0:T(8,128)S(1)}, u32[]{:S(2)}, u32[]{:S(2)}) collective-permute-start(s32[16,128]{1,0:T(8,128)S(1)} %route.1.refs_0_), channel_id=1, source_target_pairs={{0,4},{4,0},{8,12},{12,8},{1,5},{5,1},{9,13},{13,9},{2,6},{6,2},{1... | collective-permute-start | bytes 24584 | tf_op jit(solution)/shard_map/ppermute | solution.py:593
  27.1 4.7 %collective-permute-start.3 = (s32[16,128]{1,0:T(8,128)S(1)}, s32[16,128]{1,0:T(8,128)S(1)}, u32[]{:S(2)}, u32[]{:S(2)}) collective-permute-start(s32[16,128]{1,0:T(8,128)S(1)} %route.1.refs_0_), channel_id=1, source_target_pairs={{0,8},{4,12},{8,0},{12,4},{1,9},{5,13},{9,1},{13,5},{2,10},{6,14},... | collective-permute-start | bytes 24584 | tf_op jit(solution)/shard_map/ppermute | solution.py:593
  29.7 34.0 %collective-permute-start.9 = (bf16[512,512]{1,0:T(8,128)(2,1)S(1)}, bf16[512,512]{1,0:T(8,128)(2,1)S(1)}, u32[]{:S(2)}, u32[]{:S(2)}) collective-permute-start(bf16[512,512]{1,0:T(8,128)(2,1)S(1)} %copy-done.2), channel_id=1, source_target_pairs={{0,8},{4,12},{8,0},{12,4},{1,9},{5,13},{9,1},{13,5},{2,10},{6,14},... | collective-permute-start | bytes 1572872 | tf_op jit(solution)/shard_map/ppermute | solution.py:562
  31.8 13.1 %collective-permute-start.1 = (s32[16,128]{1,0:T(8,128)S(1)}, s32[16,128]{1,0:T(8,128)S(1)}, u32[]{:S(2)}, u32[]{:S(2)}) collective-permute-start(s32[16,128]{1,0:T(8,128)S(1)} %route.1.refs_0_), channel_id=1, source_target_pairs={{0,12},{4,8},{8,4},{12,0},{1,13},{5,9},{9,5},{13,1},{2,14},{6,10},... | collective-permute-start | bytes 24584 | tf_op jit(solution)/shard_map/ppermute | solution.py:593
  44.9 3.7 %collective-permute-start.6 = (f32[2,16,128]{2,1,0:T(8,128)S(1)}, f32[2,16,128]{2,1,0:T(8,128)S(1)}, u32[]{:S(2)}, u32[]{:S(2)}) collective-permute-start(f32[2,16,128]{2,1,0:T(8,128)S(1)} %pad_maximum_fusion), channel_id=1, source_target_pairs={{0,2},{1,3},{2,0},{3,1},{4,6},{5,7},{6,4},{7,5},{8,10},{9,11},{10,... | collective-permute-start | bytes 49160 | tf_op jit(solution)/shard_map/ppermute | solution.py:613
  48.6 3.7 %collective-permute-start.4 = (s32[4,8,128]{2,1,0:T(8,128)S(1)}, s32[4,8,128]{2,1,0:T(8,128)S(1)}, u32[]{:S(2)}, u32[]{:S(2)}) collective-permute-start(s32[4,8,128]{2,1,0:T(8,128)S(1)} %stack_far.1), channel_id=1, source_target_pairs={{0,2},{1,3},{2,0},{3,1},{4,6},{5,7},{6,4},{7,5},{8,10},{9,11},{10,... | collective-permute-start | bytes 49160 | tf_op jit(solution)/shard_map/ppermute | solution.py:602
  52.4 20.4 %collective-permute-start.8 = (bf16[512,512]{1,0:T(8,128)(2,1)S(1)}, bf16[512,512]{1,0:T(8,128)(2,1)S(1)}, u32[]{:S(2)}, u32[]{:S(2)}) collective-permute-start(bf16[512,512]{1,0:T(8,128)(2,1)S(1)} %copy-done.2), channel_id=1, source_target_pairs={{0,4},{4,0},{8,12},{12,8},{1,5},{5,1},{9,13},{13,9},{2,6},{6,2},{1... | collective-permute-start | bytes 1572872 | tf_op jit(solution)/shard_map/ppermute | solution.py:563
  63.6 24.6 %collective-permute-start.14 = (bf16[768,512]{1,0:T(8,128)(2,1)S(1)}, bf16[768,512]{1,0:T(8,128)(2,1)S(1)}, u32[]{:S(2)}, u32[]{:S(2)}) collective-permute-start(bf16[768,512]{1,0:T(8,128)(2,1)S(1)} %collective-permute-done.11.far_b), channel_id=1, source_target_pairs={{0,1},{1,0},{2,3},{3,2},{4,5},{5,4},{6,7},{7,6},{8,9},{9,8},{10,11... | collective-permute-start | bytes 2359304 | tf_op jit(solution)/shard_map/ppermute | solution.py:572
  63.7 24.6 %collective-permute-start.13 = (bf16[640,512]{1,0:T(8,128)(2,1)}, bf16[640,512]{1,0:T(8,128)(2,1)S(1)}, u32[]{:S(2)}, u32[]{:S(2)}) collective-permute-start(bf16[640,512]{1,0:T(8,128)(2,1)} %collective-permute-done.10.far_a), channel_id=1, source_target_pairs={{0,1},{1,0},{2,3},{3,2},{4,5},{5,4},{6,7},{7,6},{8,9},{9,8},{10,11... | collective-permute-start | bytes 1966088 | tf_op jit(solution)/shard_map/ppermute | solution.py:571
  64.2 24.1 %collective-permute-start.15 = (bf16[640,512]{1,0:T(8,128)(2,1)S(1)}, bf16[640,512]{1,0:T(8,128)(2,1)S(1)}, u32[]{:S(2)}, u32[]{:S(2)}) collective-permute-start(bf16[640,512]{1,0:T(8,128)(2,1)S(1)} %collective-permute-done.12.far_c), channel_id=1, source_target_pairs={{0,1},{1,0},{2,3},{3,2},{4,5},{5,4},{6,7},{7,6},{8,9},{9,8},{10,11... | collective-permute-start | bytes 1966088 | tf_op jit(solution)/shard_map/ppermute | solution.py:573
  72.7 11.3 %collective-permute-start.16 = (bf16[512,512]{1,0:T(8,128)(2,1)S(1)}, bf16[512,512]{1,0:T(8,128)(2,1)S(1)}, u32[]{:S(2)}, u32[]{:S(2)}) collective-permute-start(bf16[512,512]{1,0:T(8,128)(2,1)S(1)} %copy-done.2), channel_id=1, source_target_pairs={{4,8},{8,4},{5,9},{9,5},{6,10},{10,6},{7,11},{11,7},{20,24},{24,20... | collective-permute-start | bytes 1572872 | tf_op jit(solution)/shard_map/ppermute | solution.py:564
  73.4 14.8 %collective-permute-start.17 = (bf16[512,512]{1,0:T(8,128)(2,1)S(1)}, bf16[512,512]{1,0:T(8,128)(2,1)S(1)}, u32[]{:S(2)}, u32[]{:S(2)}) collective-permute-start(bf16[512,512]{1,0:T(8,128)(2,1)S(1)} %collective-permute-done.9.frames_2.refs_2_), channel_id=1, source_target_pairs={{8,12},{4,0},{9,13},{5,1},{10,14},{6,2},{11,15},{7,3},{24,28},{20,... | collective-permute-start | bytes 1572872 | tf_op jit(solution)/shard_map/ppermute | solution.py:565
  84.0 24.2 %copy-start.3 = (s32[64]{0:T(128)S(1)}, s32[64]{0:T(128)}, u32[]{:S(2)}) copy-start(s32[64]{0:T(128)} %plan_ref.1) | copy-start | bytes 772
  94.9 4.5 %collective-permute-start.18 = (f32[2,16,128]{2,1,0:T(8,128)S(1)}, f32[2,16,128]{2,1,0:T(8,128)S(1)}, u32[]{:S(2)}, u32[]{:S(2)}) collective-permute-start(f32[2,16,128]{2,1,0:T(8,128)S(1)} %far_search.1), channel_id=1, source_target_pairs={{0,4},{4,0},{8,12},{12,8},{1,5},{5,1},{9,13},{13,9},{2,6},{6,2},{1... | collective-permute-start | bytes 49160 | tf_op jit(solution)/shard_map/ppermute | solution.py:685
  96.5 4.7 %collective-permute-start.19 = (f32[2,16,128]{2,1,0:T(8,128)S(1)}, f32[2,16,128]{2,1,0:T(8,128)S(1)}, u32[]{:S(2)}, u32[]{:S(2)}) collective-permute-start(f32[2,16,128]{2,1,0:T(8,128)S(1)} %far_search.1), channel_id=1, source_target_pairs={{0,8},{4,12},{8,0},{12,4},{1,9},{5,13},{9,1},{13,5},{2,10},{6,14},... | collective-permute-start | bytes 49160 | tf_op jit(solution)/shard_map/ppermute | solution.py:685
  98.7 5.5 %collective-permute-start.20 = (f32[2,16,128]{2,1,0:T(8,128)S(1)}, f32[2,16,128]{2,1,0:T(8,128)S(1)}, u32[]{:S(2)}, u32[]{:S(2)}) collective-permute-start(f32[2,16,128]{2,1,0:T(8,128)S(1)} %far_search.1), channel_id=1, source_target_pairs={{0,12},{4,8},{8,4},{12,0},{1,13},{5,9},{9,5},{13,1},{2,14},{6,10},... | collective-permute-start | bytes 49160 | tf_op jit(solution)/shard_map/ppermute | solution.py:685
  104.3 1.9 %collective-permute-start.21 = (f32[2,16,128]{2,1,0:T(8,128)S(1)}, f32[2,16,128]{2,1,0:T(8,128)S(1)}, u32[]{:S(2)}, u32[]{:S(2)}) collective-permute-start(f32[2,16,128]{2,1,0:T(8,128)S(1)} %pad_maximum_fusion.1.part_0), channel_id=1, source_target_pairs={{0,1},{1,0},{2,3},{3,2},{4,5},{5,4},{6,7},{7,6},{8,9},{9,8},{10,11... | collective-permute-start | bytes 49160 | tf_op jit(solution)/shard_map/ppermute | solution.py:688
  104.4 3.8 %collective-permute-start.22 = (f32[2,16,128]{2,1,0:T(8,128)S(1)}, f32[2,16,128]{2,1,0:T(8,128)S(1)}, u32[]{:S(2)}, u32[]{:S(2)}) collective-permute-start(f32[2,16,128]{2,1,0:T(8,128)S(1)} %pad_maximum_fusion.1.part_0), channel_id=1, source_target_pairs={{0,2},{1,3},{2,0},{3,1},{4,6},{5,7},{6,4},{7,5},{8,10},{9,11},{10,... | collective-permute-start | bytes 49160 | tf_op jit(solution)/shard_map/ppermute | solution.py:688
  104.6 3.6 %collective-permute-start.23 = (f32[2,16,128]{2,1,0:T(8,128)S(1)}, f32[2,16,128]{2,1,0:T(8,128)S(1)}, u32[]{:S(2)}, u32[]{:S(2)}) collective-permute-start(f32[2,16,128]{2,1,0:T(8,128)S(1)} %pad_maximum_fusion.1.part_0), channel_id=1, source_target_pairs={{0,3},{1,2},{2,1},{3,0},{4,7},{5,6},{6,5},{7,4},{8,11},{9,10},{10,... | collective-permute-start | bytes 49160 | tf_op jit(solution)/shard_map/ppermute | solution.py:688

commit v4 on v3

--- a/solution.py
+++ b/solution.py
@@ -9,12 +9,13 @@
 
 
 TILE = 128
+frame_axis, group_axis, slab_axis = "frames", "medoids", "slab"
 
 
 big_value = 1e30
 per_block = 8
 unroll = 2
-together = 6
+together = 8
 small_vmem = 8 << 20
 large_vmem = 24 << 20
 whole_vmem = 125 << 19
@@ -69,8 +70,8 @@
 
 def across_groups(first, second):
     every_one, every_two = (
-        lax.all_gather(first[None], "medoids", axis=0, tiled=True),
-        lax.all_gather(second[None], "medoids", axis=0, tiled=True),
+        lax.all_gather(first[None], group_axis, axis=0, tiled=True),
+        lax.all_gather(second[None], group_axis, axis=0, tiled=True),
     )
     best_one, best_two = (every_one[0], every_two[0])
     for group in range(1, every_one.shape[0]):
@@ -81,10 +82,10 @@
 def gathered_medoids(frames, medoids, tile_ids, tile_counts, plan):
     width = frames.shape[1]
     blocks = frames.shape[0] // TILE
-    members = lax.axis_size("frames")
-    member = lax.axis_index("frames")
+    members = lax.axis_size(frame_axis)
+    member = lax.axis_index(frame_axis)
     capacity = (blocks + members - 1) // members
-    group = lax.all_gather(medoids[0], "frames", axis=0, tiled=True)
+    group = lax.all_gather(medoids[0], frame_axis, axis=0, tiled=True)
     group_tiles = group.shape[0] // TILE
     group_rows = group.reshape(group_tiles, TILE, width)
     group_norm = jnp.sum(jnp.square(group.astype(jnp.float32)), axis=1).reshape(group_tiles, TILE)
@@ -112,9 +113,9 @@
         jnp.zeros((members, capacity), jnp.int32).at[my_target, my_slot].set(tile_counts[0])
     )
     incoming_tiles, incoming_ids, incoming_counts = (
-        lax.all_to_all(outgoing_tiles, "frames", split_axis=0, concat_axis=0, tiled=True),
-        lax.all_to_all(outgoing_ids, "frames", split_axis=0, concat_axis=0, tiled=True),
-        lax.all_to_all(outgoing_counts, "frames", split_axis=0, concat_axis=0, tiled=True),
+        lax.all_to_all(outgoing_tiles, frame_axis, split_axis=0, concat_axis=0, tiled=True),
+        lax.all_to_all(outgoing_ids, frame_axis, split_axis=0, concat_axis=0, tiled=True),
+        lax.all_to_all(outgoing_counts, frame_axis, split_axis=0, concat_axis=0, tiled=True),
     )
     placed_tiles = incoming_tiles[sender, sender_slot]
     placed_ids = incoming_ids[sender, sender_slot]
@@ -145,8 +146,8 @@
 
 def cut_first_kernel(frames_ref, group_ref, mine_ref, edge_ref, sems):
     quarter, side = mine_ref.shape[0], edge_ref.shape[0]
-    start = pl.multiple_of(lax.axis_index("medoids") * quarter, TILE)
-    end = pl.multiple_of(lax.axis_index("slab") * (group_ref.shape[0] - side), TILE)
+    start = pl.multiple_of(lax.axis_index(group_axis) * quarter, TILE)
+    end = pl.multiple_of(lax.axis_index(slab_axis) * (group_ref.shape[0] - side), TILE)
     copies = start_all(
         (
             (frames_ref.at[pl.ds(start, quarter)], mine_ref),
@@ -165,7 +166,7 @@
 
 
 def split_kernel(members, tiles_here, ids_ref, lists_ref):
-    member = lax.axis_index("frames")
+    member = lax.axis_index(frame_axis)
     rows, columns = ids_ref.shape
     lanes = lists_ref.shape[1] // members
     shape = (rows, members * lanes)
@@ -187,7 +188,7 @@
 
 def route_kernel(own_ref, near_ref, out_ref):
     quarter_tiles = out_ref.shape[0] // 4
-    piece = lax.axis_index("medoids")
+    piece = lax.axis_index(group_axis)
     row = 0
     for at in (piece, jnp.bitwise_xor(piece, 2)):
         for ref in (own_ref, near_ref):
@@ -328,7 +329,7 @@
     tile_rows = own_group.shape[0]
     tiles_here = tile_rows // TILE
     quarter_tiles = own_frames.shape[0] // TILE
-    first = lax.axis_index("medoids") * quarter_tiles
+    first = lax.axis_index(group_axis) * quarter_tiles
     copies = start_all(
         (
             (own_group, rows_buf.at[pl.ds(0, tile_rows)]),
@@ -400,8 +401,8 @@
     quarter_tiles = quarter // TILE
     width = own_frames.shape[1]
     members = frames_buf.shape[0] // quarter
-    member = lax.axis_index("frames")
-    slab = lax.axis_index("slab")
+    member = lax.axis_index(frame_axis)
+    slab = lax.axis_index(slab_axis)
     side = far_a.shape[0]
     middle = far_b.shape[0]
     near_side = slab * (tile_rows - side)
@@ -500,8 +501,8 @@
 
 
 def pick_kernel(plan_ref, part_0, part_1, part_2, part_3, first_ref, second_ref, every):
-    member = lax.axis_index("frames")
-    piece = lax.axis_index("medoids")
+    member = lax.axis_index(frame_axis)
+    piece = lax.axis_index(group_axis)
     blocks = first_ref.shape[0]
     parts = (part_0, part_1, part_2, part_3)
     quarter_tiles = blocks // len(parts)
@@ -525,8 +526,8 @@
 def gathered_frames(frames, medoids, tile_ids, tile_counts, plan):
     width = frames.shape[1]
     blocks = frames.shape[0] // TILE
-    members = lax.axis_size("frames")
-    groups = lax.axis_size("medoids")
+    members = lax.axis_size(frame_axis)
+    groups = lax.axis_size(group_axis)
     rows = medoids[0]
     tile_rows = rows.shape[0]
     quarter_tiles = blocks // groups
@@ -548,7 +549,6 @@
         out_specs=(vector, vector),
         scratch_shapes=[pltpu.SemaphoreType.DMA((2,))],
         compiler_params=pltpu.CompilerParams(vmem_limit_bytes=whole_vmem),
-        name="cut_first",
     )(frames, rows)
     inside_rows = pl.pallas_call(
         functools.partial(cut_middle_kernel, side),
@@ -557,20 +557,19 @@
         out_specs=vector,
         scratch_shapes=[pltpu.SemaphoreType.DMA],
         compiler_params=small,
-        name="cut_middle",
     )(rows)
-    frames_2 = lax.ppermute(mine, "frames", exchanged(members, 2))
-    frames_1 = lax.ppermute(mine, "frames", exchanged(members, 1))
-    frames_3a = lax.ppermute(mine, "frames", [(1, 2), (2, 1)])
-    frames_3b = lax.ppermute(frames_2, "frames", [(2, 3), (1, 0)])
-
-    far_a = lax.ppermute(edge, "medoids", exchanged(groups, 2))
-    far_b = lax.ppermute(inside_rows, "medoids", exchanged(groups, 2))
-    far_c = lax.ppermute(far_a, "slab", exchanged(2, 1))
-    near_group = lax.ppermute(rows, "medoids", exchanged(groups, 1))
-    last_a = lax.ppermute(far_a, "medoids", exchanged(groups, 1))
-    last_b = lax.ppermute(far_b, "medoids", exchanged(groups, 1))
-    last_c = lax.ppermute(far_c, "medoids", exchanged(groups, 1))
+    frames_2 = lax.ppermute(mine, frame_axis, exchanged(members, 2))
+    frames_1 = lax.ppermute(mine, frame_axis, exchanged(members, 1))
+    frames_3a = lax.ppermute(mine, frame_axis, [(1, 2), (2, 1)])
+    frames_3b = lax.ppermute(frames_2, frame_axis, [(2, 3), (1, 0)])
+
+    far_a = lax.ppermute(edge, group_axis, exchanged(groups, 2))
+    far_b = lax.ppermute(inside_rows, group_axis, exchanged(groups, 2))
+    far_c = lax.ppermute(far_a, slab_axis, exchanged(2, 1))
+    near_group = lax.ppermute(rows, group_axis, exchanged(groups, 1))
+    last_a = lax.ppermute(far_a, group_axis, exchanged(groups, 1))
+    last_b = lax.ppermute(far_b, group_axis, exchanged(groups, 1))
+    last_c = lax.ppermute(far_c, group_axis, exchanged(groups, 1))
 
     tiles_here = tile_rows // TILE
     listed = pl.pallas_call(
@@ -579,45 +578,40 @@
         in_specs=[vector],
         out_specs=vector,
         compiler_params=small,
-        name="split",
     )(jnp.concatenate([tile_ids[0], tile_counts[0][:, None]], axis=1))
-    near_listed = lax.ppermute(listed, "medoids", exchanged(groups, 1))
+    near_listed = lax.ppermute(listed, group_axis, exchanged(groups, 1))
     routed = pl.pallas_call(
         route_kernel,
         out_shape=jax.ShapeDtypeStruct((4 * quarter_tiles, TILE), jnp.int32),
         in_specs=[vector] * 2,
         out_specs=vector,
         compiler_params=small,
-        name="route",
     )(listed, near_listed)
-    near_lists = [lax.ppermute(routed, "frames", exchanged(members, at)) for at in (1, 2, 3)]
+    near_lists = [lax.ppermute(routed, frame_axis, exchanged(members, at)) for at in (1, 2, 3)]
     far_lists = pl.pallas_call(
         stack_kernel,
         out_shape=jax.ShapeDtypeStruct((members, 2 * quarter_tiles, TILE), jnp.int32),
         in_specs=[vector] * 4,
         out_specs=vector,
         compiler_params=small,
-        name="stack_far",
     )(routed, *near_lists)
-    far_lists = lax.ppermute(far_lists, "medoids", exchanged(groups, 2))
+    far_lists = lax.ppermute(far_lists, group_axis, exchanged(groups, 2))
     norms = pl.pallas_call(
         functools.partial(norms_kernel, 0.5),
         out_shape=jax.ShapeDtypeStruct((tiles_here, TILE), jnp.float32),
         in_specs=[vector],
         out_specs=vector,
         compiler_params=small,
-        name="medoid_norms",
     )(rows)
-    norm_near = lax.ppermute(norms, "medoids", exchanged(groups, 1))
+    norm_near = lax.ppermute(norms, group_axis, exchanged(groups, 1))
     norm_pair = jnp.stack([norms, norm_near])
-    norm_far = lax.ppermute(norm_pair, "medoids", exchanged(groups, 2))
+    norm_far = lax.ppermute(norm_pair, group_axis, exchanged(groups, 2))
     frame_norms = pl.pallas_call(
         functools.partial(norms_kernel, 1.0),
         out_shape=jax.ShapeDtypeStruct((3 * quarter_tiles, TILE), jnp.float32),
         in_specs=[vector] * 3,
         out_specs=vector,
         compiler_params=small,
-        name="frame_norms",
     )(mine, frames_1, frames_2)
 
     total_tiles = members * quarter_tiles
@@ -638,7 +632,6 @@
             pltpu.SemaphoreType.DMA((4,)),
         ],
         compiler_params=large,
-        name="own_search",
     )(listed, near_listed, norms, norm_near, rows, near_group, mine)
     before_near = pl.pallas_call(
         near_kernel,
@@ -656,7 +649,6 @@
             pltpu.SemaphoreType.DMA((8,)),
         ],
         compiler_params=large,
-        name="near_search",
     )(*near_lists[:2], norms, norm_near, rows, near_group, frames_1, frames_2)
     found = pl.pallas_call(
         far_kernel,
@@ -674,7 +666,6 @@
             pltpu.SemaphoreType.DMA((20,)),
         ],
         compiler_params=large,
-        name="far_search",
     )(
         near_lists[2], far_lists, norms, norm_near, norm_far, before_own, before_near, frame_norms, rows, near_group,
         far_a, far_b, far_c, last_a, last_b, last_c, mine, frames_1, frames_2, frames_3a, frames_3b,
@@ -682,10 +673,10 @@
 
     one, two = found[0], found[1]
     for at in (1, 2, 3):
-        other = lax.ppermute(found, "frames", exchanged(members, at))
+        other = lax.ppermute(found, frame_axis, exchanged(members, at))
         one, two = fold_two(one, two, other[0], other[1])
     merged = jnp.stack([one, two])
-    parts = [merged] + [lax.ppermute(merged, "medoids", exchanged(groups, at)) for at in (1, 2, 3)]
+    parts = [merged] + [lax.ppermute(merged, group_axis, exchanged(groups, at)) for at in (1, 2, 3)]
     first, second = pl.pallas_call(
         pick_kernel,
         out_shape=(jax.ShapeDtypeStruct((blocks, TILE), jnp.float32),) * 2,
@@ -693,24 +684,24 @@
         out_specs=(vector, vector),
         scratch_shapes=[pltpu.VMEM((2, groups * members * quarter_tiles, TILE), jnp.float32)],
         compiler_params=small,
-        name="pick",
     )(plan, *parts)
     return (first.reshape(-1), second.reshape(-1))
 
 
 def solution(mesh):
     placed = (
-        P(("slab", "frames"), None),
-        P("medoids", "frames", None),
-        P("medoids", ("slab", "frames"), None),
-        P("medoids", ("slab", "frames")),
-        P("slab"),
+        P((slab_axis, frame_axis), None),
+        P(group_axis, frame_axis, None),
+        P(group_axis, (slab_axis, frame_axis), None),
+        P(group_axis, (slab_axis, frame_axis)),
+        P(slab_axis),
     )
 
     def per_device(frames, medoids, tile_ids, tile_counts, plan):
         blocks = frames.shape[0] // TILE
-        quarters = mesh.shape["frames"] == 4 and mesh.shape["medoids"] == 4 and mesh.shape["slab"] == 2
-        if quarters and blocks % 4 == 0 and medoids.shape[1] // TILE >= 3:
+        quarters = mesh.shape[frame_axis] == 4 and mesh.shape[group_axis] == 4 and mesh.shape[slab_axis] == 2
+        tiles_here = medoids.shape[1] // TILE
+        if quarters and blocks % 4 == 0 and 3 <= tiles_here < TILE // 4:
             return gathered_frames(frames, medoids, tile_ids, tile_counts, plan)
         return gathered_medoids(frames, medoids, tile_ids, tile_counts, plan)
 
@@ -718,6 +709,6 @@
         per_device,
         mesh=mesh,
         in_specs=placed,
-        out_specs=(P(("slab", "frames")), P(("slab", "frames"))),
+        out_specs=(P((slab_axis, frame_axis)), P((slab_axis, frame_axis))),
         check_vma=False,
     )

time: 110 us -> 110 us (level)
  transfers between devices with their start and end apart: 24 -> 24, of which waited for: 10 -> 11; matrix products, arithmetic and copies ran while one was open for 0% -> 0% of each run, Pallas kernels for 12% -> 12%
where the time goes in v4:
time: 110 us; the launch traced here: 109 us
  waiting for transfers between devices  47.6 us (43%)
  starting transfers between devices  37.9 us (34%)
  Pallas kernels  21.2 us (19%)
  local copies, waits for them, and re-layouts  1.7 us (2%)
    ppermute x1, waiting for transfers between devices, gathered_frames(): far_a = lax.ppermute(edge, group_axis, exchanged(groups, 2))  13.2 us
    ppermute x1, starting transfers between devices, gathered_frames(): frames_1 = lax.ppermute(mine, frame_axis, exchanged(members, 1))  11.3 us
    ppermute x3, waiting for transfers between devices, gathered_frames(): lax.ppermute(routed, frame_axis, exchanged(members, at))  10.5 us
    ppermute x1, waiting for transfers between devices, gathered_frames(): frames_1 = lax.ppermute(mine, frame_axis, exchanged(members, 1))  8.5 us
    ppermute x3, starting transfers between devices, gathered_frames(): lax.ppermute(routed, frame_axis, exchanged(members, at))  6.72 us
    pallas_call x1, Pallas kernels, gathered_frames(): pl.pallas_call(far_kernel, out_shape=jax.ShapeDtypeStruct((2, total_tiles...  6.61 us
    pallas_call x1, Pallas kernels, gathered_frames(): pl.pallas_call(near_kernel, out_shape=jax.ShapeDtypeStruct((2, 2 * quarte...  5.05 us
    ppermute x3, waiting for transfers between devices, gathered_frames(): other = lax.ppermute(found, frame_axis, exchanged(members, at))  4.54 us
  transfers between devices with their start and end apart: 24, of which 11 were waited for; matrix products, arithmetic and copies ran while one was open for 0% of the time, Pallas kernels for 12%

profile of v4, /device:TPU:0, one launch (start us, length us, event | category | flops | bytes accessed | tf_op | source)
XLA Modules:
  0.0 109.3 jit_solution(7720273926576090150)
XLA Ops:
  0.6 0.6 collective-permute-start.7
  1.2 2.3 %shard_map.72 = (bf16[512,512]{1,0:T(8,128)(2,1)}, bf16[640,512]{1,0:T(8,128)(2,1)}) custom-call(bf16[2048,512]{1,0:T(8,128)(2,1)} %frames_ref.1, bf16[2048,512]{1,0:T(8,128)(2,1)} %bitcast.8), custom_call_target="tpu_custom_call" | custom-call | tf_op jit(solution)/shard_map/pallas_call | solution.py:542
  3.5 0.0 copy-start.5
  3.5 2.6 %collective-permute-start.10 = (bf16[640,512]{1,0:T(8,128)(2,1)}, bf16[640,512]{1,0:T(8,128)(2,1)}, u32[]{:S(2)}, u32[]{:S(2)}) collective-permute-start(bf16[640,512]{1,0:T(8,128)(2,1)} %get-tuple-element.7), channel_id=1, source_target_pairs={{0,2},{1,3},{2,0},{3,1},{4,6},{5,7},{6,4},{7,5},{8,10},{9,11},{10,... | collective-permute-start | bytes 1966088 | tf_op jit(solution)/shard_map/ppermute | solution.py:566
  6.1 1.6 %copy-done = bf16[1,2048,512]{2,1,0:T(8,128)(2,1)S(1)} copy-done((bf16[1,2048,512]{2,1,0:T(8,128)(2,1)S(1)}, bf16[1,2048,512]{2,1,0:T(8,128)(2,1)}, u32[]{:S(2)}) %copy-start) | copy-done | bytes 2097176
  7.7 0.9 shard_map.76
  8.6 0.1 collective-permute-start.11
  8.7 0.0 copy-done.5
  8.7 0.1 copy.7
  8.8 13.2 %collective-permute-done.10.far_a = bf16[640,512]{1,0:T(8,128)(2,1)} collective-permute-done((bf16[640,512]{1,0:T(8,128)(2,1)}, bf16[640,512]{1,0:T(8,128)(2,1)}, u32[]{:S(2)}, u32[]{:S(2)}) %collective-permute-start.10) | collective-permute-done | bytes 655392 | tf_op jit(solution)/shard_map/ppermute | solution.py:566
  22.0 2.0 %collective-permute-start.12 = (bf16[640,512]{1,0:T(8,128)(2,1)}, bf16[640,512]{1,0:T(8,128)(2,1)S(1)}, u32[]{:S(2)}, u32[]{:S(2)}) collective-permute-start(bf16[640,512]{1,0:T(8,128)(2,1)} %collective-permute-done.10.far_a), channel_id=1, source_target_pairs={{0,16},{16,0},{1,17},{17,1},{2,18},{18,2},{3,19},{19,3},{4,20},{20... | collective-permute-start | bytes 1966088 | tf_op jit(solution)/shard_map/ppermute | solution.py:568
  24.0 0.1 pad_add_fusion.ids_ref
  24.1 0.2 shard_map.68.own_ref.own_listed
  24.3 0.1 collective-permute-start
  24.3 0.5 shard_map.71.norms_own
  24.8 0.6 collective-permute-start.5
  25.4 0.1 collective-permute-done.near_ref.near_listed
  25.5 1.6 %collective-permute-start.2 = (s32[16,128]{1,0:T(8,128)S(1)}, s32[16,128]{1,0:T(8,128)S(1)}, u32[]{:S(2)}, u32[]{:S(2)}) collective-permute-start(s32[16,128]{1,0:T(8,128)S(1)} %shard_map.69.refs_0_), channel_id=1, source_target_pairs={{0,4},{4,0},{8,12},{12,8},{1,5},{5,1},{9,13},{13,9},{2,6},{6,2},{1... | collective-permute-start | bytes 24584 | tf_op jit(solution)/shard_map/ppermute | solution.py:590
  27.1 0.0 collective-permute-done.5.norms_near
  27.1 2.6 %collective-permute-start.3 = (s32[16,128]{1,0:T(8,128)S(1)}, s32[16,128]{1,0:T(8,128)S(1)}, u32[]{:S(2)}, u32[]{:S(2)}) collective-permute-start(s32[16,128]{1,0:T(8,128)S(1)} %shard_map.69.refs_0_), channel_id=1, source_target_pairs={{0,8},{4,12},{8,0},{12,4},{1,9},{5,13},{9,1},{13,5},{2,10},{6,14},... | collective-permute-start | bytes 24584 | tf_op jit(solution)/shard_map/ppermute | solution.py:590
  29.7 0.0 collective-permute-done.2.refs_1_.lists_1
  29.7 0.0 copy-done.2
  29.7 2.1 %collective-permute-start.9 = (bf16[512,512]{1,0:T(8,128)(2,1)S(1)}, bf16[512,512]{1,0:T(8,128)(2,1)S(1)}, u32[]{:S(2)}, u32[]{:S(2)}) collective-permute-start(bf16[512,512]{1,0:T(8,128)(2,1)S(1)} %copy-done.2), channel_id=1, source_target_pairs={{0,8},{4,12},{8,0},{12,4},{1,9},{5,13},{9,1},{13,5},{2,10},{6,14},... | collective-permute-start | bytes 1572872 | tf_op jit(solution)/shard_map/ppermute | solution.py:561
  31.8 0.0 collective-permute-done.3.refs_2_.lists_2
  31.8 2.6 %collective-permute-start.1 = (s32[16,128]{1,0:T(8,128)S(1)}, s32[16,128]{1,0:T(8,128)S(1)}, u32[]{:S(2)}, u32[]{:S(2)}) collective-permute-start(s32[16,128]{1,0:T(8,128)S(1)} %shard_map.69.refs_0_), channel_id=1, source_target_pairs={{0,12},{4,8},{8,4},{12,0},{1,13},{5,9},{9,5},{13,1},{2,14},{6,10},... | collective-permute-start | bytes 24584 | tf_op jit(solution)/shard_map/ppermute | solution.py:590
  34.4 10.5 %collective-permute-done.1.refs_3_.near_lists = s32[16,128]{1,0:T(8,128)S(1)} collective-permute-done((s32[16,128]{1,0:T(8,128)S(1)}, s32[16,128]{1,0:T(8,128)S(1)}, u32[]{:S(2)}, u32[]{:S(2)}) %collective-permute-start.1) | collective-permute-done | bytes 8224 | tf_op jit(solution)/shard_map/ppermute | solution.py:590
  44.9 1.5 %collective-permute-start.6 = (f32[2,16,128]{2,1,0:T(8,128)S(1)}, f32[2,16,128]{2,1,0:T(8,128)S(1)}, u32[]{:S(2)}, u32[]{:S(2)}) collective-permute-start(f32[2,16,128]{2,1,0:T(8,128)S(1)} %pad_maximum_fusion), channel_id=1, source_target_pairs={{0,2},{1,3},{2,0},{3,1},{4,6},{5,7},{6,4},{7,5},{8,10},{9,11},{10,... | collective-permute-start | bytes 49160 | tf_op jit(solution)/shard_map/ppermute | solution.py:608
  46.4 2.2 %collective-permute-done.6.norms_far = f32[2,16,128]{2,1,0:T(8,128)S(1)} collective-permute-done((f32[2,16,128]{2,1,0:T(8,128)S(1)}, f32[2,16,128]{2,1,0:T(8,128)S(1)}, u32[]{:S(2)}, u32[]{:S(2)}) %collective-permute-start.6) | collective-permute-done | bytes 16416 | tf_op jit(solution)/shard_map/ppermute | solution.py:608
  48.6 1.5 %collective-permute-start.4 = (s32[4,8,128]{2,1,0:T(8,128)S(1)}, s32[4,8,128]{2,1,0:T(8,128)S(1)}, u32[]{:S(2)}, u32[]{:S(2)}) collective-permute-start(s32[4,8,128]{2,1,0:T(8,128)S(1)} %shard_map.70), channel_id=1, source_target_pairs={{0,2},{1,3},{2,0},{3,1},{4,6},{5,7},{6,4},{7,5},{8,10},{9,11},{10,... | collective-permute-start | bytes 49160 | tf_op jit(solution)/shard_map/ppermute | solution.py:598
  50.1 2.2 %collective-permute-done.4.far_lists = s32[4,8,128]{2,1,0:T(8,128)S(1)} collective-permute-done((s32[4,8,128]{2,1,0:T(8,128)S(1)}, s32[4,8,128]{2,1,0:T(8,128)S(1)}, u32[]{:S(2)}, u32[]{:S(2)}) %collective-permute-start.4) | collective-permute-done | bytes 16416 | tf_op jit(solution)/shard_map/ppermute | solution.py:598
  52.4 11.3 %collective-permute-start.8 = (bf16[512,512]{1,0:T(8,128)(2,1)S(1)}, bf16[512,512]{1,0:T(8,128)(2,1)S(1)}, u32[]{:S(2)}, u32[]{:S(2)}) collective-permute-start(bf16[512,512]{1,0:T(8,128)(2,1)S(1)} %copy-done.2), channel_id=1, source_target_pairs={{0,4},{4,0},{8,12},{12,8},{1,5},{5,1},{9,13},{13,9},{2,6},{6,2},{1... | collective-permute-start | bytes 1572872 | tf_op jit(solution)/shard_map/ppermute | solution.py:562
  63.6 0.0 collective-permute-done.11.far_b
  63.6 0.0 collective-permute-start.14
  63.6 0.0 collective-permute-done.9.frames_2.refs_2_
  63.7 0.5 collective-permute-start.13
  64.2 0.0 collective-permute-done.12.far_c
  64.2 0.1 collective-permute-start.15
  64.2 8.5 %collective-permute-done.8.frames_1.refs_1_ = bf16[512,512]{1,0:T(8,128)(2,1)S(1)} collective-permute-done((bf16[512,512]{1,0:T(8,128)(2,1)S(1)}, bf16[512,512]{1,0:T(8,128)(2,1)S(1)}, u32[]{:S(2)}, u32[]{:S(2)}) %collective-permute-start.8) | collective-permute-done | bytes 524320 | tf_op jit(solution)/shard_map/ppermute | solution.py:562
  72.7 0.7 collective-permute-start.16
  73.4 0.0 collective-permute-done.7.near_group
  73.4 1.3 %collective-permute-start.17 = (bf16[512,512]{1,0:T(8,128)(2,1)S(1)}, bf16[512,512]{1,0:T(8,128)(2,1)S(1)}, u32[]{:S(2)}, u32[]{:S(2)}) collective-permute-start(bf16[512,512]{1,0:T(8,128)(2,1)S(1)} %collective-permute-done.9.frames_2.refs_2_), channel_id=1, source_target_pairs={{8,12},{4,0},{9,13},{5,1},{10,14},{6,2},{11,15},{7,3},{24,28},{20,... | collective-permute-start | bytes 1572872 | tf_op jit(solution)/shard_map/ppermute | solution.py:564
  74.7 0.4 shard_map.75.frame_norms
  75.1 5.1 %shard_map.74.before_near = f32[2,8,128]{2,1,0:T(8,128)S(1)} custom-call(s32[16,128]{1,0:T(8,128)S(1)} %collective-permute-done.2.refs_1_.lists_1, s32[16,128]{1,0:T(8,128)S(1)} %collective-permute-done.3.refs_2_.lists_2, f32[16,128]{1,0:T(8,128)S(1)} %shard_map.71.norms_own, f32[16,128]{1,0:T(8,128)S(1)} %collective-permute-done.5.norms_near, ...), custom_call_target="tpu_custom_call" | custom-call | tf_op jit(solution)/shard_map/pallas_call | solution.py:636
  80.2 3.9 %shard_map.73.before_own = f32[2,4,128]{2,1,0:T(4,128)S(1)} custom-call(s32[16,128]{1,0:T(8,128)S(1)} %shard_map.68.own_ref.own_listed, s32[16,128]{1,0:T(8,128)S(1)} %collective-permute-done.near_ref.near_listed, f32[16,128]{1,0:T(8,128)S(1)} %shard_map.71.norms_own, f32[16,128]{1,0:T(8,128)S(1)} %collective-permute-done.5.norms_near, ...), custom_call_target="tpu_custom_call" | custom-call | tf_op jit(solution)/shard_map/pallas_call | solution.py:620
  84.1 0.0 copy-start.3
  84.1 0.0 collective-permute-done.16.frames_3a
  84.2 4.1 %collective-permute-done.17.frames_3b = bf16[512,512]{1,0:T(8,128)(2,1)S(1)} collective-permute-done((bf16[512,512]{1,0:T(8,128)(2,1)S(1)}, bf16[512,512]{1,0:T(8,128)(2,1)S(1)}, u32[]{:S(2)}, u32[]{:S(2)}) %collective-permute-start.17) | collective-permute-done | bytes 524320 | tf_op jit(solution)/shard_map/ppermute | solution.py:564
  88.2 0.0 collective-permute-done.13.last_a
  88.2 0.0 collective-permute-done.14.last_b
  88.2 0.0 collective-permute-done.15.last_c
  88.2 6.6 %shard_map.77 = f32[2,16,128]{2,1,0:T(8,128)S(1)} custom-call(s32[16,128]{1,0:T(8,128)S(1)} %collective-permute-done.1.refs_3_.near_lists, s32[4,8,128]{2,1,0:T(8,128)S(1)} %collective-permute-done.4.far_lists, f32[16,128]{1,0:T(8,128)S(1)} %shard_map.71.norms_own, f32[16,128]{1,0:T(8,128)S(1)} %collective-permute-done.5.norms_near, ...), custom_call_target="tpu_custom_call" | custom-call | tf_op jit(solution)/shard_map/pallas_call | solution.py:653
  94.9 1.1 %collective-permute-start.18 = (f32[2,16,128]{2,1,0:T(8,128)S(1)}, f32[2,16,128]{2,1,0:T(8,128)S(1)}, u32[]{:S(2)}, u32[]{:S(2)}) collective-permute-start(f32[2,16,128]{2,1,0:T(8,128)S(1)} %shard_map.77), channel_id=1, source_target_pairs={{0,4},{4,0},{8,12},{12,8},{1,5},{5,1},{9,13},{13,9},{2,6},{6,2},{1... | collective-permute-start | bytes 49160 | tf_op jit(solution)/shard_map/ppermute | solution.py:676
  96.0 2.3 %collective-permute-start.19 = (f32[2,16,128]{2,1,0:T(8,128)S(1)}, f32[2,16,128]{2,1,0:T(8,128)S(1)}, u32[]{:S(2)}, u32[]{:S(2)}) collective-permute-start(f32[2,16,128]{2,1,0:T(8,128)S(1)} %shard_map.77), channel_id=1, source_target_pairs={{0,8},{4,12},{8,0},{12,4},{1,9},{5,13},{9,1},{13,5},{2,10},{6,14},... | collective-permute-start | bytes 49160 | tf_op jit(solution)/shard_map/ppermute | solution.py:676
  98.3 1.0 collective-permute-start.20
  99.3 0.0 collective-permute-done.18
  99.3 1.3 %collective-permute-done.19 = f32[2,16,128]{2,1,0:T(8,128)S(1)} collective-permute-done((f32[2,16,128]{2,1,0:T(8,128)S(1)}, f32[2,16,128]{2,1,0:T(8,128)S(1)}, u32[]{:S(2)}, u32[]{:S(2)}) %collective-permute-start.19) | collective-permute-done | bytes 16416 | tf_op jit(solution)/shard_map/ppermute | solution.py:676
  100.6 3.2 %collective-permute-done.20 = f32[2,16,128]{2,1,0:T(8,128)S(1)} collective-permute-done((f32[2,16,128]{2,1,0:T(8,128)S(1)}, f32[2,16,128]{2,1,0:T(8,128)S(1)}, u32[]{:S(2)}, u32[]{:S(2)}) %collective-permute-start.20) | collective-permute-done | bytes 16416 | tf_op jit(solution)/shard_map/ppermute | solution.py:676
  103.9 0.1 collective-permute-start.21
  104.0 0.7 collective-permute-start.22
  104.7 1.1 %collective-permute-start.23 = (f32[2,16,128]{2,1,0:T(8,128)S(1)}, f32[2,16,128]{2,1,0:T(8,128)S(1)}, u32[]{:S(2)}, u32[]{:S(2)}) collective-permute-start(f32[2,16,128]{2,1,0:T(8,128)S(1)} %pad_maximum_fusion.1.part_0), channel_id=1, source_target_pairs={{0,3},{1,2},{2,1},{3,0},{4,7},{5,6},{6,5},{7,4},{8,11},{9,10},{10,... | collective-permute-start | bytes 49160 | tf_op jit(solution)/shard_map/ppermute | solution.py:679
  105.8 0.0 collective-permute-done.21.part_1
  105.8 2.0 %collective-permute-done.22.part_2 = f32[2,16,128]{2,1,0:T(8,128)S(1)} collective-permute-done((f32[2,16,128]{2,1,0:T(8,128)S(1)}, f32[2,16,128]{2,1,0:T(8,128)S(1)}, u32[]{:S(2)}, u32[]{:S(2)}) %collective-permute-start.22) | collective-permute-done | bytes 16416 | tf_op jit(solution)/shard_map/ppermute | solution.py:679
  107.8 0.1 collective-permute-done.23.part_3
  107.9 1.3 %shard_map.78 = (f32[16,128]{1,0:T(8,128)}, f32[16,128]{1,0:T(8,128)}) custom-call(s32[64]{0:T(128)S(1)} %copy-done.3, f32[2,16,128]{2,1,0:T(8,128)S(1)} %pad_maximum_fusion.1.part_0, f32[2,16,128]{2,1,0:T(8,128)S(1)} %collective-permute-done.21.part_1, f32[2,16,128]{2,1,0:T(8,128)S(1)} %collective-permute-done.22.part_2, ...), custom_call_target="tpu_custom_call" | custom-call | tf_op jit(solution)/shard_map/pallas_call | solution.py:680
  (12 shorter events, 0.0 us)
Async XLA Ops:
  0.6 72.8 %collective-permute-start.7 = (bf16[2048,512]{1,0:T(8,128)(2,1)}, bf16[2048,512]{1,0:T(8,128)(2,1)}, u32[]{:S(2)}, u32[]{:S(2)}) collective-permute-start(bf16[2048,512]{1,0:T(8,128)(2,1)} %bitcast.7), channel_id=1, source_target_pairs={{0,1},{1,0},{2,3},{3,2},{4,5},{5,4},{6,7},{7,6},{8,9},{9,8},{10,11... | collective-permute-start | bytes 6291464 | tf_op jit(solution)/shard_map/ppermute | solution.py:569
  1.2 22.8 %copy-start.4 = (s32[1,16,24]{2,1,0:T(8,128)S(1)}, s32[1,16,24]{2,1,0:T(8,128)}, u32[]{:S(2)}) copy-start(s32[1,16,24]{2,1,0:T(8,128)} %param.7) | copy-start | bytes 4612
  3.5 5.2 %copy-start.5 = (s32[1,16]{1,0:T(1,128)S(1)}, s32[1,16]{1,0:T(1,128)}, u32[]{:S(2)}) copy-start(s32[1,16]{1,0:T(1,128)} %param.8) | copy-start | bytes 196
  3.5 18.5 %collective-permute-start.10 = (bf16[640,512]{1,0:T(8,128)(2,1)}, bf16[640,512]{1,0:T(8,128)(2,1)}, u32[]{:S(2)}, u32[]{:S(2)}) collective-permute-start(bf16[640,512]{1,0:T(8,128)(2,1)} %get-tuple-element.7), channel_id=1, source_target_pairs={{0,2},{1,3},{2,0},{3,1},{4,6},{5,7},{6,4},{7,5},{8,10},{9,11},{10,... | collective-permute-start | bytes 1966088 | tf_op jit(solution)/shard_map/ppermute | solution.py:566
  6.1 1.6 %copy-start = (bf16[1,2048,512]{2,1,0:T(8,128)(2,1)S(1)}, bf16[1,2048,512]{2,1,0:T(8,128)(2,1)}, u32[]{:S(2)}) copy-start(bf16[1,2048,512]{2,1,0:T(8,128)(2,1)} %param.6) | copy-start | bytes 6291460
  7.7 16.7 %copy-start.1 = (bf16[1,2048,512]{2,1,0:T(8,128)(2,1)S(1)}, bf16[1,2048,512]{2,1,0:T(8,128)(2,1)}, u32[]{:S(2)}) copy-start(bf16[1,2048,512]{2,1,0:T(8,128)(2,1)} %param.6) | copy-start | bytes 6291460
  7.7 22.0 %copy-start.2 = (bf16[512,512]{1,0:T(8,128)(2,1)S(1)}, bf16[512,512]{1,0:T(8,128)(2,1)}, u32[]{:S(2)}) copy-start(bf16[512,512]{1,0:T(8,128)(2,1)} %get-tuple-element.6.own_frames.refs_0_) | copy-start | bytes 1572868
  8.6 55.0 %collective-permute-start.11 = (bf16[768,512]{1,0:T(8,128)(2,1)}, bf16[768,512]{1,0:T(8,128)(2,1)S(1)}, u32[]{:S(2)}, u32[]{:S(2)}) collective-permute-start(bf16[768,512]{1,0:T(8,128)(2,1)} %shard_map.76), channel_id=1, source_target_pairs={{0,2},{1,3},{2,0},{3,1},{4,6},{5,7},{6,4},{7,5},{8,10},{9,11},{10,... | collective-permute-start | bytes 2359304 | tf_op jit(solution)/shard_map/ppermute | solution.py:567
  22.0 42.2 %collective-permute-start.12 = (bf16[640,512]{1,0:T(8,128)(2,1)}, bf16[640,512]{1,0:T(8,128)(2,1)S(1)}, u32[]{:S(2)}, u32[]{:S(2)}) collective-permute-start(bf16[640,512]{1,0:T(8,128)(2,1)} %collective-permute-done.10.far_a), channel_id=1, source_target_pairs={{0,16},{16,0},{1,17},{17,1},{2,18},{18,2},{3,19},{19,3},{4,20},{20... | collective-permute-start | bytes 1966088 | tf_op jit(solution)/shard_map/ppermute | solution.py:568
  24.3 1.2 %collective-permute-start = (s32[16,128]{1,0:T(8,128)S(1)}, s32[16,128]{1,0:T(8,128)S(1)}, u32[]{:S(2)}, u32[]{:S(2)}) collective-permute-start(s32[16,128]{1,0:T(8,128)S(1)} %shard_map.68.own_ref.own_listed), channel_id=1, source_target_pairs={{0,1},{1,0},{2,3},{3,2},{4,5},{5,4},{6,7},{7,6},{8,9},{9,8},{10,11... | collective-permute-start | bytes 24584 | tf_op jit(solution)/shard_map/ppermute | solution.py:582
  24.8 2.2 %collective-permute-start.5 = (f32[16,128]{1,0:T(8,128)S(1)}, f32[16,128]{1,0:T(8,128)S(1)}, u32[]{:S(2)}, u32[]{:S(2)}) collective-permute-start(f32[16,128]{1,0:T(8,128)S(1)} %shard_map.71.norms_own), channel_id=1, source_target_pairs={{0,1},{1,0},{2,3},{3,2},{4,5},{5,4},{6,7},{7,6},{8,9},{9,8},{10,11... | collective-permute-start | bytes 24584 | tf_op jit(solution)/shard_map/ppermute | solution.py:606
  25.5 4.2 %collective-permute-start.2 = (s32[16,128]{1,0:T(8,128)S(1)}, s32[16,128]{1,0:T(8,128)S(1)}, u32[]{:S(2)}, u32[]{:S(2)}) collective-permute-start(s32[16,128]{1,0:T(8,128)S(1)} %shard_map.69.refs_0_), channel_id=1, source_target_pairs={{0,4},{4,0},{8,12},{12,8},{1,5},{5,1},{9,13},{13,9},{2,6},{6,2},{1... | collective-permute-start | bytes 24584 | tf_op jit(solution)/shard_map/ppermute | solution.py:590
  27.1 4.7 %collective-permute-start.3 = (s32[16,128]{1,0:T(8,128)S(1)}, s32[16,128]{1,0:T(8,128)S(1)}, u32[]{:S(2)}, u32[]{:S(2)}) collective-permute-start(s32[16,128]{1,0:T(8,128)S(1)} %shard_map.69.refs_0_), channel_id=1, source_target_pairs={{0,8},{4,12},{8,0},{12,4},{1,9},{5,13},{9,1},{13,5},{2,10},{6,14},... | collective-permute-start | bytes 24584 | tf_op jit(solution)/shard_map/ppermute | solution.py:590
  29.7 34.0 %collective-permute-start.9 = (bf16[512,512]{1,0:T(8,128)(2,1)S(1)}, bf16[512,512]{1,0:T(8,128)(2,1)S(1)}, u32[]{:S(2)}, u32[]{:S(2)}) collective-permute-start(bf16[512,512]{1,0:T(8,128)(2,1)S(1)} %copy-done.2), channel_id=1, source_target_pairs={{0,8},{4,12},{8,0},{12,4},{1,9},{5,13},{9,1},{13,5},{2,10},{6,14},... | collective-permute-start | bytes 1572872 | tf_op jit(solution)/shard_map/ppermute | solution.py:561
  31.8 13.1 %collective-permute-start.1 = (s32[16,128]{1,0:T(8,128)S(1)}, s32[16,128]{1,0:T(8,128)S(1)}, u32[]{:S(2)}, u32[]{:S(2)}) collective-permute-start(s32[16,128]{1,0:T(8,128)S(1)} %shard_map.69.refs_0_), channel_id=1, source_target_pairs={{0,12},{4,8},{8,4},{12,0},{1,13},{5,9},{9,5},{13,1},{2,14},{6,10},... | collective-permute-start | bytes 24584 | tf_op jit(solution)/shard_map/ppermute | solution.py:590
  44.9 3.7 %collective-permute-start.6 = (f32[2,16,128]{2,1,0:T(8,128)S(1)}, f32[2,16,128]{2,1,0:T(8,128)S(1)}, u32[]{:S(2)}, u32[]{:S(2)}) collective-permute-start(f32[2,16,128]{2,1,0:T(8,128)S(1)} %pad_maximum_fusion), channel_id=1, source_target_pairs={{0,2},{1,3},{2,0},{3,1},{4,6},{5,7},{6,4},{7,5},{8,10},{9,11},{10,... | collective-permute-start | bytes 49160 | tf_op jit(solution)/shard_map/ppermute | solution.py:608
  48.6 3.7 %collective-permute-start.4 = (s32[4,8,128]{2,1,0:T(8,128)S(1)}, s32[4,8,128]{2,1,0:T(8,128)S(1)}, u32[]{:S(2)}, u32[]{:S(2)}) collective-permute-start(s32[4,8,128]{2,1,0:T(8,128)S(1)} %shard_map.70), channel_id=1, source_target_pairs={{0,2},{1,3},{2,0},{3,1},{4,6},{5,7},{6,4},{7,5},{8,10},{9,11},{10,... | collective-permute-start | bytes 49160 | tf_op jit(solution)/shard_map/ppermute | solution.py:598
  52.4 20.4 %collective-permute-start.8 = (bf16[512,512]{1,0:T(8,128)(2,1)S(1)}, bf16[512,512]{1,0:T(8,128)(2,1)S(1)}, u32[]{:S(2)}, u32[]{:S(2)}) collective-permute-start(bf16[512,512]{1,0:T(8,128)(2,1)S(1)} %copy-done.2), channel_id=1, source_target_pairs={{0,4},{4,0},{8,12},{12,8},{1,5},{5,1},{9,13},{13,9},{2,6},{6,2},{1... | collective-permute-start | bytes 1572872 | tf_op jit(solution)/shard_map/ppermute | solution.py:562
  63.6 24.6 %collective-permute-start.14 = (bf16[768,512]{1,0:T(8,128)(2,1)S(1)}, bf16[768,512]{1,0:T(8,128)(2,1)S(1)}, u32[]{:S(2)}, u32[]{:S(2)}) collective-permute-start(bf16[768,512]{1,0:T(8,128)(2,1)S(1)} %collective-permute-done.11.far_b), channel_id=1, source_target_pairs={{0,1},{1,0},{2,3},{3,2},{4,5},{5,4},{6,7},{7,6},{8,9},{9,8},{10,11... | collective-permute-start | bytes 2359304 | tf_op jit(solution)/shard_map/ppermute | solution.py:571
  63.7 24.6 %collective-permute-start.13 = (bf16[640,512]{1,0:T(8,128)(2,1)}, bf16[640,512]{1,0:T(8,128)(2,1)S(1)}, u32[]{:S(2)}, u32[]{:S(2)}) collective-permute-start(bf16[640,512]{1,0:T(8,128)(2,1)} %collective-permute-done.10.far_a), channel_id=1, source_target_pairs={{0,1},{1,0},{2,3},{3,2},{4,5},{5,4},{6,7},{7,6},{8,9},{9,8},{10,11... | collective-permute-start | bytes 1966088 | tf_op jit(solution)/shard_map/ppermute | solution.py:570
  64.2 24.1 %collective-permute-start.15 = (bf16[640,512]{1,0:T(8,128)(2,1)S(1)}, bf16[640,512]{1,0:T(8,128)(2,1)S(1)}, u32[]{:S(2)}, u32[]{:S(2)}) collective-permute-start(bf16[640,512]{1,0:T(8,128)(2,1)S(1)} %collective-permute-done.12.far_c), channel_id=1, source_target_pairs={{0,1},{1,0},{2,3},{3,2},{4,5},{5,4},{6,7},{7,6},{8,9},{9,8},{10,11... | collective-permute-start | bytes 1966088 | tf_op jit(solution)/shard_map/ppermute | solution.py:572
  72.7 11.4 %collective-permute-start.16 = (bf16[512,512]{1,0:T(8,128)(2,1)S(1)}, bf16[512,512]{1,0:T(8,128)(2,1)S(1)}, u32[]{:S(2)}, u32[]{:S(2)}) collective-permute-start(bf16[512,512]{1,0:T(8,128)(2,1)S(1)} %copy-done.2), channel_id=1, source_target_pairs={{4,8},{8,4},{5,9},{9,5},{6,10},{10,6},{7,11},{11,7},{20,24},{24,20... | collective-permute-start | bytes 1572872 | tf_op jit(solution)/shard_map/ppermute | solution.py:563
  73.4 14.8 %collective-permute-start.17 = (bf16[512,512]{1,0:T(8,128)(2,1)S(1)}, bf16[512,512]{1,0:T(8,128)(2,1)S(1)}, u32[]{:S(2)}, u32[]{:S(2)}) collective-permute-start(bf16[512,512]{1,0:T(8,128)(2,1)S(1)} %collective-permute-done.9.frames_2.refs_2_), channel_id=1, source_target_pairs={{8,12},{4,0},{9,13},{5,1},{10,14},{6,2},{11,15},{7,3},{24,28},{20,... | collective-permute-start | bytes 1572872 | tf_op jit(solution)/shard_map/ppermute | solution.py:564
  84.1 23.8 %copy-start.3 = (s32[64]{0:T(128)S(1)}, s32[64]{0:T(128)}, u32[]{:S(2)}) copy-start(s32[64]{0:T(128)} %plan_ref.1) | copy-start | bytes 772
  94.9 4.5 %collective-permute-start.18 = (f32[2,16,128]{2,1,0:T(8,128)S(1)}, f32[2,16,128]{2,1,0:T(8,128)S(1)}, u32[]{:S(2)}, u32[]{:S(2)}) collective-permute-start(f32[2,16,128]{2,1,0:T(8,128)S(1)} %shard_map.77), channel_id=1, source_target_pairs={{0,4},{4,0},{8,12},{12,8},{1,5},{5,1},{9,13},{13,9},{2,6},{6,2},{1... | collective-permute-start | bytes 49160 | tf_op jit(solution)/shard_map/ppermute | solution.py:676
  96.0 4.6 %collective-permute-start.19 = (f32[2,16,128]{2,1,0:T(8,128)S(1)}, f32[2,16,128]{2,1,0:T(8,128)S(1)}, u32[]{:S(2)}, u32[]{:S(2)}) collective-permute-start(f32[2,16,128]{2,1,0:T(8,128)S(1)} %shard_map.77), channel_id=1, source_target_pairs={{0,8},{4,12},{8,0},{12,4},{1,9},{5,13},{9,1},{13,5},{2,10},{6,14},... | collective-permute-start | bytes 49160 | tf_op jit(solution)/shard_map/ppermute | solution.py:676
  98.3 5.5 %collective-permute-start.20 = (f32[2,16,128]{2,1,0:T(8,128)S(1)}, f32[2,16,128]{2,1,0:T(8,128)S(1)}, u32[]{:S(2)}, u32[]{:S(2)}) collective-permute-start(f32[2,16,128]{2,1,0:T(8,128)S(1)} %shard_map.77), channel_id=1, source_target_pairs={{0,12},{4,8},{8,4},{12,0},{1,13},{5,9},{9,5},{13,1},{2,14},{6,10},... | collective-permute-start | bytes 49160 | tf_op jit(solution)/shard_map/ppermute | solution.py:676
  103.9 1.9 %collective-permute-start.21 = (f32[2,16,128]{2,1,0:T(8,128)S(1)}, f32[2,16,128]{2,1,0:T(8,128)S(1)}, u32[]{:S(2)}, u32[]{:S(2)}) collective-permute-start(f32[2,16,128]{2,1,0:T(8,128)S(1)} %pad_maximum_fusion.1.part_0), channel_id=1, source_target_pairs={{0,1},{1,0},{2,3},{3,2},{4,5},{5,4},{6,7},{7,6},{8,9},{9,8},{10,11... | collective-permute-start | bytes 49160 | tf_op jit(solution)/shard_map/ppermute | solution.py:679
  104.0 3.9 %collective-permute-start.22 = (f32[2,16,128]{2,1,0:T(8,128)S(1)}, f32[2,16,128]{2,1,0:T(8,128)S(1)}, u32[]{:S(2)}, u32[]{:S(2)}) collective-permute-start(f32[2,16,128]{2,1,0:T(8,128)S(1)} %pad_maximum_fusion.1.part_0), channel_id=1, source_target_pairs={{0,2},{1,3},{2,0},{3,1},{4,6},{5,7},{6,4},{7,5},{8,10},{9,11},{10,... | collective-permute-start | bytes 49160 | tf_op jit(solution)/shard_map/ppermute | solution.py:679
  104.7 3.3 %collective-permute-start.23 = (f32[2,16,128]{2,1,0:T(8,128)S(1)}, f32[2,16,128]{2,1,0:T(8,128)S(1)}, u32[]{:S(2)}, u32[]{:S(2)}) collective-permute-start(f32[2,16,128]{2,1,0:T(8,128)S(1)} %pad_maximum_fusion.1.part_0), channel_id=1, source_target_pairs={{0,3},{1,2},{2,1},{3,0},{4,7},{5,6},{6,5},{7,4},{8,11},{9,10},{10,... | collective-permute-start | bytes 49160 | tf_op jit(solution)/shard_map/ppermute | solution.py:679
